TPU v7x, 32 devices: a whole 2x2x4 slice. The times are simulated.
32 devices in a mesh: cohort: 2 (over x), region: 16 (over z, y, core).
Axes of the slice: x: 2, y: 2, z: 4, core: 2. Of those that a mesh axis runs over, the one named last changes fastest.
Arguments:
- dosage: bfloat16 [4096, 16384], P('cohort', 'region'), parts along dimension 0, may hold values from 0 to 2, as said below
- eigvec: bfloat16 [16384, 2048], P('region', 'cohort'), parts along dimension 1, may hold values from -1 to 1, as said below
- eigval: float32 [2, 16384], P('cohort', 'region'), parts along dimension 0, may hold values from 64 to 65536
- pheno: bfloat16 [4096, 128], P('cohort'), parts along dimension 0, may hold values from 0 to 1, as said below
Outputs:
- level1_weights: float32 [128, 128], P('region', 'cohort'), parts along dimension 1
There are 2 independent parts, one for each index of `cohort`. A program takes and returns all parts, laid end to end along the dimension named above; each array names one. Nothing has to cross between parts.
Inputs may be any that keep to these rules, and one draw needn't show every extreme that they name: Every entry is a whole dosage 0, 1 or 2. `eigvec`: the rows of each block form an orthonormal basis up to rounding. `pheno`: every entry is 0 or 1.
All inputs are finite; a program needn't handle non-finite values.
Results may differ from a plain program's by a relative error of at most 0.0051.
Values may be sent and summed in bfloat16 or wider, within the bound.
No kernel may reach another device: no remote copies, remote signals or barrier semaphores. Data moves between devices by JAX's collectives and lax.ppermute only.
A program may use at most 64 MiB of HBM per device.

v0:
```python
import jax
import jax.numpy as jnp
from jax import lax
from jax.sharding import PartitionSpec as P

NEWTON = 3


EPSILON = 1e-05
HERITABILITY = (0.01, 0.25, 0.75, 0.99)
LEVEL_ONE = 0.03125


def standardize(values):
    values = values.astype(jnp.float32)
    center = jnp.mean(values, axis=0)
    spread = jnp.sqrt(jnp.mean(jnp.square(values - center), axis=0) + EPSILON)
    return ((values - center) / spread).astype(jnp.bfloat16)


def fit_traits(moved, target, total_samples):
    count_traits = moved.shape[1]
    design = jnp.moveaxis(moved, 1, 0).reshape(count_traits, -1, moved.shape[3])
    predictors = design.shape[1]
    level_ridge = LEVEL_ONE * total_samples
    all_weights = jnp.zeros((count_traits, predictors), jnp.float32)
    own_weights = jnp.zeros((count_traits, predictors), jnp.float32)
    identity = jnp.eye(predictors, dtype=jnp.float32)
    for newton_step in range(NEWTON):
        logits = jnp.einsum(
            "kqn,kq->kn",
            design,
            all_weights.astype(jnp.bfloat16),
            preferred_element_type=jnp.float32,
        )
        prob = jax.nn.sigmoid(logits)
        resid = (target - prob).astype(jnp.bfloat16)
        weighted = (design * (prob * (1.0 - prob))[:, None, :]).astype(jnp.bfloat16)
        gram = jnp.einsum("kqn,kpn->kqp", weighted, design, preferred_element_type=jnp.float32)
        grad = jnp.einsum("kqn,kn->kq", design, resid, preferred_element_type=jnp.float32)
        grad = grad - level_ridge * own_weights
        factor = jnp.linalg.cholesky(gram + level_ridge * identity)
        partial_solve = lax.linalg.triangular_solve(
            factor, grad[:, :, None], left_side=True, lower=True
        )
        update = lax.linalg.triangular_solve(
            factor, partial_solve, left_side=True, lower=True, transpose_a=True
        )
        own_weights = own_weights + update[:, :, 0]
        all_weights = own_weights
    return own_weights


def on_device(dosage, eigvec, eigval, pheno):
    samples, width = dosage.shape
    traits = pheno.shape[1]
    regions = lax.axis_size("region")
    ridges = len(HERITABILITY)
    per_device = traits // regions
    shrink = jnp.array([width * (1.0 - value) / value for value in HERITABILITY], jnp.float32)
    std_trait = standardize(pheno)
    std_geno = standardize(dosage)
    cross = lax.dot_general(
        std_geno, std_trait, (((0,), (0,)), ((), ())), preferred_element_type=jnp.float32
    ).astype(jnp.bfloat16)
    rotated = lax.dot_general(
        eigvec, cross, (((0,), (0,)), ((), ())), preferred_element_type=jnp.float32
    )
    scaled = (rotated[:, None, :] / (eigval[0][:, None, None] + shrink[None, :, None])).astype(
        jnp.bfloat16
    )
    ridge = jnp.dot(
        eigvec, scaled.reshape(width, ridges * traits), preferred_element_type=jnp.float32
    ).astype(jnp.bfloat16)
    position = lax.axis_index("region")
    predicted = lax.dot_general(
        ridge, std_geno, (((0,), (1,)), ((), ())), preferred_element_type=jnp.float32
    ).astype(jnp.bfloat16)
    predicted = predicted.reshape(ridges, traits, 1, samples)
    moved = lax.all_to_all(predicted, "region", split_axis=1, concat_axis=2, tiled=True)
    target = lax.dynamic_slice_in_dim(pheno, position * per_device, per_device, 1)
    weights = fit_traits(moved, target.astype(jnp.float32).T, samples)
    return weights


def solution(mesh):
    return jax.shard_map(
        on_device,
        mesh=mesh,
        in_specs=(
            P("cohort", "region"),
            P("region", "cohort"),
            P("cohort", "region"),
            P("cohort", None),
        ),
        out_specs=P("region", "cohort"),
        check_vma=False,
    )
```

profile of v0, /device:TPU:17, one launch (start us, length us, event | category | flops | bytes accessed | tf_op | source)
XLA Modules:
  0.0 363.3 jit_solution(3730043652886165444)
XLA Ops:
  0.0 0.0 copy-start
  0.0 0.0 copy-start.1
  0.0 3.0 convert_reduce_fusion
  3.1 0.5 copy-done.1
  3.6 1.1 fusion.2
  4.8 0.0 copy-start.5
  4.8 3.2 fusion.3
  8.0 0.0 copy-done.5
  8.0 0.3 convert_reduce_fusion.1
  8.3 0.3 fusion.27
  8.6 0.0 copy-done
  8.6 0.0 copy-start.6
  8.6 0.0 copy-start.7
  8.6 5.0 %convolution_bitcast_fusion = f32[1024,128]{0,1:T(8,128)} fusion(bf16[1024,1024]{1,0:T(8,128)(2,1)S(1)} %copy-done, bf16[2048,1024]{1,0:T(8,128)(2,1)} %fusion.3, bf16[2048,128]{1,0:T(8,128)(2,1)S(1)} %copy-done.5, f32[128]{0:T(128)S(1)} %add_sqrt_fusion.1, f32[128]{0:T(128)S(1)} %broadcast_multiply_fusion.1), kind=kOutput, calls=%fused_computation.25 | convolution fusion | flops 806486016 | bytes 7341056 | tf_op jit(solution)/shard_map/dot_general | solution.py:66
  13.6 1.2 copy.50
  14.9 0.0 copy-done.6
  14.9 0.0 copy-done.7
  14.9 0.2 broadcast_add_fusion
  15.1 4.6 %divide_convert_fusion = bf16[1024,4,128]{2,1,0:T(4,128)(2,1)} fusion(f32[1024,4]{1,0:T(8,128)S(1)} %broadcast_add_fusion, f32[1024,128]{1,0:T(8,128)S(1)} %copy.50), kind=kLoop, calls=%fused_computation.16 | loop fusion | flops 1048576 | bytes 1589248 | tf_op jit(solution)/shard_map/convert_element_type | solution.py:69
  19.7 7.3 %convolution_convert_fusion = bf16[512,2048]{1,0:T(8,128)(2,1)} fusion(bf16[2048,1024]{1,0:T(8,128)(2,1)} %fusion.3, bf16[1024,1024]{1,0:T(8,128)(2,1)S(1)} %copy-done, bf16[128,8,4,128]{3,2,1,0:T(4,128)(2,1)} %bitcast.211), kind=kOutput, calls=%fused_computation.15 | convolution fusion | flops 3222798336 | bytes 9437184 | tf_op jit(solution)/shard_map/dot_general | solution.py:76
  27.0 4.6 %copy.51 = bf16[4,128,1,2048]{3,0,2,1:T(4,128)(2,1)} copy(bf16[4,128,1,2048]{3,1,0,2:T(8,128)(2,1)} %bitcast.210) | data formatting | bytes 4194304 | tf_op jit(solution)/shard_map/reshape | solution.py:79
  31.6 6.7 %all-to-all-start = ((bf16[4,128,1,2048]{3,0,2,1:T(4,128)(2,1)}), bf16[4,128,1,2048]{3,0,2,1:T(4,128)(2,1)}, u32[]{:S(2)}, u32[]{:S(2)}) async-start(bf16[4,128,1,2048]{3,0,2,1:T(4,128)(2,1)} %copy.51), calls=%async_computation | async-start | bytes 4194304 | tf_op jit(solution)/shard_map/all_to_all | solution.py:80
  38.2 0.2 constant_dynamic-slice_fusion
  38.5 0.2 copy.90
  38.7 46.8 %all-to-all-done = bf16[4,128,1,2048]{3,0,2,1:T(4,128)(2,1)} async-done(((bf16[4,128,1,2048]{3,0,2,1:T(4,128)(2,1)}), bf16[4,128,1,2048]{3,0,2,1:T(4,128)(2,1)}, u32[]{:S(2)}, u32[]{:S(2)}) %all-to-all-start) | async-done | bytes 2097184 | tf_op jit(solution)/shard_map/all_to_all | solution.py:80
  85.5 2.8 copy.52
  88.3 0.0 copy-start.2
  88.3 0.4 fusion.76
  88.7 0.9 copy-done.2
  89.6 0.7 fusion.18
  90.4 0.1 copy.54
  90.5 46.9 %custom-call.15 = f32[8,64,64]{2,1,0:T(8,128)S(1)} custom-call(f32[8,64,64]{2,1,0:T(8,128)S(1)} %fusion.50), custom_call_target="Cholesky" | custom-call | tf_op jit(solution)/shard_map/jit(cholesky)/cholesky | solution.py:42
  137.5 0.1 compare_reduce_fusion.2
  137.6 0.1 select_bitcast_fusion.2
  137.7 39.3 %custom-call.17 = f32[8,1,64,64]{2,3,1,0:T(8,128)S(1)} custom-call(f32[8,1,64,64]{3,2,1,0:T(8,128)S(1)} %select_bitcast_fusion.2), custom_call_target="InvertDiagBlocksLowerTriangular" | custom-call | tf_op jit(solution)/shard_map/triangular_solve/custom-call.2 | solution.py:46
  177.0 0.0 copy-start.3
  177.1 2.4 convolution_bitcast_fusion.4
  179.4 0.4 convolution_bitcast_fusion.3
  179.8 0.5 fusion.48
  180.3 0.0 copy-done.3
  180.3 0.4 fusion.74
  180.8 0.8 fusion.21
  181.5 0.1 copy.58
  181.7 46.9 %custom-call.18 = f32[8,64,64]{2,1,0:T(8,128)S(1)} custom-call(f32[8,64,64]{2,1,0:T(8,128)S(1)} %fusion.46), custom_call_target="Cholesky" | custom-call | tf_op jit(solution)/shard_map/jit(cholesky)/cholesky | solution.py:42
  228.7 0.1 compare_reduce_fusion.1
  228.8 0.1 select_bitcast_fusion.1
  228.9 39.3 %custom-call.20 = f32[8,1,64,64]{2,3,1,0:T(8,128)S(1)} custom-call(f32[8,1,64,64]{3,2,1,0:T(8,128)S(1)} %select_bitcast_fusion.1), custom_call_target="InvertDiagBlocksLowerTriangular" | custom-call | tf_op jit(solution)/shard_map/triangular_solve/custom-call.2 | solution.py:46
  268.2 0.0 copy-start.4
  268.2 2.4 fusion.65
  270.6 0.4 convolution_bitcast_fusion.2
  271.0 0.5 fusion.44
  271.5 0.0 copy-done.4
  271.5 0.4 fusion.72
  272.0 0.7 fusion.24
  272.7 0.1 copy.61
  272.9 47.1 %custom-call.21 = f32[8,64,64]{2,1,0:T(8,128)S(1)} custom-call(f32[8,64,64]{2,1,0:T(8,128)S(1)} %fusion.42), custom_call_target="Cholesky" | custom-call | tf_op jit(solution)/shard_map/jit(cholesky)/cholesky | solution.py:42
  320.1 0.1 compare_reduce_fusion
  320.2 0.1 select_bitcast_fusion
  320.3 39.3 %custom-call.23 = f32[8,1,64,64]{2,3,1,0:T(8,128)S(1)} custom-call(f32[8,1,64,64]{3,2,1,0:T(8,128)S(1)} %select_bitcast_fusion), custom_call_target="InvertDiagBlocksLowerTriangular" | custom-call | tf_op jit(solution)/shard_map/triangular_solve/custom-call.2 | solution.py:46
  359.6 2.2 fusion.63
  361.9 0.4 convolution_bitcast_fusion.1
  362.2 0.5 fusion.40
  362.7 0.6 add_bitcast_fusion
  (20 shorter events, 0.5 us)
Async XLA Ops:
  0.0 8.6 %copy-start = (bf16[1024,1024]{1,0:T(8,128)(2,1)S(1)}, bf16[1024,1024]{1,0:T(8,128)(2,1)}, u32[]{:S(2)}) copy-start(bf16[1024,1024]{1,0:T(8,128)(2,1)} %param.11) | copy-start | bytes 6291460
  0.0 3.6 copy-start.1
  4.8 3.2 copy-start.5
  8.6 6.3 %copy-start.6 = (f32[1,1024]{1,0:T(1,128)S(1)}, f32[1,1024]{1,0:T(1,128)}, u32[]{:S(2)}) copy-start(f32[1,1024]{1,0:T(1,128)} %param.12) | copy-start | bytes 12292
  8.6 6.3 %copy-start.7 = (f32[4]{0:T(128)S(1)}, f32[4]{0:T(128)}, u32[]{:S(2)}) copy-start(f32[4]{0:T(128)} %constant.65.clone) | copy-start | bytes 52
  31.6 53.9 %all-to-all-start = ((bf16[4,128,1,2048]{3,0,2,1:T(4,128)(2,1)}), bf16[4,128,1,2048]{3,0,2,1:T(4,128)(2,1)}, u32[]{:S(2)}, u32[]{:S(2)}) async-start(bf16[4,128,1,2048]{3,0,2,1:T(4,128)(2,1)} %copy.51), calls=%async_computation | async-start | bytes 4194304 | tf_op jit(solution)/shard_map/all_to_all | solution.py:80
  88.3 1.4 copy-start.2
  177.0 3.3 copy-start.3
  268.2 3.3 copy-start.4
where the time goes:
time: 364 us; the launch traced here: 363 us
  other arithmetic  273 us (75%)
  waiting for transfers between devices  46.8 us (13%)
  matrix products  25.4 us (7%)
  local copies, waits for them, and re-layouts  10.8 us (3%)
  starting transfers between devices  6.68 us (2%)
    another operation x10, other arithmetic, fit_traits(): factor = jnp.linalg.cholesky(gram + level_ridge * identity)  141 us
    another operation x7, other arithmetic, fit_traits(): lax.linalg.triangular_solve(factor, partial_solve, left_side=True, lower=...  118 us
    all_to_all x1, waiting for transfers between devices, on_device(): lax.all_to_all(predicted, 'region', split_axis=1, concat_axis=2, tiled=True)  46.8 us
    dot_general x1, matrix products, on_device(): lax.dot_general(ridge, std_geno, (((0,), (1,)), ((), ())), preferred_elem...  7.31 us
  transfers between devices with their start and end apart: 1, of which 1 were waited for; matrix products, arithmetic and copies ran while one was open for 0% of the time, Pallas kernels for 0%

commit v1 on v0

v1 whole, which is shorter than its diff:
```python
import functools

import jax
import jax.numpy as jnp
from jax import lax
from jax.experimental import pallas as pl
from jax.experimental.pallas import tpu as pltpu
from jax.sharding import PartitionSpec as P

NEWTON = 3
EPSILON = 1e-05
HERITABILITY = (0.01, 0.25, 0.75, 0.99)
LEVEL_ONE = 0.03125
RIDGES = len(HERITABILITY)
LANES = 128
TILE = 256


def standardize(values):
    values = values.astype(jnp.float32)
    center = jnp.mean(values, axis=0)
    spread = jnp.sqrt(jnp.mean(jnp.square(values - center), axis=0) + EPSILON)
    return ((values - center) / spread).astype(jnp.bfloat16)


def reorder_matrix(traits, blocks):
    size = blocks * RIDGES * traits
    row = lax.broadcasted_iota(jnp.int32, (size, size), 0)
    column = lax.broadcasted_iota(jnp.int32, (size, size), 1)
    trait, rest = row // (RIDGES * blocks), row % (RIDGES * blocks)
    source = (rest // RIDGES) * (RIDGES * traits) + (rest % RIDGES) * traits + trait
    return jnp.where(column == source, 1.0, 0.0).astype(jnp.bfloat16)


def newton_kernel(traits, predictors, arrived, target, out, design, lhs, system):
    samples = arrived.shape[1]
    blocks = TILE // (RIDGES * traits)
    width = RIDGES * blocks
    order = reorder_matrix(traits, blocks)
    for part in range(arrived.shape[0] // TILE):
        moved = jnp.dot(
            order, arrived[part * TILE : (part + 1) * TILE, :], preferred_element_type=jnp.float32
        ).astype(jnp.bfloat16)
        for t in range(traits):
            start = t * predictors + part * width
            design[start : start + width, :] = moved[t * width : (t + 1) * width]
    level_ridge = LEVEL_ONE * samples
    lane = lax.broadcasted_iota(jnp.int32, (traits, LANES), 1)
    sub = lax.broadcasted_iota(jnp.int32, (traits, LANES), 0)
    row = lax.broadcasted_iota(jnp.int32, (predictors, predictors), 0)
    column = lax.broadcasted_iota(jnp.int32, (predictors, predictors), 1)
    diagonal = jnp.where(row == column, level_ridge, 0.0).astype(jnp.float32)
    fold = LANES // predictors
    pheno = target[...]

    def step(_, weights):
        spread_out = [
            jnp.where(lane // predictors + fold * v == sub, weights, 0.0).astype(jnp.bfloat16)
            for v in range(traits // fold)
        ]
        logits = jnp.dot(
            jnp.concatenate(spread_out, axis=1), design[...], preferred_element_type=jnp.float32
        )
        prob = 1.0 / (1.0 + jnp.exp(-logits))
        curve = prob * (1.0 - prob)
        resid = pheno - prob
        resid = jnp.concatenate([resid, jnp.zeros_like(resid)], axis=0).astype(jnp.bfloat16)
        grad = jnp.zeros((traits, predictors), jnp.float32)
        for t in range(traits):
            own = design[t * predictors : (t + 1) * predictors, :]
            lhs[t, 0:predictors, :] = (own.astype(jnp.float32) * curve[t : t + 1, :]).astype(
                jnp.bfloat16
            )
            lhs[t, predictors : predictors + 2 * traits, :] = resid
            result = lax.dot_general(
                lhs[t], own, (((1,), (1,)), ((), ())), preferred_element_type=jnp.float32
            )
            system[:, t, 0:predictors] = result[0:predictors] + diagonal
            grad = jnp.where(
                sub[:, 0:predictors] == t, result[predictors : predictors + traits], grad
            )
        grad = grad - level_ridge * weights[:, 0:predictors]
        right = jnp.concatenate(
            [
                jnp.broadcast_to(grad[:, i : i + 1], (traits, LANES))[None]
                for i in range(predictors)
            ],
            axis=0,
        )
        table = jnp.where(lane[None] < predictors, system[...], right)
        for k in range(predictors):
            pivot = table[k]
            scaled = (pivot * (1.0 / pivot[:, k : k + 1]))[None]
            below = table - table[:, :, k : k + 1] * scaled
            pieces = [scaled]
            if k > 0:
                pieces = [below[:k]] + pieces
            if k < predictors - 1:
                pieces = pieces + [below[k + 1 :]]
            table = jnp.concatenate(pieces, axis=0)
        for i in range(predictors):
            solved = jnp.broadcast_to(table[i][:, predictors : predictors + 1], (traits, LANES))
            weights = weights + jnp.where(lane % predictors == i, solved, 0.0)
        return weights

    out[...] = lax.fori_loop(0, NEWTON, step, jnp.zeros((traits, LANES), jnp.float32))


def newton(arrived, target):
    rows, samples = arrived.shape
    traits = target.shape[0]
    predictors = rows // traits
    weights = pl.pallas_call(
        functools.partial(newton_kernel, traits, predictors),
        out_shape=jax.ShapeDtypeStruct((traits, LANES), jnp.float32),
        in_specs=[pl.BlockSpec(memory_space=pltpu.VMEM)] * 2,
        out_specs=pl.BlockSpec(memory_space=pltpu.VMEM),
        scratch_shapes=[
            pltpu.VMEM((rows, samples), jnp.bfloat16),
            pltpu.VMEM((traits, predictors + 2 * traits, samples), jnp.bfloat16),
            pltpu.VMEM((predictors, traits, LANES), jnp.float32),
        ],
        compiler_params=pltpu.CompilerParams(vmem_limit_bytes=48 << 20),
        name="newton",
    )(arrived, target)
    return weights[:, :predictors]


def fit_traits(arrived, target):
    rows, samples = arrived.shape
    count = target.shape[0]
    predictors = rows // count
    design = arrived.reshape(-1, RIDGES, count, samples).transpose(2, 0, 1, 3)
    design = design.reshape(count, predictors, samples)
    level_ridge = LEVEL_ONE * samples
    weights = jnp.zeros((count, predictors), jnp.float32)
    identity = jnp.eye(predictors, dtype=jnp.float32)
    for _ in range(NEWTON):
        logits = jnp.einsum(
            "kqn,kq->kn", design, weights.astype(jnp.bfloat16), preferred_element_type=jnp.float32
        )
        prob = jax.nn.sigmoid(logits)
        resid = (target - prob).astype(jnp.bfloat16)
        weighted = (design * (prob * (1.0 - prob))[:, None, :]).astype(jnp.bfloat16)
        gram = jnp.einsum("kqn,kpn->kqp", weighted, design, preferred_element_type=jnp.float32)
        grad = jnp.einsum("kqn,kn->kq", design, resid, preferred_element_type=jnp.float32)
        grad = grad - level_ridge * weights
        factor = jnp.linalg.cholesky(gram + level_ridge * identity)
        partial_solve = lax.linalg.triangular_solve(
            factor, grad[:, :, None], left_side=True, lower=True
        )
        update = lax.linalg.triangular_solve(
            factor, partial_solve, left_side=True, lower=True, transpose_a=True
        )
        weights = weights + update[:, :, 0]
    return weights


def on_device(dosage, eigvec, eigval, pheno):
    samples, width = dosage.shape
    traits = pheno.shape[1]
    regions = lax.axis_size("region")
    per_device = traits // regions
    shrink = jnp.array([width * (1.0 - value) / value for value in HERITABILITY], jnp.float32)
    std_trait = standardize(pheno)
    std_geno = standardize(dosage)
    cross = lax.dot_general(
        std_trait, std_geno, (((0,), (0,)), ((), ())), preferred_element_type=jnp.float32
    ).astype(jnp.bfloat16)
    rotated = jnp.dot(cross, eigvec, preferred_element_type=jnp.float32)
    scaled = rotated.reshape(regions, 1, per_device, width) / (
        eigval[0][None, None, None, :] + shrink[None, :, None, None]
    )
    scaled = scaled.astype(jnp.bfloat16).reshape(RIDGES * traits, width)
    ridge = lax.dot_general(
        scaled, eigvec, (((1,), (1,)), ((), ())), preferred_element_type=jnp.float32
    ).astype(jnp.bfloat16)
    predicted = lax.dot_general(
        ridge, std_geno, (((1,), (1,)), ((), ())), preferred_element_type=jnp.float32
    ).astype(jnp.bfloat16)
    arrived = lax.all_to_all(predicted, "region", split_axis=0, concat_axis=0, tiled=True)
    position = lax.axis_index("region")
    target = lax.dynamic_slice_in_dim(pheno, position * per_device, per_device, 1)
    target = target.astype(jnp.float32).T
    predictors = RIDGES * regions
    if per_device == 8 and LANES % predictors == 0 and predictors < LANES:
        weights = newton(arrived, target)
    else:
        weights = fit_traits(arrived, target)
    weights = weights.reshape(per_device, regions, RIDGES).swapaxes(1, 2)
    return weights.reshape(per_device, predictors)


def solution(mesh):
    return jax.shard_map(
        on_device,
        mesh=mesh,
        in_specs=(
            P("cohort", "region"),
            P("region", "cohort"),
            P("cohort", "region"),
            P("cohort", None),
        ),
        out_specs=P("region", "cohort"),
        check_vma=False,
    )
```

time: 364 us -> 108 us (0.30)
  other arithmetic: 273 us -> 9.29 us
  Pallas kernels: 0 us -> 32.7 us
  matrix products: 25.4 us -> 10.6 us
  local copies, waits for them, and re-layouts: 10.8 us -> 1.79 us
    another operation x17 -> x0, other arithmetic: 260 us -> none  [the longest x10 141 us: fit_traits(): factor = jnp.linalg.cholesky(gram + level_ridge * identity)]
    pallas_call x0 -> x1, Pallas kernels: none -> 32.7 us  [newton(): pl.pallas_call(functools.partial(newton_kernel, traits, predictors), out_...]
    dot_general x11 -> x2, matrix products: 22.8 us -> 10.6 us  [the longest x1 7.3 us: on_device(): lax.dot_general(ridge, std_geno, (((1,), (1,)), ((), ())), preferred_elem...]
    reshape x1, local copies, waits for them, and re-layouts: 4.56 us -> 0.68 us  [on_device(): return weights.reshape(per_device, predictors)]
where the time goes in v1:
time: 108 us
  waiting for transfers between devices  46.8 us (43%)
  Pallas kernels  32.7 us (30%)
  matrix products  10.6 us (10%)
  other arithmetic  9.29 us (9%)
  starting transfers between devices  6.49 us (6%)
  local copies, waits for them, and re-layouts  1.79 us (2%)
    all_to_all x1, waiting for transfers between devices, on_device(): lax.all_to_all(predicted, 'region', split_axis=0, concat_axis=0, tiled=True)  46.8 us
    pallas_call x1, Pallas kernels, newton(): pl.pallas_call(functools.partial(newton_kernel, traits, predictors), out_...  32.7 us
    dot_general x1, matrix products, on_device(): lax.dot_general(ridge, std_geno, (((1,), (1,)), ((), ())), preferred_elem...  7.3 us
    all_to_all x1, starting transfers between devices, on_device(): lax.all_to_all(predicted, 'region', split_axis=0, concat_axis=0, tiled=True)  6.49 us
    reduce_sum x2, other arithmetic, standardize(): center = jnp.mean(values, axis=0)  3.33 us
    dot_general x1, matrix products, on_device(): rotated = jnp.dot(cross, eigvec, preferred_element_type=jnp.float32)  3.29 us
    convert_element_type x1, other arithmetic, standardize(): return ((values - center) / spread).astype(jnp.bfloat16)  3.21 us
  transfers between devices with their start and end apart: 1, of which 1 were waited for; matrix products, arithmetic and copies ran while one was open for 0% of the time, Pallas kernels for 0%

profile of v1, /device:TPU:17, one launch (start us, length us, event | category | flops | bytes accessed | tf_op | source)
XLA Modules:
  0.0 107.8 jit_solution(13765535848704772228)
XLA Ops:
  0.0 0.0 copy-start
  0.0 0.0 copy-start.1
  0.0 3.0 %convert_reduce_fusion = f32[1024]{0:T(1024)S(1)} fusion(bf16[2048,1024]{1,0:T(8,128)(2,1)} %param.5), kind=kLoop, calls=%fused_computation.1 | loop fusion | flops 4193280 | bytes 4198400 | tf_op jit(solution)/shard_map/reduce_sum | solution.py:21
  3.1 0.5 copy-done.1
  3.6 1.1 %fusion.2 = f32[1024]{0:T(1024)S(1)} fusion(bf16[2048,1024]{1,0:T(8,128)(2,1)S(1)} %copy-done.1, f32[1024]{0:T(1024)S(1)} %broadcast_multiply_fusion), kind=kLoop, calls=%fused_computation.4 | loop fusion | flops 8387584 | bytes 4202496 | tf_op jit(solution)/shard_map/reduce_sum | solution.py:22
  4.8 0.0 copy-start.2
  4.8 0.0 copy-start.3
  4.8 0.0 copy-start.4
  4.8 3.2 %fusion.3 = bf16[2048,1024]{1,0:T(8,128)(2,1)} fusion(bf16[2048,1024]{1,0:T(8,128)(2,1)S(1)} %copy-done.1, f32[1024]{0:T(1024)S(1)} %add_sqrt_fusion, f32[1024]{0:T(1024)S(1)} %broadcast_multiply_fusion), kind=kLoop, calls=%fused_computation.5 | loop fusion | flops 8388608 | bytes 8396800 | tf_op jit(solution)/shard_map/convert_element_type | solution.py:23
  8.0 0.0 copy-done.2
  8.0 0.3 convert_reduce_fusion.1
  8.3 0.3 fusion.6
  8.6 0.0 copy-done.3
  8.6 0.0 copy-done.4
  8.6 0.1 broadcast_add_fusion
  8.7 0.0 copy-done
  8.7 3.3 %convolution_bitcast_fusion = f32[16,8,1024]{2,1,0:T(8,128)S(1)} fusion(bf16[1024,1024]{1,0:T(8,128)(2,1)S(1)} %copy-done, bf16[2048,1024]{1,0:T(8,128)(2,1)} %fusion.3, bf16[2048,128]{1,0:T(8,128)(2,1)S(1)} %copy-done.2, f32[128]{0:T(128)S(1)} %add_sqrt_fusion.1, f32[128]{0:T(128)S(1)} %broadcast_multiply_fusion.1), kind=kOutput, calls=%fused_computation.13 | convolution fusion | flops 806486016 | bytes 7341056 | tf_op jit(solution)/shard_map/dot_general | solution.py:170
  12.0 1.2 %divide_convert_fusion = bf16[16,4,8,1024]{3,2,1,0:T(8,128)(2,1)} fusion(f32[4,1024]{1,0:T(4,128)S(1)} %broadcast_add_fusion, f32[16,8,1024]{2,1,0:T(8,128)S(1)} %convolution_bitcast_fusion), kind=kLoop, calls=%fused_computation.7 | loop fusion | flops 1048576 | bytes 1589248 | tf_op jit(solution)/shard_map/convert_element_type | solution.py:174
  13.2 7.3 %convolution_convert_fusion = bf16[512,2048]{1,0:T(8,128)(2,1)} fusion(bf16[2048,1024]{1,0:T(8,128)(2,1)} %fusion.3, bf16[512,1024]{1,0:T(8,128)(2,1)} %bitcast.19, bf16[1024,1024]{1,0:T(8,128)(2,1)S(1)} %copy-done), kind=kOutput, calls=%fused_computation.6 | convolution fusion | flops 3222798336 | bytes 9437184 | tf_op jit(solution)/shard_map/dot_general | solution.py:178
  20.5 6.5 %all-to-all-start = ((bf16[16,32,2048]{2,1,0:T(8,128)(2,1)}), bf16[16,32,2048]{2,1,0:T(8,128)(2,1)}, u32[]{:S(2)}, u32[]{:S(2)}) async-start(bf16[16,32,2048]{2,1,0:T(8,128)(2,1)} %bitcast.18), calls=%async_computation | async-start | bytes 4194304 | tf_op jit(solution)/shard_map/all_to_all | solution.py:181
  27.0 0.2 constant_dynamic-slice_fusion
  27.2 0.2 copy.13
  27.4 46.8 %all-to-all-done = bf16[16,32,2048]{2,1,0:T(8,128)(2,1)} async-done(((bf16[16,32,2048]{2,1,0:T(8,128)(2,1)}), bf16[16,32,2048]{2,1,0:T(8,128)(2,1)}, u32[]{:S(2)}, u32[]{:S(2)}) %all-to-all-start) | async-done | bytes 2097184 | tf_op jit(solution)/shard_map/all_to_all | solution.py:181
  74.2 32.7 %newton.1 = f32[8,128]{1,0:T(8,128)S(1)} custom-call(bf16[512,2048]{1,0:T(8,128)(2,1)} %bitcast.4.arrived, f32[8,2048]{1,0:T(8,128)S(1)} %convert_bitcast_fusion.target), custom_call_target="tpu_custom_call" | custom-call | tf_op jit(solution)/shard_map/newton/pallas_call | solution.py:113
  106.9 0.1 copy.11
  107.0 0.1 copy.12
  107.1 0.7 reshape.65
  (5 shorter events, 0.0 us)
Async XLA Ops:
  0.0 8.7 %copy-start = (bf16[1024,1024]{1,0:T(8,128)(2,1)S(1)}, bf16[1024,1024]{1,0:T(8,128)(2,1)}, u32[]{:S(2)}) copy-start(bf16[1024,1024]{1,0:T(8,128)(2,1)} %param.6) | copy-start | bytes 6291460
  0.0 3.6 %copy-start.1 = (bf16[2048,1024]{1,0:T(8,128)(2,1)S(1)}, bf16[2048,1024]{1,0:T(8,128)(2,1)}, u32[]{:S(2)}) copy-start(bf16[2048,1024]{1,0:T(8,128)(2,1)} %param.5) | copy-start | bytes 12582916
  4.8 3.2 %copy-start.2 = (bf16[2048,128]{1,0:T(8,128)(2,1)S(1)}, bf16[2048,128]{1,0:T(8,128)(2,1)}, u32[]{:S(2)}) copy-start(bf16[2048,128]{1,0:T(8,128)(2,1)} %param.8) | copy-start | bytes 1572868
  4.8 3.8 %copy-start.3 = (f32[1,1024]{1,0:T(1,128)S(1)}, f32[1,1024]{1,0:T(1,128)}, u32[]{:S(2)}) copy-start(f32[1,1024]{1,0:T(1,128)} %param.7) | copy-start | bytes 12292
  4.8 3.8 %copy-start.4 = (f32[4]{0:T(128)S(1)}, f32[4]{0:T(128)}, u32[]{:S(2)}) copy-start(f32[4]{0:T(128)} %constant.24.clone) | copy-start | bytes 52
  20.5 53.7 %all-to-all-start = ((bf16[16,32,2048]{2,1,0:T(8,128)(2,1)}), bf16[16,32,2048]{2,1,0:T(8,128)(2,1)}, u32[]{:S(2)}, u32[]{:S(2)}) async-start(bf16[16,32,2048]{2,1,0:T(8,128)(2,1)} %bitcast.18), calls=%async_computation | async-start | bytes 4194304 | tf_op jit(solution)/shard_map/all_to_all | solution.py:181

commit v2 on v1

v2 whole, which is shorter than its diff:
```python
import functools

import jax
import jax.numpy as jnp
from jax import lax
from jax.experimental import pallas as pl
from jax.experimental.pallas import tpu as pltpu
from jax.sharding import PartitionSpec as P

NEWTON = 3
EPSILON = 1e-05
HERITABILITY = (0.01, 0.25, 0.75, 0.99)
LEVEL_ONE = 0.03125
RIDGES = len(HERITABILITY)
LANES = 128
SUBLANES = 8
TILE = 256


def standardize(values):
    values = values.astype(jnp.float32)
    center = jnp.mean(values, axis=0)
    spread = jnp.sqrt(jnp.mean(jnp.square(values - center), axis=0) + EPSILON)
    return ((values - center) / spread).astype(jnp.bfloat16)


def reorder_matrix(traits, blocks, parts):
    size = blocks * RIDGES * traits // parts
    row = lax.broadcasted_iota(jnp.int32, (size, size), 0)
    column = lax.broadcasted_iota(jnp.int32, (size, size), 1)
    group = blocks // parts
    block, rest = row % group, row // group
    ridge, pair = rest % RIDGES, rest // RIDGES
    trait = (pair % 2) * (traits // 2) + pair // 2
    return jnp.where(column == (block * RIDGES + ridge) * traits + trait, 1.0, 0.0).astype(
        jnp.bfloat16
    )


def inverse_two(m):
    (a, b), (c, d) = m
    scale = 1.0 / (a * d - b * c)
    return ((d * scale, -b * scale), (-c * scale, a * scale))


def product(x, y):
    return tuple(
        tuple(x[i][0] * y[0][j] + x[i][1] * y[1][j] for j in range(2)) for i in range(2)
    )


def negative(x):
    return tuple(tuple(-value for value in row) for row in x)


def inverse_four(m):
    def corner(i, j):
        return ((m[i][j], m[i][j + 1]), (m[i + 1][j], m[i + 1][j + 1]))

    first = inverse_two(corner(0, 0))
    left = product(corner(2, 0), first)
    right = product(first, corner(0, 2))
    inner = product(left, corner(0, 2))
    last = corner(2, 2)
    second = inverse_two(
        tuple(tuple(last[i][j] - inner[i][j] for j in range(2)) for i in range(2))
    )
    below = product(second, left)
    back = product(right, below)
    top = tuple(tuple(first[i][j] + back[i][j] for j in range(2)) for i in range(2))
    beside, below = negative(product(right, second)), negative(below)
    return [list(top[i]) + list(beside[i]) for i in range(2)] + [
        list(below[i]) + list(second[i]) for i in range(2)
    ]


def gather_lanes(tile, lanes):
    return jnp.take_along_axis(tile, lanes, axis=1)


def solve(table, span):
    heights, tiles = len(table), len(table[0])
    lane = lax.broadcasted_iota(jnp.int32, (SUBLANES, LANES), 1)
    within = lane % span
    for k in range(0, (tiles - 1) * SUBLANES, 4):
        home, low = k // span, k % span
        first, sub = k // SUBLANES, k % SUBLANES
        rows = [
            [gather_lanes(table[home][r], (lane - within) + low + m) for r in range(first, tiles)]
            for m in range(4)
        ]
        columns = [
            [
                jnp.broadcast_to(table[h][first][sub + m : sub + m + 1], (SUBLANES, LANES))
                for h in range(heights)
            ]
            for m in range(4)
        ]
        pivot = [
            [
                jnp.broadcast_to(rows[m][0][sub + n : sub + n + 1], (SUBLANES, LANES))
                for n in range(4)
            ]
            for m in range(4)
        ]
        inverse = inverse_four(pivot)
        chosen = (within >= low) & (within < low + 4)
        for h in range(heights):
            factors = []
            for n in range(4):
                factor = (columns[0][h] * inverse[0][n] + columns[1][h] * inverse[1][n]) + (
                    columns[2][h] * inverse[2][n] + columns[3][h] * inverse[3][n]
                )
                if h == home:
                    for m in range(4):
                        factor = jnp.where(within == low + m, -inverse[m][n], factor)
                factors.append(factor)
            for r in range(first, tiles):
                base = table[h][r]
                if h == home:
                    base = jnp.where(chosen, 0.0, base)
                table[h][r] = (
                    base
                    - (factors[0] * rows[0][r - first] + factors[1] * rows[1][r - first])
                    - (factors[2] * rows[2][r - first] + factors[3] * rows[3][r - first])
                )
    return [table[h][tiles - 1] for h in range(heights)]


def exchange(tiles, span):
    lane = lax.broadcasted_iota(jnp.int32, (SUBLANES, LANES), 1)
    tiles = list(tiles)
    for bit in (1, 2):
        shift = bit * span
        odd = (lane // shift) % 2 == 1
        for i in range(4):
            if not i & bit:
                x, y = tiles[i], tiles[i | bit]
                tiles[i] = jnp.where(odd, pltpu.roll(y, shift, 1), x)
                tiles[i | bit] = jnp.where(odd, y, pltpu.roll(x, LANES - shift, 1))
    return tiles


def newton_kernel(traits, blocks, arrived, target, out, design, lhs):
    samples = arrived.shape[1]
    predictors = RIDGES * blocks
    half = traits // 2
    parts = arrived.shape[0] // TILE
    order = reorder_matrix(traits, blocks, parts)
    group = blocks // parts
    for part in range(parts):
        moved = jnp.dot(
            order, arrived[part * TILE : (part + 1) * TILE, :], preferred_element_type=jnp.float32
        )
        for i in range(TILE // group):
            start = i * blocks + part * group
            design[start : start + group, :] = moved[i * group : (i + 1) * group].astype(
                jnp.bfloat16
            )
    level_ridge = LEVEL_ONE * samples
    lane = lax.broadcasted_iota(jnp.int32, (SUBLANES, LANES), 1)
    sub = lax.broadcasted_iota(jnp.int32, (SUBLANES, LANES), 0)
    upper = lane >= predictors
    pheno = target[...]
    middle = predictors + 2 * traits

    def step(_, weights):
        spread_out = [
            jnp.where((lane // predictors) * half + s == sub, w, 0.0).astype(jnp.bfloat16)
            for s, w in enumerate(exchange(weights, blocks))
        ]
        logits = jnp.dot(
            jnp.concatenate(spread_out, axis=1), design[...], preferred_element_type=jnp.float32
        )
        prob = 1.0 / (1.0 + jnp.exp(-logits))
        curve = prob * (1.0 - prob)
        resid = pheno - prob
        resid = jnp.concatenate([resid, jnp.zeros_like(resid)], axis=0).astype(jnp.bfloat16)
        found = []
        for s in range(half):
            base = s * 2 * predictors
            for start, trait, place in ((0, s, 0), (predictors, s + half, middle)):
                own = design[base + start : base + start + predictors, :].astype(jnp.float32)
                lhs[s, place : place + predictors, :] = (own * curve[trait : trait + 1, :]).astype(
                    jnp.bfloat16
                )
            lhs[s, predictors:middle, :] = resid
            result = lax.dot_general(
                lhs[s],
                design[base : base + 2 * predictors, :],
                (((1,), (1,)), ((), ())),
                preferred_element_type=jnp.float32,
            )
            tiles = [
                jnp.where(
                    upper,
                    result[middle + SUBLANES * r : middle + SUBLANES * (r + 1)],
                    result[SUBLANES * r : SUBLANES * (r + 1)],
                )
                for r in range(predictors // SUBLANES)
            ]
            first, second = predictors + s, predictors + s + half
            tiles.append(
                jnp.where(
                    upper[:1], result[second : second + 1], result[first : first + 1]
                )
                + jnp.zeros((SUBLANES, LANES), jnp.float32)
            )
            found.append(tiles)
        table = [[] for _ in range(RIDGES)]
        for r in range(predictors // SUBLANES + 1):
            for h, tile in enumerate(exchange([found[s][r] for s in range(half)], blocks)):
                if r < predictors // SUBLANES:
                    same = SUBLANES * r + sub == h * blocks + lane % blocks
                    tile = tile + jnp.where(same, level_ridge, 0.0)
                else:
                    tile = tile - level_ridge * weights[h]
                table[h].append(tile)
        solved = solve(table, blocks)
        return tuple(
            weights[h] + jnp.broadcast_to(solved[h][0:1], (SUBLANES, LANES))
            for h in range(RIDGES)
        )

    start = tuple(jnp.zeros((SUBLANES, LANES), jnp.float32) for _ in range(RIDGES))
    weights = lax.fori_loop(0, NEWTON, step, start)
    out[...] = jnp.concatenate([w[0:1] for w in weights], axis=0)


def newton(arrived, target, blocks):
    rows, samples = arrived.shape
    traits = target.shape[0]
    predictors = rows // traits
    weights = pl.pallas_call(
        functools.partial(newton_kernel, traits, blocks),
        out_shape=jax.ShapeDtypeStruct((RIDGES, LANES), jnp.float32),
        in_specs=[pl.BlockSpec(memory_space=pltpu.VMEM)] * 2,
        out_specs=pl.BlockSpec(memory_space=pltpu.VMEM),
        scratch_shapes=[
            pltpu.VMEM((rows, samples), jnp.bfloat16),
            pltpu.VMEM((traits // 2, 2 * predictors + 2 * traits, samples), jnp.bfloat16),
        ],
        compiler_params=pltpu.CompilerParams(vmem_limit_bytes=48 << 20),
        name="newton",
    )(arrived, target)
    return weights.reshape(RIDGES, traits, blocks).swapaxes(0, 1).reshape(traits, predictors)


def fit_traits(arrived, target):
    rows, samples = arrived.shape
    count = target.shape[0]
    predictors = rows // count
    design = arrived.reshape(-1, RIDGES, count, samples).transpose(2, 0, 1, 3)
    design = design.reshape(count, predictors, samples)
    level_ridge = LEVEL_ONE * samples
    weights = jnp.zeros((count, predictors), jnp.float32)
    identity = jnp.eye(predictors, dtype=jnp.float32)
    for _ in range(NEWTON):
        logits = jnp.einsum(
            "kqn,kq->kn", design, weights.astype(jnp.bfloat16), preferred_element_type=jnp.float32
        )
        prob = jax.nn.sigmoid(logits)
        resid = (target - prob).astype(jnp.bfloat16)
        weighted = (design * (prob * (1.0 - prob))[:, None, :]).astype(jnp.bfloat16)
        gram = jnp.einsum("kqn,kpn->kqp", weighted, design, preferred_element_type=jnp.float32)
        grad = jnp.einsum("kqn,kn->kq", design, resid, preferred_element_type=jnp.float32)
        grad = grad - level_ridge * weights
        factor = jnp.linalg.cholesky(gram + level_ridge * identity)
        partial_solve = lax.linalg.triangular_solve(
            factor, grad[:, :, None], left_side=True, lower=True
        )
        update = lax.linalg.triangular_solve(
            factor, partial_solve, left_side=True, lower=True, transpose_a=True
        )
        weights = weights + update[:, :, 0]
    return weights.reshape(count, -1, RIDGES).swapaxes(1, 2).reshape(count, predictors)


def on_device(dosage, eigvec, eigval, pheno):
    samples, width = dosage.shape
    traits = pheno.shape[1]
    regions = lax.axis_size("region")
    per_device = traits // regions
    shrink = jnp.array([width * (1.0 - value) / value for value in HERITABILITY], jnp.float32)
    std_trait = standardize(pheno)
    std_geno = standardize(dosage)
    cross = lax.dot_general(
        std_trait, std_geno, (((0,), (0,)), ((), ())), preferred_element_type=jnp.float32
    ).astype(jnp.bfloat16)
    rotated = jnp.dot(cross, eigvec, preferred_element_type=jnp.float32)
    scaled = rotated.reshape(regions, 1, per_device, width) / (
        eigval[0][None, None, None, :] + shrink[None, :, None, None]
    )
    scaled = scaled.astype(jnp.bfloat16).reshape(RIDGES * traits, width)
    ridge = lax.dot_general(
        scaled, eigvec, (((1,), (1,)), ((), ())), preferred_element_type=jnp.float32
    ).astype(jnp.bfloat16)
    predicted = lax.dot_general(
        ridge, std_geno, (((1,), (1,)), ((), ())), preferred_element_type=jnp.float32
    ).astype(jnp.bfloat16)
    arrived = lax.all_to_all(predicted, "region", split_axis=0, concat_axis=0, tiled=True)
    position = lax.axis_index("region")
    target = lax.dynamic_slice_in_dim(pheno, position * per_device, per_device, 1)
    target = target.astype(jnp.float32).T
    if per_device == SUBLANES and per_device * regions == LANES:
        return newton(arrived, target, regions)
    return fit_traits(arrived, target)


def solution(mesh):
    return jax.shard_map(
        on_device,
        mesh=mesh,
        in_specs=(
            P("cohort", "region"),
            P("region", "cohort"),
            P("cohort", "region"),
            P("cohort", None),
        ),
        out_specs=P("region", "cohort"),
        check_vma=False,
    )
```

time: 108 us -> 88.7 us (0.82)
  Pallas kernels: 32.7 us -> 13.2 us
    pallas_call x1, Pallas kernels: 32.7 us -> 13.2 us  [newton(): pl.pallas_call(functools.partial(newton_kernel, traits, blocks), out_shap...]
where the time goes in v2:
time: 88.7 us; the launch traced here: 88.1 us
  waiting for transfers between devices  46.8 us (53%)
  Pallas kernels  13.2 us (15%)
  matrix products  10.6 us (12%)
  other arithmetic  9.29 us (10%)
  starting transfers between devices  6.5 us (7%)
  local copies, waits for them, and re-layouts  1.71 us (2%)
    all_to_all x1, waiting for transfers between devices, on_device(): lax.all_to_all(predicted, 'region', split_axis=0, concat_axis=0, tiled=True)  46.8 us
    pallas_call x1, Pallas kernels, newton(): pl.pallas_call(functools.partial(newton_kernel, traits, blocks), out_shap...  13.2 us
    dot_general x1, matrix products, on_device(): lax.dot_general(ridge, std_geno, (((1,), (1,)), ((), ())), preferred_elem...  7.3 us
    all_to_all x1, starting transfers between devices, on_device(): lax.all_to_all(predicted, 'region', split_axis=0, concat_axis=0, tiled=True)  6.5 us
    reduce_sum x2, other arithmetic, standardize(): center = jnp.mean(values, axis=0)  3.33 us
    dot_general x1, matrix products, on_device(): rotated = jnp.dot(cross, eigvec, preferred_element_type=jnp.float32)  3.28 us
    convert_element_type x1, other arithmetic, standardize(): return ((values - center) / spread).astype(jnp.bfloat16)  3.21 us
  transfers between devices with their start and end apart: 1, of which 1 were waited for; matrix products, arithmetic and copies ran while one was open for 0% of the time, Pallas kernels for 0%

profile of v2, /device:TPU:17, one launch (start us, length us, event | category | flops | bytes accessed | tf_op | source)
XLA Modules:
  0.0 88.1 jit_solution(8490774073984220807)
XLA Ops:
  0.0 0.0 copy-start
  0.0 0.0 copy-start.1
  0.0 3.0 %convert_reduce_fusion = f32[1024]{0:T(1024)S(1)} fusion(bf16[2048,1024]{1,0:T(8,128)(2,1)} %param.5), kind=kLoop, calls=%fused_computation.1 | loop fusion | flops 4193280 | bytes 4198400 | tf_op jit(solution)/shard_map/reduce_sum | solution.py:22
  3.1 0.5 copy-done.1
  3.6 1.1 %fusion.2 = f32[1024]{0:T(1024)S(1)} fusion(bf16[2048,1024]{1,0:T(8,128)(2,1)S(1)} %copy-done.1, f32[1024]{0:T(1024)S(1)} %broadcast_multiply_fusion), kind=kLoop, calls=%fused_computation.4 | loop fusion | flops 8387584 | bytes 4202496 | tf_op jit(solution)/shard_map/reduce_sum | solution.py:23
  4.8 0.0 copy-start.2
  4.8 0.0 copy-start.3
  4.8 0.0 copy-start.4
  4.8 3.2 %fusion.3 = bf16[2048,1024]{1,0:T(8,128)(2,1)} fusion(bf16[2048,1024]{1,0:T(8,128)(2,1)S(1)} %copy-done.1, f32[1024]{0:T(1024)S(1)} %add_sqrt_fusion, f32[1024]{0:T(1024)S(1)} %broadcast_multiply_fusion), kind=kLoop, calls=%fused_computation.5 | loop fusion | flops 8388608 | bytes 8396800 | tf_op jit(solution)/shard_map/convert_element_type | solution.py:24
  8.0 0.0 copy-done.2
  8.0 0.3 convert_reduce_fusion.1
  8.3 0.3 fusion.6
  8.6 0.0 copy-done.3
  8.6 0.0 copy-done.4
  8.6 0.1 broadcast_add_fusion
  8.7 0.0 copy-done
  8.7 3.3 %convolution_bitcast_fusion = f32[16,8,1024]{2,1,0:T(8,128)S(1)} fusion(bf16[1024,1024]{1,0:T(8,128)(2,1)S(1)} %copy-done, bf16[2048,1024]{1,0:T(8,128)(2,1)} %fusion.3, bf16[2048,128]{1,0:T(8,128)(2,1)S(1)} %copy-done.2, f32[128]{0:T(128)S(1)} %add_sqrt_fusion.1, f32[128]{0:T(128)S(1)} %broadcast_multiply_fusion.1), kind=kOutput, calls=%fused_computation.13 | convolution fusion | flops 806486016 | bytes 7341056 | tf_op jit(solution)/shard_map/dot_general | solution.py:290
  12.0 1.2 %divide_convert_fusion = bf16[16,4,8,1024]{3,2,1,0:T(8,128)(2,1)} fusion(f32[4,1024]{1,0:T(4,128)S(1)} %broadcast_add_fusion, f32[16,8,1024]{2,1,0:T(8,128)S(1)} %convolution_bitcast_fusion), kind=kLoop, calls=%fused_computation.7 | loop fusion | flops 1048576 | bytes 1589248 | tf_op jit(solution)/shard_map/convert_element_type | solution.py:294
  13.2 7.3 %convolution_convert_fusion = bf16[512,2048]{1,0:T(8,128)(2,1)} fusion(bf16[2048,1024]{1,0:T(8,128)(2,1)} %fusion.3, bf16[512,1024]{1,0:T(8,128)(2,1)} %bitcast.15, bf16[1024,1024]{1,0:T(8,128)(2,1)S(1)} %copy-done), kind=kOutput, calls=%fused_computation.6 | convolution fusion | flops 3222798336 | bytes 9437184 | tf_op jit(solution)/shard_map/dot_general | solution.py:298
  20.5 6.5 %all-to-all-start = ((bf16[16,32,2048]{2,1,0:T(8,128)(2,1)}), bf16[16,32,2048]{2,1,0:T(8,128)(2,1)}, u32[]{:S(2)}, u32[]{:S(2)}) async-start(bf16[16,32,2048]{2,1,0:T(8,128)(2,1)} %bitcast.14), calls=%async_computation | async-start | bytes 4194304 | tf_op jit(solution)/shard_map/all_to_all | solution.py:301
  27.0 0.2 constant_dynamic-slice_fusion
  27.2 0.2 copy.8
  27.4 46.8 %all-to-all-done = bf16[16,32,2048]{2,1,0:T(8,128)(2,1)} async-done(((bf16[16,32,2048]{2,1,0:T(8,128)(2,1)}), bf16[16,32,2048]{2,1,0:T(8,128)(2,1)}, u32[]{:S(2)}, u32[]{:S(2)}) %all-to-all-start) | async-done | bytes 2097184 | tf_op jit(solution)/shard_map/all_to_all | solution.py:301
  74.2 13.2 %newton.1 = f32[4,128]{1,0:T(4,128)S(1)} custom-call(bf16[512,2048]{1,0:T(8,128)(2,1)} %bitcast.4.arrived, f32[8,2048]{1,0:T(8,128)S(1)} %convert_bitcast_fusion.target), custom_call_target="tpu_custom_call" | custom-call | tf_op jit(solution)/shard_map/newton/pallas_call | solution.py:234
  87.4 0.1 reshape.64
  87.5 0.7 reshape.65
  (6 shorter events, 0.1 us)
Async XLA Ops:
  0.0 8.7 %copy-start = (bf16[1024,1024]{1,0:T(8,128)(2,1)S(1)}, bf16[1024,1024]{1,0:T(8,128)(2,1)}, u32[]{:S(2)}) copy-start(bf16[1024,1024]{1,0:T(8,128)(2,1)} %param.6) | copy-start | bytes 6291460
  0.0 3.6 %copy-start.1 = (bf16[2048,1024]{1,0:T(8,128)(2,1)S(1)}, bf16[2048,1024]{1,0:T(8,128)(2,1)}, u32[]{:S(2)}) copy-start(bf16[2048,1024]{1,0:T(8,128)(2,1)} %param.5) | copy-start | bytes 12582916
  4.8 3.2 %copy-start.2 = (bf16[2048,128]{1,0:T(8,128)(2,1)S(1)}, bf16[2048,128]{1,0:T(8,128)(2,1)}, u32[]{:S(2)}) copy-start(bf16[2048,128]{1,0:T(8,128)(2,1)} %param.8) | copy-start | bytes 1572868
  4.8 3.8 %copy-start.3 = (f32[1,1024]{1,0:T(1,128)S(1)}, f32[1,1024]{1,0:T(1,128)}, u32[]{:S(2)}) copy-start(f32[1,1024]{1,0:T(1,128)} %param.7) | copy-start | bytes 12292
  4.8 3.8 %copy-start.4 = (f32[4]{0:T(128)S(1)}, f32[4]{0:T(128)}, u32[]{:S(2)}) copy-start(f32[4]{0:T(128)} %constant.24.clone) | copy-start | bytes 52
  20.5 53.7 %all-to-all-start = ((bf16[16,32,2048]{2,1,0:T(8,128)(2,1)}), bf16[16,32,2048]{2,1,0:T(8,128)(2,1)}, u32[]{:S(2)}, u32[]{:S(2)}) async-start(bf16[16,32,2048]{2,1,0:T(8,128)(2,1)} %bitcast.14), calls=%async_computation | async-start | bytes 4194304 | tf_op jit(solution)/shard_map/all_to_all | solution.py:301

commit v3 on v2

--- a/solution.py
+++ b/solution.py
@@ -15,13 +15,146 @@
 LANES = 128
 SUBLANES = 8
 TILE = 256
-
-
-def standardize(values):
-    values = values.astype(jnp.float32)
-    center = jnp.mean(values, axis=0)
-    spread = jnp.sqrt(jnp.mean(jnp.square(values - center), axis=0) + EPSILON)
-    return ((values - center) / spread).astype(jnp.bfloat16)
+WIDE = 512
+
+
+def level_zero_kernel(
+    dosage_hbm, eigvec_hbm, eigval, pheno, out_hbm, dosage, eigvec, covariance, squares, scaled, slope, predicted, sems
+):
+    samples, width = dosage.shape
+    traits = pheno.shape[1]
+    chunks = width // TILE
+    copies = [
+        pltpu.make_async_copy(
+            dosage_hbm.at[:, pl.ds(c * TILE, TILE)], dosage.at[:, pl.ds(c * TILE, TILE)], sems.at[c]
+        )
+        for c in range(chunks)
+    ]
+    basis = pltpu.make_async_copy(eigvec_hbm, eigvec, sems.at[chunks])
+    for copy in copies:
+        copy.start()
+    basis.start()
+
+    row = lax.broadcasted_iota(jnp.int32, (traits, traits), 0)
+    column = lax.broadcasted_iota(jnp.int32, (traits, traits), 1)
+    turned = lax.dot_general(
+        jnp.where(row == column, 1.0, 0.0).astype(jnp.bfloat16),
+        pheno[...],
+        (((1,), (1,)), ((), ())),
+        preferred_element_type=jnp.float32,
+    )
+    cases = jnp.sum(turned, axis=1, keepdims=True)
+    center = cases / samples
+    spread = jnp.sqrt(
+        (cases * samples - cases * cases) / (samples * float(samples)) + EPSILON
+    )
+    ones = ((1.0 - center) / spread).astype(jnp.bfloat16).astype(jnp.float32)
+    zeros = ((0.0 - center) / spread).astype(jnp.bfloat16).astype(jnp.float32)
+    delta = ones - zeros
+    left = jnp.concatenate([turned, jnp.ones((2 * SUBLANES, samples), jnp.float32)], axis=0).astype(
+        jnp.bfloat16
+    )
+    for c in range(chunks):
+        copies[c].wait()
+        part = dosage[:, c * TILE : (c + 1) * TILE]
+        covariance[:, c * TILE : (c + 1) * TILE] = jnp.dot(
+            left, part, preferred_element_type=jnp.float32
+        )
+        square = part * part
+        rows = samples
+        while rows > 4 * SUBLANES:
+            rows //= 2
+            square = square[:rows] + square[rows : 2 * rows]
+        squares[:, c * TILE : (c + 1) * TILE] = jnp.sum(
+            square.astype(jnp.float32), axis=0, keepdims=True
+        )
+    total = covariance[traits : traits + 1, :]
+    mean = total / samples
+    deviation = jnp.sqrt(
+        (squares[...] * samples - total * total) / (samples * float(samples)) + EPSILON
+    )
+    inverse = 1.0 / deviation
+    cross = (
+        (covariance[:traits, :] - cases * mean) * delta * inverse
+    ).astype(jnp.bfloat16)
+    basis.wait()
+    rotated = jnp.dot(cross, eigvec[...], preferred_element_type=jnp.float32)
+    for r, value in enumerate(HERITABILITY):
+        shrunk = rotated * (1.0 / (eigval[...] + width * (1.0 - value) / value))
+        for g in range(traits // SUBLANES):
+            start = (g * RIDGES + r) * SUBLANES
+            scaled[start : start + SUBLANES, :] = shrunk[
+                g * SUBLANES : (g + 1) * SUBLANES
+            ].astype(jnp.bfloat16)
+    for c in range(chunks):
+        ridge = lax.dot_general(
+            scaled[...],
+            eigvec[c * TILE : (c + 1) * TILE, :],
+            (((1,), (1,)), ((), ())),
+            preferred_element_type=jnp.float32,
+        )
+        slope[:, c * TILE : (c + 1) * TILE] = (
+            ridge * inverse[:, c * TILE : (c + 1) * TILE]
+        ).astype(jnp.bfloat16)
+    high = mean.astype(jnp.bfloat16).astype(jnp.float32)
+    low = (mean - high).astype(jnp.bfloat16).astype(jnp.float32)
+    rest = mean - high - low
+    place = lax.broadcasted_iota(jnp.int32, (2 * SUBLANES, width), 0)
+    means = jnp.where(place == 0, high, jnp.where(place == 1, low, jnp.where(place == 2, rest, 0.0)))
+    offset = jnp.sum(
+        lax.dot_general(
+            slope[...],
+            means.astype(jnp.bfloat16),
+            (((1,), (1,)), ((), ())),
+            preferred_element_type=jnp.float32,
+        ),
+        axis=1,
+        keepdims=True,
+    )
+    outs = []
+    for n in range(samples // WIDE):
+        found = lax.dot_general(
+            slope[...],
+            dosage[n * WIDE : (n + 1) * WIDE, :],
+            (((1,), (1,)), ((), ())),
+            preferred_element_type=jnp.float32,
+        )
+        predicted[:, n * WIDE : (n + 1) * WIDE] = (found - offset).astype(jnp.bfloat16)
+        copy = pltpu.make_async_copy(
+            predicted.at[:, pl.ds(n * WIDE, WIDE)],
+            out_hbm.at[:, pl.ds(n * WIDE, WIDE)],
+            sems.at[chunks + 1 + n],
+        )
+        copy.start()
+        outs.append(copy)
+    for copy in outs:
+        copy.wait()
+
+
+def level_zero(dosage, eigvec, eigval, pheno):
+    samples, width = dosage.shape
+    traits = pheno.shape[1]
+    rows = RIDGES * traits
+    anywhere = pl.BlockSpec(memory_space=pl.ANY)
+    inside = pl.BlockSpec(memory_space=pltpu.VMEM)
+    return pl.pallas_call(
+        level_zero_kernel,
+        out_shape=jax.ShapeDtypeStruct((rows, samples), jnp.bfloat16),
+        in_specs=[anywhere, anywhere, inside, inside],
+        out_specs=anywhere,
+        scratch_shapes=[
+            pltpu.VMEM((samples, width), jnp.bfloat16),
+            pltpu.VMEM((width, width), jnp.bfloat16),
+            pltpu.VMEM((traits + 2 * SUBLANES, width), jnp.float32),
+            pltpu.VMEM((1, width), jnp.float32),
+            pltpu.VMEM((rows, width), jnp.bfloat16),
+            pltpu.VMEM((rows, width), jnp.bfloat16),
+            pltpu.VMEM((rows, samples), jnp.bfloat16),
+            pltpu.SemaphoreType.DMA((width // TILE + 1 + samples // WIDE,)),
+        ],
+        compiler_params=pltpu.CompilerParams(vmem_limit_bytes=48 << 20),
+        name="level_zero",
+    )(dosage, eigvec, eigval, pheno)
 
 
 def reorder_matrix(traits, blocks, parts):
@@ -277,27 +410,13 @@
 
 
 def on_device(dosage, eigvec, eigval, pheno):
-    samples, width = dosage.shape
     traits = pheno.shape[1]
     regions = lax.axis_size("region")
     per_device = traits // regions
-    shrink = jnp.array([width * (1.0 - value) / value for value in HERITABILITY], jnp.float32)
-    std_trait = standardize(pheno)
-    std_geno = standardize(dosage)
-    cross = lax.dot_general(
-        std_trait, std_geno, (((0,), (0,)), ((), ())), preferred_element_type=jnp.float32
-    ).astype(jnp.bfloat16)
-    rotated = jnp.dot(cross, eigvec, preferred_element_type=jnp.float32)
-    scaled = rotated.reshape(regions, 1, per_device, width) / (
-        eigval[0][None, None, None, :] + shrink[None, :, None, None]
-    )
-    scaled = scaled.astype(jnp.bfloat16).reshape(RIDGES * traits, width)
-    ridge = lax.dot_general(
-        scaled, eigvec, (((1,), (1,)), ((), ())), preferred_element_type=jnp.float32
-    ).astype(jnp.bfloat16)
-    predicted = lax.dot_general(
-        ridge, std_geno, (((1,), (1,)), ((), ())), preferred_element_type=jnp.float32
-    ).astype(jnp.bfloat16)
+    predicted = level_zero(dosage, eigvec, eigval, pheno)
+    if per_device != SUBLANES:
+        predicted = predicted.reshape(-1, RIDGES, SUBLANES // per_device, per_device, dosage.shape[0])
+        predicted = predicted.swapaxes(1, 2).reshape(RIDGES * traits, dosage.shape[0])
     arrived = lax.all_to_all(predicted, "region", split_axis=0, concat_axis=0, tiled=True)
     position = lax.axis_index("region")
     target = lax.dynamic_slice_in_dim(pheno, position * per_device, per_device, 1)

time: 88.7 us -> 80 us (0.902)
  matrix products: 10.6 us -> 0 us
  other arithmetic: 9.29 us -> 0.01 us
  Pallas kernels: 13.2 us -> 20.2 us
  local copies, waits for them, and re-layouts: 1.71 us -> 5.81 us
    dot_general x2 -> x0, matrix products: 10.6 us -> none  [the longest x1 7.3 us: on_device(): lax.dot_general(ridge, std_geno, (((1,), (1,)), ((), ())), preferred_elem...]
    pallas_call x0 -> x1, Pallas kernels: none -> 8.59 us  [level_zero(): pl.pallas_call(level_zero_kernel, out_shape=jax.ShapeDtypeStruct((rows, s...]
    reduce_sum x4 -> x0, other arithmetic: 4.77 us -> none  [the longest x2 3.33 us: standardize(): center = jnp.mean(values, axis=0)]
    convert_element_type x2 -> x0, other arithmetic: 4.4 us -> none  [the longest x1 3.21 us: standardize(): return ((values - center) / spread).astype(jnp.bfloat16)]
    unnamed x11, local copies, waits for them, and re-layouts: 0.73 us -> 4.84 us
    pallas_call x1, Pallas kernels: 13.2 us -> 11.6 us  [newton(): pl.pallas_call(functools.partial(newton_kernel, traits, blocks), out_shap...]
where the time goes in v3:
time: 80 us; the launch traced here: 79.4 us
  waiting for transfers between devices  46.7 us (58%)
  Pallas kernels  20.2 us (25%)
  starting transfers between devices  6.63 us (8%)
  local copies, waits for them, and re-layouts  5.81 us (7%)
    all_to_all x1, waiting for transfers between devices, on_device(): lax.all_to_all(predicted, 'region', split_axis=0, concat_axis=0, tiled=True)  46.7 us
    pallas_call x1, Pallas kernels, newton(): pl.pallas_call(functools.partial(newton_kernel, traits, blocks), out_shap...  11.6 us
    pallas_call x1, Pallas kernels, level_zero(): pl.pallas_call(level_zero_kernel, out_shape=jax.ShapeDtypeStruct((rows, s...  8.59 us
    all_to_all x1, starting transfers between devices, on_device(): lax.all_to_all(predicted, 'region', split_axis=0, concat_axis=0, tiled=True)  6.63 us
    unnamed x11, local copies, waits for them, and re-layouts  4.84 us
  transfers between devices with their start and end apart: 1, of which 1 were waited for; matrix products, arithmetic and copies ran while one was open for 0% of the time, Pallas kernels for 0%

profile of v3, /device:TPU:17, one launch (start us, length us, event | category | flops | bytes accessed | tf_op | source)
XLA Modules:
  0.0 79.4 jit_solution(4451672367707698139)
XLA Ops:
  0.0 0.0 copy-start.1
  0.0 1.0 %copy-done.1 = bf16[2048,128]{1,0:T(8,128)(2,1)S(1)} copy-done((bf16[2048,128]{1,0:T(8,128)(2,1)S(1)}, bf16[2048,128]{1,0:T(8,128)(2,1)}, u32[]{:S(2)}) %copy-start.1) | copy-done | bytes 524312
  1.0 0.0 copy-start.3
  1.0 1.6 %copy-done.3 = bf16[1024,1024]{1,0:T(8,128)(2,1)S(1)} copy-done((bf16[1024,1024]{1,0:T(8,128)(2,1)S(1)}, bf16[1024,1024]{1,0:T(8,128)(2,1)}, u32[]{:S(2)}) %copy-start.3) | copy-done | bytes 2097176
  2.6 0.0 copy-start.4
  2.6 0.7 copy-done.4
  3.3 8.6 %level_zero.1 = bf16[512,2048]{1,0:T(8,128)(2,1)S(1)} custom-call(bf16[2048,1024]{1,0:T(8,128)(2,1)} %dosage_hbm.1, bf16[1024,1024]{1,0:T(8,128)(2,1)S(1)} %copy-done.3, f32[1,1024]{1,0:T(1,128)S(1)} %copy-done.4, bf16[2048,128]{1,0:T(8,128)(2,1)S(1)} %copy-done.1), custom_call_target="tpu_custom_call" | custom-call | tf_op jit(solution)/shard_map/level_zero/pallas_call | solution.py:140
  11.9 0.0 copy-start
  11.9 1.3 %copy-done = bf16[512,2048]{1,0:T(8,128)(2,1)} copy-done((bf16[512,2048]{1,0:T(8,128)(2,1)}, bf16[512,2048]{1,0:T(8,128)(2,1)S(1)}, u32[]{:S(2)}) %copy-start) | copy-done | bytes 2097176
  13.3 0.0 copy-start.2
  13.3 6.6 %all-to-all-start = ((bf16[16,32,2048]{2,1,0:T(8,128)(2,1)}), bf16[16,32,2048]{2,1,0:T(8,128)(2,1)S(1)}, u32[]{:S(2)}, u32[]{:S(2)}) async-start(bf16[16,32,2048]{2,1,0:T(8,128)(2,1)} %bitcast.6), calls=%async_computation | async-start | bytes 4194304 | tf_op jit(solution)/shard_map/all_to_all | solution.py:420
  19.9 0.0 copy-done.2
  19.9 0.2 constant_dynamic-slice_fusion
  20.1 0.2 copy.7
  20.3 46.7 %all-to-all-done = bf16[16,32,2048]{2,1,0:T(8,128)(2,1)S(1)} async-done(((bf16[16,32,2048]{2,1,0:T(8,128)(2,1)}), bf16[16,32,2048]{2,1,0:T(8,128)(2,1)S(1)}, u32[]{:S(2)}, u32[]{:S(2)}) %all-to-all-start) | async-done | bytes 2097184 | tf_op jit(solution)/shard_map/all_to_all | solution.py:420
  67.0 11.6 %newton.1 = f32[4,128]{1,0:T(4,128)S(1)} custom-call(bf16[512,2048]{1,0:T(8,128)(2,1)S(1)} %bitcast.5, f32[8,2048]{1,0:T(8,128)S(1)} %convert_bitcast_fusion.target), custom_call_target="tpu_custom_call" | custom-call | tf_op jit(solution)/shard_map/newton/pallas_call | solution.py:367
  78.6 0.1 reshape.8
  78.7 0.7 reshape.9
  (2 shorter events, 0.0 us)
Async XLA Ops:
  0.0 1.0 %copy-start.1 = (bf16[2048,128]{1,0:T(8,128)(2,1)S(1)}, bf16[2048,128]{1,0:T(8,128)(2,1)}, u32[]{:S(2)}) copy-start(bf16[2048,128]{1,0:T(8,128)(2,1)} %pheno.1) | copy-start | bytes 1572868
  1.0 1.6 %copy-start.3 = (bf16[1024,1024]{1,0:T(8,128)(2,1)S(1)}, bf16[1024,1024]{1,0:T(8,128)(2,1)}, u32[]{:S(2)}) copy-start(bf16[1024,1024]{1,0:T(8,128)(2,1)} %eigvec_hbm.1) | copy-start | bytes 6291460
  2.6 0.7 copy-start.4
  11.9 1.4 %copy-start = (bf16[512,2048]{1,0:T(8,128)(2,1)}, bf16[512,2048]{1,0:T(8,128)(2,1)S(1)}, u32[]{:S(2)}) copy-start(bf16[512,2048]{1,0:T(8,128)(2,1)S(1)} %level_zero.1) | copy-start | bytes 6291460
  13.3 6.6 %copy-start.2 = (bf16[2048,128]{1,0:T(8,128)(2,1)S(1)}, bf16[2048,128]{1,0:T(8,128)(2,1)}, u32[]{:S(2)}) copy-start(bf16[2048,128]{1,0:T(8,128)(2,1)} %pheno.1) | copy-start | bytes 1572868
  13.3 53.8 %all-to-all-start = ((bf16[16,32,2048]{2,1,0:T(8,128)(2,1)}), bf16[16,32,2048]{2,1,0:T(8,128)(2,1)S(1)}, u32[]{:S(2)}, u32[]{:S(2)}) async-start(bf16[16,32,2048]{2,1,0:T(8,128)(2,1)} %bitcast.6), calls=%async_computation | async-start | bytes 4194304 | tf_op jit(solution)/shard_map/all_to_all | solution.py:420

commit v4 on v3

--- a/solution.py
+++ b/solution.py
@@ -19,7 +19,21 @@
 
 
 def level_zero_kernel(
-    dosage_hbm, eigvec_hbm, eigval, pheno, out_hbm, dosage, eigvec, covariance, squares, scaled, slope, predicted, sems
+    dosage_hbm,
+    eigvec_hbm,
+    eigval_hbm,
+    pheno_hbm,
+    out_hbm,
+    dosage,
+    eigvec,
+    eigval,
+    pheno,
+    covariance,
+    squares,
+    scaled,
+    slope,
+    predicted,
+    sems,
 ):
     samples, width = dosage.shape
     traits = pheno.shape[1]
@@ -30,13 +44,18 @@
         )
         for c in range(chunks)
     ]
-    basis = pltpu.make_async_copy(eigvec_hbm, eigvec, sems.at[chunks])
+    cases_copy = pltpu.make_async_copy(pheno_hbm, pheno, sems.at[chunks])
+    basis = pltpu.make_async_copy(eigvec_hbm, eigvec, sems.at[chunks + 1])
+    values = pltpu.make_async_copy(eigval_hbm, eigval, sems.at[chunks + 2])
+    cases_copy.start()
     for copy in copies:
         copy.start()
     basis.start()
+    values.start()
 
     row = lax.broadcasted_iota(jnp.int32, (traits, traits), 0)
     column = lax.broadcasted_iota(jnp.int32, (traits, traits), 1)
+    cases_copy.wait()
     turned = lax.dot_general(
         jnp.where(row == column, 1.0, 0.0).astype(jnp.bfloat16),
         pheno[...],
@@ -78,6 +97,7 @@
         (covariance[:traits, :] - cases * mean) * delta * inverse
     ).astype(jnp.bfloat16)
     basis.wait()
+    values.wait()
     rotated = jnp.dot(cross, eigvec[...], preferred_element_type=jnp.float32)
     for r, value in enumerate(HERITABILITY):
         shrunk = rotated * (1.0 / (eigval[...] + width * (1.0 - value) / value))
@@ -123,7 +143,7 @@
         copy = pltpu.make_async_copy(
             predicted.at[:, pl.ds(n * WIDE, WIDE)],
             out_hbm.at[:, pl.ds(n * WIDE, WIDE)],
-            sems.at[chunks + 1 + n],
+            sems.at[chunks + 3 + n],
         )
         copy.start()
         outs.append(copy)
@@ -136,23 +156,24 @@
     traits = pheno.shape[1]
     rows = RIDGES * traits
     anywhere = pl.BlockSpec(memory_space=pl.ANY)
-    inside = pl.BlockSpec(memory_space=pltpu.VMEM)
     return pl.pallas_call(
         level_zero_kernel,
         out_shape=jax.ShapeDtypeStruct((rows, samples), jnp.bfloat16),
-        in_specs=[anywhere, anywhere, inside, inside],
+        in_specs=[anywhere] * 4,
         out_specs=anywhere,
         scratch_shapes=[
             pltpu.VMEM((samples, width), jnp.bfloat16),
             pltpu.VMEM((width, width), jnp.bfloat16),
+            pltpu.VMEM((1, width), jnp.float32),
+            pltpu.VMEM((samples, traits), jnp.bfloat16),
             pltpu.VMEM((traits + 2 * SUBLANES, width), jnp.float32),
             pltpu.VMEM((1, width), jnp.float32),
             pltpu.VMEM((rows, width), jnp.bfloat16),
             pltpu.VMEM((rows, width), jnp.bfloat16),
             pltpu.VMEM((rows, samples), jnp.bfloat16),
-            pltpu.SemaphoreType.DMA((width // TILE + 1 + samples // WIDE,)),
+            pltpu.SemaphoreType.DMA((width // TILE + 3 + samples // WIDE,)),
         ],
-        compiler_params=pltpu.CompilerParams(vmem_limit_bytes=48 << 20),
+        compiler_params=pltpu.CompilerParams(vmem_limit_bytes=63 << 20),
         name="level_zero",
     )(dosage, eigvec, eigval, pheno)
 
@@ -213,22 +234,21 @@
 
 def solve(table, span):
     heights, tiles = len(table), len(table[0])
+    size = (tiles - 1) * SUBLANES
     lane = lax.broadcasted_iota(jnp.int32, (SUBLANES, LANES), 1)
     within = lane % span
-    for k in range(0, (tiles - 1) * SUBLANES, 4):
+
+    def pivot_rows(k):
+        lanes = (lane - within) + k % span
+        return [
+            [gather_lanes(table[k // span][r], lanes + m) for r in range(k // SUBLANES, tiles)]
+            for m in range(4)
+        ]
+
+    rows = pivot_rows(0)
+    for k in range(0, size, 4):
         home, low = k // span, k % span
         first, sub = k // SUBLANES, k % SUBLANES
-        rows = [
-            [gather_lanes(table[home][r], (lane - within) + low + m) for r in range(first, tiles)]
-            for m in range(4)
-        ]
-        columns = [
-            [
-                jnp.broadcast_to(table[h][first][sub + m : sub + m + 1], (SUBLANES, LANES))
-                for h in range(heights)
-            ]
-            for m in range(4)
-        ]
         pivot = [
             [
                 jnp.broadcast_to(rows[m][0][sub + n : sub + n + 1], (SUBLANES, LANES))
@@ -238,11 +258,17 @@
         ]
         inverse = inverse_four(pivot)
         chosen = (within >= low) & (within < low + 4)
-        for h in range(heights):
+        after = min(k + 4, size - 4)
+        current = rows
+        for h in sorted(range(heights), key=lambda h: h != after // span):
+            columns = [
+                jnp.broadcast_to(table[h][first][sub + m : sub + m + 1], (SUBLANES, LANES))
+                for m in range(4)
+            ]
             factors = []
             for n in range(4):
-                factor = (columns[0][h] * inverse[0][n] + columns[1][h] * inverse[1][n]) + (
-                    columns[2][h] * inverse[2][n] + columns[3][h] * inverse[3][n]
+                factor = (columns[0] * inverse[0][n] + columns[1] * inverse[1][n]) + (
+                    columns[2] * inverse[2][n] + columns[3] * inverse[3][n]
                 )
                 if h == home:
                     for m in range(4):
@@ -252,11 +278,14 @@
                 base = table[h][r]
                 if h == home:
                     base = jnp.where(chosen, 0.0, base)
+                values = [current[m][r - first] for m in range(4)]
                 table[h][r] = (
                     base
-                    - (factors[0] * rows[0][r - first] + factors[1] * rows[1][r - first])
-                    - (factors[2] * rows[2][r - first] + factors[3] * rows[3][r - first])
+                    - (factors[0] * values[0] + factors[1] * values[1])
+                    - (factors[2] * values[2] + factors[3] * values[3])
                 )
+            if h == after // span and k < after:
+                rows = pivot_rows(after)
     return [table[h][tiles - 1] for h in range(heights)]
 
 

time: 80 us -> 75.5 us (0.944)
  local copies, waits for them, and re-layouts: 5.81 us -> 1.15 us
    unnamed x11 -> x3, local copies, waits for them, and re-layouts: 4.84 us -> 0.18 us
  transfers between devices with their start and end apart: 1 -> 1, of which waited for: 1 -> 1; matrix products, arithmetic and copies ran while one was open for 0% -> 1% of each run, Pallas kernels for 0% -> 0%
where the time goes in v4:
time: 75.5 us; the launch traced here: 74.9 us
  waiting for transfers between devices  46.7 us (62%)
  Pallas kernels  20.4 us (27%)
  starting transfers between devices  6.64 us (9%)
  local copies, waits for them, and re-layouts  1.15 us (2%)
    all_to_all x1, waiting for transfers between devices, on_device(): lax.all_to_all(predicted, 'region', split_axis=0, concat_axis=0, tiled=True)  46.7 us
    pallas_call x1, Pallas kernels, newton(): pl.pallas_call(functools.partial(newton_kernel, traits, blocks), out_shap...  11.6 us
    pallas_call x1, Pallas kernels, level_zero(): pl.pallas_call(level_zero_kernel, out_shape=jax.ShapeDtypeStruct((rows, s...  8.8 us
    all_to_all x1, starting transfers between devices, on_device(): lax.all_to_all(predicted, 'region', split_axis=0, concat_axis=0, tiled=True)  6.64 us
  transfers between devices with their start and end apart: 1, of which 1 were waited for; matrix products, arithmetic and copies ran while one was open for 1% of the time, Pallas kernels for 0%

profile of v4, /device:TPU:17, one launch (start us, length us, event | category | flops | bytes accessed | tf_op | source)
XLA Modules:
  0.0 74.9 jit_solution(3912041961525234537)
XLA Ops:
  0.0 8.8 %level_zero.1 = bf16[512,2048]{1,0:T(8,128)(2,1)} custom-call(bf16[2048,1024]{1,0:T(8,128)(2,1)} %dosage_hbm.1, bf16[1024,1024]{1,0:T(8,128)(2,1)} %eigvec_hbm.1, f32[1,1024]{1,0:T(1,128)} %eigval_hbm.1, bf16[2048,128]{1,0:T(8,128)(2,1)} %pheno_hbm.1), custom_call_target="tpu_custom_call" | custom-call | tf_op jit(solution)/shard_map/level_zero/pallas_call | solution.py:159
  8.8 0.0 copy-start
  8.8 6.6 %all-to-all-start = ((bf16[16,32,2048]{2,1,0:T(8,128)(2,1)}), bf16[16,32,2048]{2,1,0:T(8,128)(2,1)S(1)}, u32[]{:S(2)}, u32[]{:S(2)}) async-start(bf16[16,32,2048]{2,1,0:T(8,128)(2,1)} %bitcast.6), calls=%async_computation | async-start | bytes 4194304 | tf_op jit(solution)/shard_map/all_to_all | solution.py:449
  15.5 0.0 copy-done
  15.5 0.2 constant_dynamic-slice_fusion
  15.7 0.2 copy.7
  15.9 46.7 %all-to-all-done = bf16[16,32,2048]{2,1,0:T(8,128)(2,1)S(1)} async-done(((bf16[16,32,2048]{2,1,0:T(8,128)(2,1)}), bf16[16,32,2048]{2,1,0:T(8,128)(2,1)S(1)}, u32[]{:S(2)}, u32[]{:S(2)}) %all-to-all-start) | async-done | bytes 2097184 | tf_op jit(solution)/shard_map/all_to_all | solution.py:449
  62.6 11.6 %newton.1 = f32[4,128]{1,0:T(4,128)S(1)} custom-call(bf16[512,2048]{1,0:T(8,128)(2,1)S(1)} %bitcast.5, f32[8,2048]{1,0:T(8,128)S(1)} %convert_bitcast_fusion.target), custom_call_target="tpu_custom_call" | custom-call | tf_op jit(solution)/shard_map/newton/pallas_call | solution.py:396
  74.2 0.1 reshape.8
  74.2 0.7 reshape.9
  (2 shorter events, 0.0 us)
Async XLA Ops:
  8.8 6.7 %copy-start = (bf16[2048,128]{1,0:T(8,128)(2,1)S(1)}, bf16[2048,128]{1,0:T(8,128)(2,1)}, u32[]{:S(2)}) copy-start(bf16[2048,128]{1,0:T(8,128)(2,1)} %pheno_hbm.1) | copy-start | bytes 1572868
  8.8 53.8 %all-to-all-start = ((bf16[16,32,2048]{2,1,0:T(8,128)(2,1)}), bf16[16,32,2048]{2,1,0:T(8,128)(2,1)S(1)}, u32[]{:S(2)}, u32[]{:S(2)}) async-start(bf16[16,32,2048]{2,1,0:T(8,128)(2,1)} %bitcast.6), calls=%async_computation | async-start | bytes 4194304 | tf_op jit(solution)/shard_map/all_to_all | solution.py:449

commit v5 on v4

--- a/solution.py
+++ b/solution.py
@@ -238,15 +238,7 @@
     lane = lax.broadcasted_iota(jnp.int32, (SUBLANES, LANES), 1)
     within = lane % span
 
-    def pivot_rows(k):
-        lanes = (lane - within) + k % span
-        return [
-            [gather_lanes(table[k // span][r], lanes + m) for r in range(k // SUBLANES, tiles)]
-            for m in range(4)
-        ]
-
-    rows = pivot_rows(0)
-    for k in range(0, size, 4):
+    def eliminate(k, rows, count):
         home, low = k // span, k % span
         first, sub = k // SUBLANES, k % SUBLANES
         pivot = [
@@ -254,38 +246,54 @@
                 jnp.broadcast_to(rows[m][0][sub + n : sub + n + 1], (SUBLANES, LANES))
                 for n in range(4)
             ]
-            for m in range(4)
+            for m in range(count)
         ]
-        inverse = inverse_four(pivot)
+        inverse = inverse_four(pivot[:4])
+
+        def combine(values):
+            return [
+                (values[0] * inverse[0][n] + values[1] * inverse[1][n])
+                + (values[2] * inverse[2][n] + values[3] * inverse[3][n])
+                for n in range(4)
+            ]
+
+        def clear(base, factors, r):
+            return (
+                base
+                - (factors[0] * rows[0][r] + factors[1] * rows[1][r])
+                - (factors[2] * rows[2][r] + factors[3] * rows[3][r])
+            )
+
+        later = []
+        for m in range(4, count):
+            factors = combine(pivot[m])
+            later.append([clear(rows[m][r], factors, r) for r in range(tiles - first)])
         chosen = (within >= low) & (within < low + 4)
-        after = min(k + 4, size - 4)
-        current = rows
-        for h in sorted(range(heights), key=lambda h: h != after // span):
-            columns = [
-                jnp.broadcast_to(table[h][first][sub + m : sub + m + 1], (SUBLANES, LANES))
-                for m in range(4)
-            ]
-            factors = []
-            for n in range(4):
-                factor = (columns[0] * inverse[0][n] + columns[1] * inverse[1][n]) + (
-                    columns[2] * inverse[2][n] + columns[3] * inverse[3][n]
-                )
-                if h == home:
+        for h in sorted(range(heights), key=lambda h: h != min(k + 4, size - 4) // span):
+            factors = combine(
+                [
+                    jnp.broadcast_to(table[h][first][sub + m : sub + m + 1], (SUBLANES, LANES))
+                    for m in range(4)
+                ]
+            )
+            if h == home:
+                for n in range(4):
                     for m in range(4):
-                        factor = jnp.where(within == low + m, -inverse[m][n], factor)
-                factors.append(factor)
+                        factors[n] = jnp.where(within == low + m, -inverse[m][n], factors[n])
             for r in range(first, tiles):
                 base = table[h][r]
                 if h == home:
                     base = jnp.where(chosen, 0.0, base)
-                values = [current[m][r - first] for m in range(4)]
-                table[h][r] = (
-                    base
-                    - (factors[0] * values[0] + factors[1] * values[1])
-                    - (factors[2] * values[2] + factors[3] * values[3])
-                )
-            if h == after // span and k < after:
-                rows = pivot_rows(after)
+                table[h][r] = clear(base, factors, r - first)
+        return later
+
+    for k in range(0, size, 8):
+        lanes = (lane - within) + k % span
+        rows = [
+            [gather_lanes(table[k // span][r], lanes + m) for r in range(k // SUBLANES, tiles)]
+            for m in range(8)
+        ]
+        eliminate(k + 4, eliminate(k, rows, 8), 4)
     return [table[h][tiles - 1] for h in range(heights)]
 
 
@@ -303,7 +311,7 @@
     return tiles
 
 
-def newton_kernel(traits, blocks, arrived, target, out, design, lhs):
+def newton_kernel(traits, blocks, arrived, target, out, design, lhs, table_ref):
     samples = arrived.shape[1]
     predictors = RIDGES * blocks
     half = traits // 2
@@ -325,33 +333,37 @@
     upper = lane >= predictors
     pheno = target[...]
     middle = predictors + 2 * traits
-
-    def step(_, weights):
-        spread_out = [
-            jnp.where((lane // predictors) * half + s == sub, w, 0.0).astype(jnp.bfloat16)
-            for s, w in enumerate(exchange(weights, blocks))
-        ]
-        logits = jnp.dot(
-            jnp.concatenate(spread_out, axis=1), design[...], preferred_element_type=jnp.float32
-        )
-        prob = 1.0 / (1.0 + jnp.exp(-logits))
-        curve = prob * (1.0 - prob)
-        resid = pheno - prob
+    rows = predictors // SUBLANES
+
+    def systems(weights):
+        if weights is None:
+            resid = pheno - 0.5
+        else:
+            spread_out = [
+                jnp.where((lane // predictors) * half + s == sub, w, 0.0).astype(jnp.bfloat16)
+                for s, w in enumerate(exchange(weights, blocks))
+            ]
+            logits = jnp.dot(
+                jnp.concatenate(spread_out, axis=1), design[...], preferred_element_type=jnp.float32
+            )
+            prob = 1.0 / (1.0 + jnp.exp(-logits))
+            curve = prob * (1.0 - prob)
+            resid = pheno - prob
         resid = jnp.concatenate([resid, jnp.zeros_like(resid)], axis=0).astype(jnp.bfloat16)
         found = []
         for s in range(half):
             base = s * 2 * predictors
+            pair = design[base : base + 2 * predictors, :]
+            lhs[s, predictors:middle, :] = resid
             for start, trait, place in ((0, s, 0), (predictors, s + half, middle)):
-                own = design[base + start : base + start + predictors, :].astype(jnp.float32)
-                lhs[s, place : place + predictors, :] = (own * curve[trait : trait + 1, :]).astype(
-                    jnp.bfloat16
-                )
-            lhs[s, predictors:middle, :] = resid
+                own = design[base + start : base + start + predictors, :]
+                if weights is not None:
+                    own = (own.astype(jnp.float32) * curve[trait : trait + 1, :]).astype(
+                        jnp.bfloat16
+                    )
+                lhs[s, place : place + predictors, :] = own
             result = lax.dot_general(
-                lhs[s],
-                design[base : base + 2 * predictors, :],
-                (((1,), (1,)), ((), ())),
-                preferred_element_type=jnp.float32,
+                lhs[s], pair, (((1,), (1,)), ((), ())), preferred_element_type=jnp.float32
             )
             tiles = [
                 jnp.where(
@@ -359,53 +371,64 @@
                     result[middle + SUBLANES * r : middle + SUBLANES * (r + 1)],
                     result[SUBLANES * r : SUBLANES * (r + 1)],
                 )
-                for r in range(predictors // SUBLANES)
+                for r in range(rows)
             ]
+            if weights is None:
+                tiles = [tile * 0.25 for tile in tiles]
             first, second = predictors + s, predictors + s + half
-            tiles.append(
-                jnp.where(
-                    upper[:1], result[second : second + 1], result[first : first + 1]
-                )
-                + jnp.zeros((SUBLANES, LANES), jnp.float32)
-            )
+            gradient = jnp.where(upper[:1], result[second : second + 1], result[first : first + 1])
+            tiles.append(jnp.broadcast_to(gradient, (SUBLANES, LANES)))
             found.append(tiles)
-        table = [[] for _ in range(RIDGES)]
-        for r in range(predictors // SUBLANES + 1):
+        for r in range(rows + 1):
             for h, tile in enumerate(exchange([found[s][r] for s in range(half)], blocks)):
-                if r < predictors // SUBLANES:
+                if r < rows:
                     same = SUBLANES * r + sub == h * blocks + lane % blocks
                     tile = tile + jnp.where(same, level_ridge, 0.0)
-                else:
+                elif weights is not None:
                     tile = tile - level_ridge * weights[h]
-                table[h].append(tile)
+                table_ref[h, r] = tile
+
+    def step(index, weights):
+        table = [[table_ref[h, r] for r in range(rows + 1)] for h in range(RIDGES)]
         solved = solve(table, blocks)
-        return tuple(
+        weights = tuple(
             weights[h] + jnp.broadcast_to(solved[h][0:1], (SUBLANES, LANES))
             for h in range(RIDGES)
         )
 
+        @pl.when(index < NEWTON - 1)
+        def _():
+            systems(weights)
+
+        return weights
+
+    systems(None)
     start = tuple(jnp.zeros((SUBLANES, LANES), jnp.float32) for _ in range(RIDGES))
     weights = lax.fori_loop(0, NEWTON, step, start)
-    out[...] = jnp.concatenate([w[0:1] for w in weights], axis=0)
+    result = jnp.zeros((SUBLANES, LANES), jnp.float32)
+    for s, tile in enumerate(exchange(weights, blocks)):
+        result = jnp.where(sub == s, tile, result)
+        result = jnp.where(sub == s + half, pltpu.roll(tile, predictors, 1), result)
+    out[...] = result[:, :predictors]
 
 
 def newton(arrived, target, blocks):
     rows, samples = arrived.shape
     traits = target.shape[0]
     predictors = rows // traits
-    weights = pl.pallas_call(
+    return pl.pallas_call(
         functools.partial(newton_kernel, traits, blocks),
-        out_shape=jax.ShapeDtypeStruct((RIDGES, LANES), jnp.float32),
+        out_shape=jax.ShapeDtypeStruct((traits, predictors), jnp.float32),
         in_specs=[pl.BlockSpec(memory_space=pltpu.VMEM)] * 2,
         out_specs=pl.BlockSpec(memory_space=pltpu.VMEM),
         scratch_shapes=[
             pltpu.VMEM((rows, samples), jnp.bfloat16),
             pltpu.VMEM((traits // 2, 2 * predictors + 2 * traits, samples), jnp.bfloat16),
+            pltpu.VMEM((RIDGES, predictors // SUBLANES + 1, SUBLANES, LANES), jnp.float32),
         ],
         compiler_params=pltpu.CompilerParams(vmem_limit_bytes=48 << 20),
         name="newton",
     )(arrived, target)
-    return weights.reshape(RIDGES, traits, blocks).swapaxes(0, 1).reshape(traits, predictors)
 
 
 def fit_traits(arrived, target):

time: 75.5 us -> 74.3 us (0.984)
  local copies, waits for them, and re-layouts: 1.15 us -> 0.39 us
    reshape x2 -> x0, local copies, waits for them, and re-layouts: 0.76 us -> none  [newton(): weights.reshape(RIDGES, traits, blocks).swapaxes(0, 1)]
where the time goes in v5:
time: 74.3 us; the launch traced here: 73.7 us
  waiting for transfers between devices  46.7 us (63%)
  Pallas kernels  19.9 us (27%)
  starting transfers between devices  6.64 us (9%)
    all_to_all x1, waiting for transfers between devices, on_device(): lax.all_to_all(predicted, 'region', split_axis=0, concat_axis=0, tiled=True)  46.7 us
    pallas_call x1, Pallas kernels, newton(): pl.pallas_call(functools.partial(newton_kernel, traits, blocks), out_shap...  11.2 us
    pallas_call x1, Pallas kernels, level_zero(): pl.pallas_call(level_zero_kernel, out_shape=jax.ShapeDtypeStruct((rows, s...  8.8 us
    all_to_all x1, starting transfers between devices, on_device(): lax.all_to_all(predicted, 'region', split_axis=0, concat_axis=0, tiled=True)  6.64 us
  transfers between devices with their start and end apart: 1, of which 1 were waited for; matrix products, arithmetic and copies ran while one was open for 1% of the time, Pallas kernels for 0%

profile of v5, /device:TPU:17, one launch (start us, length us, event | category | flops | bytes accessed | tf_op | source)
XLA Modules:
  0.0 73.7 jit_solution(5022637311559499318)
XLA Ops:
  0.0 8.8 %level_zero.1 = bf16[512,2048]{1,0:T(8,128)(2,1)} custom-call(bf16[2048,1024]{1,0:T(8,128)(2,1)} %dosage_hbm.1, bf16[1024,1024]{1,0:T(8,128)(2,1)} %eigvec_hbm.1, f32[1,1024]{1,0:T(1,128)} %eigval_hbm.1, bf16[2048,128]{1,0:T(8,128)(2,1)} %pheno_hbm.1), custom_call_target="tpu_custom_call" | custom-call | tf_op jit(solution)/shard_map/level_zero/pallas_call | solution.py:159
  8.8 0.0 copy-start
  8.8 6.6 %all-to-all-start = ((bf16[16,32,2048]{2,1,0:T(8,128)(2,1)}), bf16[16,32,2048]{2,1,0:T(8,128)(2,1)S(1)}, u32[]{:S(2)}, u32[]{:S(2)}) async-start(bf16[16,32,2048]{2,1,0:T(8,128)(2,1)} %bitcast.5), calls=%async_computation | async-start | bytes 4194304 | tf_op jit(solution)/shard_map/all_to_all | solution.py:472
  15.5 0.0 copy-done
  15.5 0.2 constant_dynamic-slice_fusion
  15.7 0.2 copy.6
  15.9 46.7 %all-to-all-done = bf16[16,32,2048]{2,1,0:T(8,128)(2,1)S(1)} async-done(((bf16[16,32,2048]{2,1,0:T(8,128)(2,1)}), bf16[16,32,2048]{2,1,0:T(8,128)(2,1)S(1)}, u32[]{:S(2)}, u32[]{:S(2)}) %all-to-all-start) | async-done | bytes 2097184 | tf_op jit(solution)/shard_map/all_to_all | solution.py:472
  62.6 11.2 %newton.1 = f32[8,64]{1,0:T(8,128)} custom-call(bf16[512,2048]{1,0:T(8,128)(2,1)S(1)} %bitcast.4, f32[8,2048]{1,0:T(8,128)S(1)} %convert_bitcast_fusion.target), custom_call_target="tpu_custom_call" | custom-call | tf_op jit(solution)/shard_map/newton/pallas_call | solution.py:419
  (1 shorter events, 0.0 us)
Async XLA Ops:
  8.8 6.7 %copy-start = (bf16[2048,128]{1,0:T(8,128)(2,1)S(1)}, bf16[2048,128]{1,0:T(8,128)(2,1)}, u32[]{:S(2)}) copy-start(bf16[2048,128]{1,0:T(8,128)(2,1)} %pheno_hbm.1) | copy-start | bytes 1572868
  8.8 53.8 %all-to-all-start = ((bf16[16,32,2048]{2,1,0:T(8,128)(2,1)}), bf16[16,32,2048]{2,1,0:T(8,128)(2,1)S(1)}, u32[]{:S(2)}, u32[]{:S(2)}) async-start(bf16[16,32,2048]{2,1,0:T(8,128)(2,1)} %bitcast.5), calls=%async_computation | async-start | bytes 4194304 | tf_op jit(solution)/shard_map/all_to_all | solution.py:472

commit v6 on v5

--- a/solution.py
+++ b/solution.py
@@ -16,6 +16,7 @@
 SUBLANES = 8
 TILE = 256
 WIDE = 512
+HALF = 8
 
 
 def level_zero_kernel(
@@ -23,7 +24,21 @@
     eigvec_hbm,
     eigval_hbm,
     pheno_hbm,
-    out_hbm,
+    place,
+    *rest,
+):
+    count = len(rest) - 10
+    outs_hbm, scratch = rest[:count], rest[count:]
+    level_zero_body(dosage_hbm, eigvec_hbm, eigval_hbm, pheno_hbm, place, outs_hbm, *scratch)
+
+
+def level_zero_body(
+    dosage_hbm,
+    eigvec_hbm,
+    eigval_hbm,
+    pheno_hbm,
+    place,
+    outs_hbm,
     dosage,
     eigvec,
     eigval,
@@ -119,8 +134,8 @@
     high = mean.astype(jnp.bfloat16).astype(jnp.float32)
     low = (mean - high).astype(jnp.bfloat16).astype(jnp.float32)
     rest = mean - high - low
-    place = lax.broadcasted_iota(jnp.int32, (2 * SUBLANES, width), 0)
-    means = jnp.where(place == 0, high, jnp.where(place == 1, low, jnp.where(place == 2, rest, 0.0)))
+    line = lax.broadcasted_iota(jnp.int32, (2 * SUBLANES, width), 0)
+    means = jnp.where(line == 0, high, jnp.where(line == 1, low, jnp.where(line == 2, rest, 0.0)))
     offset = jnp.sum(
         lax.dot_general(
             slope[...],
@@ -140,27 +155,36 @@
             preferred_element_type=jnp.float32,
         )
         predicted[:, n * WIDE : (n + 1) * WIDE] = (found - offset).astype(jnp.bfloat16)
-        copy = pltpu.make_async_copy(
-            predicted.at[:, pl.ds(n * WIDE, WIDE)],
-            out_hbm.at[:, pl.ds(n * WIDE, WIDE)],
-            sems.at[chunks + 3 + n],
-        )
-        copy.start()
-        outs.append(copy)
+        for i, out in enumerate(outs_hbm):
+            height = out.shape[0]
+            if len(outs_hbm) == 1:
+                first = 0
+            elif i == 0:
+                first = pl.multiple_of((place[0] // HALF) * height, height)
+            else:
+                first = pl.multiple_of((place[0] ^ (HALF + i - 1)) * height, height)
+            copy = pltpu.make_async_copy(
+                predicted.at[pl.ds(first, height), pl.ds(n * WIDE, WIDE)],
+                out.at[:, pl.ds(n * WIDE, WIDE)],
+                sems.at[chunks + 3 + n * len(outs_hbm) + i],
+            )
+            copy.start()
+            outs.append(copy)
     for copy in outs:
         copy.wait()
 
 
-def level_zero(dosage, eigvec, eigval, pheno):
+def level_zero(dosage, eigvec, eigval, pheno, place, heights):
     samples, width = dosage.shape
     traits = pheno.shape[1]
     rows = RIDGES * traits
     anywhere = pl.BlockSpec(memory_space=pl.ANY)
+    copies = width // TILE + 3 + len(heights) * (samples // WIDE)
     return pl.pallas_call(
         level_zero_kernel,
-        out_shape=jax.ShapeDtypeStruct((rows, samples), jnp.bfloat16),
-        in_specs=[anywhere] * 4,
-        out_specs=anywhere,
+        out_shape=[jax.ShapeDtypeStruct((height, samples), jnp.bfloat16) for height in heights],
+        in_specs=[anywhere] * 4 + [pl.BlockSpec(memory_space=pltpu.SMEM)],
+        out_specs=[anywhere] * len(heights),
         scratch_shapes=[
             pltpu.VMEM((samples, width), jnp.bfloat16),
             pltpu.VMEM((width, width), jnp.bfloat16),
@@ -171,11 +195,11 @@
             pltpu.VMEM((rows, width), jnp.bfloat16),
             pltpu.VMEM((rows, width), jnp.bfloat16),
             pltpu.VMEM((rows, samples), jnp.bfloat16),
-            pltpu.SemaphoreType.DMA((width // TILE + 3 + samples // WIDE,)),
+            pltpu.SemaphoreType.DMA((copies,)),
         ],
         compiler_params=pltpu.CompilerParams(vmem_limit_bytes=63 << 20),
         name="level_zero",
-    )(dosage, eigvec, eigval, pheno)
+    )(dosage, eigvec, eigval, pheno, place)
 
 
 def reorder_matrix(traits, blocks, parts):
@@ -311,18 +335,18 @@
     return tiles
 
 
-def newton_kernel(traits, blocks, arrived, target, out, design, lhs, table_ref):
-    samples = arrived.shape[1]
+def newton_kernel(traits, blocks, place, near, *rest):
+    *far, target, out, design, lhs, table_ref = rest
+    samples = near.shape[1]
     predictors = RIDGES * blocks
     half = traits // 2
-    parts = arrived.shape[0] // TILE
+    parts = 2
     order = reorder_matrix(traits, blocks, parts)
     group = blocks // parts
     for part in range(parts):
-        moved = jnp.dot(
-            order, arrived[part * TILE : (part + 1) * TILE, :], preferred_element_type=jnp.float32
-        )
-        for i in range(TILE // group):
+        arrived = near[...] if part == 0 else jnp.concatenate([block[...] for block in far], axis=0)
+        moved = jnp.dot(order, arrived, preferred_element_type=jnp.float32)
+        for i in range(arrived.shape[0] // group):
             start = i * blocks + part * group
             design[start : start + group, :] = moved[i * group : (i + 1) * group].astype(
                 jnp.bfloat16
@@ -409,26 +433,31 @@
     for s, tile in enumerate(exchange(weights, blocks)):
         result = jnp.where(sub == s, tile, result)
         result = jnp.where(sub == s + half, pltpu.roll(tile, predictors, 1), result)
+    block = lane % blocks
+    own = block // HALF == place[0] // HALF
+    source = jnp.where(own, block % HALF, HALF + (block ^ place[0]) % HALF)
+    result = gather_lanes(result, (lane - block) + source)
     out[...] = result[:, :predictors]
 
 
-def newton(arrived, target, blocks):
-    rows, samples = arrived.shape
+def newton(place, near, far, target, blocks):
+    samples = near.shape[1]
     traits = target.shape[0]
-    predictors = rows // traits
+    predictors = RIDGES * blocks
+    inside = pl.BlockSpec(memory_space=pltpu.VMEM)
     return pl.pallas_call(
         functools.partial(newton_kernel, traits, blocks),
         out_shape=jax.ShapeDtypeStruct((traits, predictors), jnp.float32),
-        in_specs=[pl.BlockSpec(memory_space=pltpu.VMEM)] * 2,
-        out_specs=pl.BlockSpec(memory_space=pltpu.VMEM),
+        in_specs=[pl.BlockSpec(memory_space=pltpu.SMEM)] + [inside] * (len(far) + 2),
+        out_specs=inside,
         scratch_shapes=[
-            pltpu.VMEM((rows, samples), jnp.bfloat16),
+            pltpu.VMEM((traits * predictors, samples), jnp.bfloat16),
             pltpu.VMEM((traits // 2, 2 * predictors + 2 * traits, samples), jnp.bfloat16),
             pltpu.VMEM((RIDGES, predictors // SUBLANES + 1, SUBLANES, LANES), jnp.float32),
         ],
         compiler_params=pltpu.CompilerParams(vmem_limit_bytes=48 << 20),
         name="newton",
-    )(arrived, target)
+    )(place, near, *far, target)
 
 
 def fit_traits(arrived, target):
@@ -462,19 +491,32 @@
 
 
 def on_device(dosage, eigvec, eigval, pheno):
+    samples = dosage.shape[0]
     traits = pheno.shape[1]
     regions = lax.axis_size("region")
     per_device = traits // regions
-    predicted = level_zero(dosage, eigvec, eigval, pheno)
-    if per_device != SUBLANES:
-        predicted = predicted.reshape(-1, RIDGES, SUBLANES // per_device, per_device, dosage.shape[0])
-        predicted = predicted.swapaxes(1, 2).reshape(RIDGES * traits, dosage.shape[0])
-    arrived = lax.all_to_all(predicted, "region", split_axis=0, concat_axis=0, tiled=True)
+    rows = RIDGES * per_device
     position = lax.axis_index("region")
+    place = position.astype(jnp.int32).reshape(1)
     target = lax.dynamic_slice_in_dim(pheno, position * per_device, per_device, 1)
     target = target.astype(jnp.float32).T
-    if per_device == SUBLANES and per_device * regions == LANES:
-        return newton(arrived, target, regions)
+    if per_device == SUBLANES and regions == 2 * HALF:
+        near, *far = level_zero(
+            dosage, eigvec, eigval, pheno, place, [HALF * rows] + [rows] * HALF
+        )
+        halves = [list(range(HALF)), list(range(HALF, 2 * HALF))]
+        near = lax.all_to_all(
+            near, "region", split_axis=0, concat_axis=0, tiled=True, axis_index_groups=halves
+        )
+        far = [
+            lax.ppermute(block, "region", [(i, i ^ (HALF + j)) for i in range(regions)])
+            for j, block in enumerate(far)
+        ]
+        return newton(place, near, far, target, regions)
+    (predicted,) = level_zero(dosage, eigvec, eigval, pheno, place, [RIDGES * traits])
+    predicted = predicted.reshape(-1, RIDGES, SUBLANES // per_device, per_device, samples)
+    predicted = predicted.swapaxes(1, 2).reshape(RIDGES * traits, samples)
+    arrived = lax.all_to_all(predicted, "region", split_axis=0, concat_axis=0, tiled=True)
     return fit_traits(arrived, target)
 
 

time: 74.3 us -> 74.7 us (level)
  starting transfers between devices: 6.64 us -> 21.1 us
  waiting for transfers between devices: 46.7 us -> 32.6 us
    all_to_all x1, waiting for transfers between devices: 46.7 us -> 0.01 us  [on_device(): lax.all_to_all(near, 'region', split_axis=0, concat_axis=0, tiled=True, a...]
    ppermute x0 -> x8, waiting for transfers between devices: none -> 32.6 us  [on_device(): lax.ppermute(block, 'region', [(i, i ^ HALF + j) for i in range(regions)])]
    ppermute x0 -> x8, starting transfers between devices: none -> 16.6 us  [on_device(): lax.ppermute(block, 'region', [(i, i ^ HALF + j) for i in range(regions)])]
    all_to_all x1, starting transfers between devices: 6.64 us -> 4.49 us  [on_device(): lax.all_to_all(near, 'region', split_axis=0, concat_axis=0, tiled=True, a...]
  transfers between devices with their start and end apart: 1 -> 9, of which waited for: 1 -> 5; matrix products, arithmetic and copies ran while one was open for 1% -> 1% of each run, Pallas kernels for 0% -> 0%
where the time goes in v6:
time: 74.7 us; the launch traced here: 74.5 us
  waiting for transfers between devices  32.6 us (44%)
  starting transfers between devices  21.1 us (28%)
  Pallas kernels  20.4 us (27%)
    ppermute x8, waiting for transfers between devices, on_device(): lax.ppermute(block, 'region', [(i, i ^ HALF + j) for i in range(regions)])  32.6 us
    ppermute x8, starting transfers between devices, on_device(): lax.ppermute(block, 'region', [(i, i ^ HALF + j) for i in range(regions)])  16.6 us
    pallas_call x1, Pallas kernels, newton(): pl.pallas_call(functools.partial(newton_kernel, traits, blocks), out_shap...  11.2 us
    pallas_call x1, Pallas kernels, level_zero(): pl.pallas_call(level_zero_kernel, out_shape=[jax.ShapeDtypeStruct((height...  9.17 us
    all_to_all x1, starting transfers between devices, on_device(): lax.all_to_all(near, 'region', split_axis=0, concat_axis=0, tiled=True, a...  4.49 us
  transfers between devices with their start and end apart: 9, of which 5 were waited for; matrix products, arithmetic and copies ran while one was open for 1% of the time, Pallas kernels for 0%

profile of v6, /device:TPU:17, one launch (start us, length us, event | category | flops | bytes accessed | tf_op | source)
XLA Modules:
  0.0 74.5 jit_solution(2430759741996426)
XLA Ops:
  0.0 0.0 copy-start
  0.0 9.2 %level_zero.1 = (bf16[256,2048]{1,0:T(8,128)(2,1)}, bf16[32,2048]{1,0:T(8,128)(2,1)}, bf16[32,2048]{1,0:T(8,128)(2,1)}, bf16[32,2048]{1,0:T(8,128)(2,1)}, bf16[3...) custom-call(bf16[2048,1024]{1,0:T(8,128)(2,1)} %dosage_hbm.1, ...), custom_call_target="tpu_custom_call" | custom-call | tf_op jit(solution)/shard_map/level_zero/pallas_call | solution.py:183
  9.2 4.5 %all-to-all-start = ((bf16[8,32,2048]{2,1,0:T(8,128)(2,1)}), bf16[8,32,2048]{2,1,0:T(8,128)(2,1)S(1)}, u32[]{:S(2)}, u32[]{:S(2)}) async-start(bf16[8,32,2048]{2,1,0:T(8,128)(2,1)} %bitcast.6), calls=%async_computation | async-start | bytes 2097152 | tf_op jit(solution)/shard_map/all_to_all | solution.py:508
  13.7 0.1 collective-permute-start
  13.7 2.5 %collective-permute-start.1 = (bf16[32,2048]{1,0:T(8,128)(2,1)}, bf16[32,2048]{1,0:T(8,128)(2,1)S(1)}, u32[]{:S(2)}, u32[]{:S(2)}) collective-permute-start(bf16[32,2048]{1,0:T(8,128)(2,1)} %get-tuple-element.16), channel_id=1, source_target_pairs={{0,9},{1,8},{2,11},{3,10},{4,13},{5,12},{6,15},{7,14},{8,1},{9,0},... | collective-permute-start | bytes 393224 | tf_op jit(solution)/shard_map/ppermute | solution.py:512
  16.2 1.5 %collective-permute-start.2 = (bf16[32,2048]{1,0:T(8,128)(2,1)}, bf16[32,2048]{1,0:T(8,128)(2,1)S(1)}, u32[]{:S(2)}, u32[]{:S(2)}) collective-permute-start(bf16[32,2048]{1,0:T(8,128)(2,1)} %get-tuple-element.17), channel_id=1, source_target_pairs={{0,10},{1,11},{2,8},{3,9},{4,14},{5,15},{6,12},{7,13},{8,2},{9,3},... | collective-permute-start | bytes 393224 | tf_op jit(solution)/shard_map/ppermute | solution.py:512
  17.7 2.1 %collective-permute-start.3 = (bf16[32,2048]{1,0:T(8,128)(2,1)}, bf16[32,2048]{1,0:T(8,128)(2,1)S(1)}, u32[]{:S(2)}, u32[]{:S(2)}) collective-permute-start(bf16[32,2048]{1,0:T(8,128)(2,1)} %get-tuple-element.18), channel_id=1, source_target_pairs={{0,11},{1,10},{2,9},{3,8},{4,15},{5,14},{6,13},{7,12},{8,3},{9,2},... | collective-permute-start | bytes 393224 | tf_op jit(solution)/shard_map/ppermute | solution.py:512
  19.9 0.5 collective-permute-start.4
  20.3 0.0 copy-done
  20.3 0.2 constant_dynamic-slice_fusion
  20.5 0.2 copy.6
  20.7 8.4 %collective-permute-done.rest_0_ = bf16[32,2048]{1,0:T(8,128)(2,1)S(1)} collective-permute-done((bf16[32,2048]{1,0:T(8,128)(2,1)}, bf16[32,2048]{1,0:T(8,128)(2,1)S(1)}, u32[]{:S(2)}, u32[]{:S(2)}) %collective-permute-start) | collective-permute-done | bytes 131104 | tf_op jit(solution)/shard_map/ppermute | solution.py:512
  29.1 3.5 %collective-permute-start.5 = (bf16[32,2048]{1,0:T(8,128)(2,1)}, bf16[32,2048]{1,0:T(8,128)(2,1)S(1)}, u32[]{:S(2)}, u32[]{:S(2)}) collective-permute-start(bf16[32,2048]{1,0:T(8,128)(2,1)} %get-tuple-element.20), channel_id=1, source_target_pairs={{0,13},{1,12},{2,15},{3,14},{4,9},{5,8},{6,11},{7,10},{8,5},{9,4},... | collective-permute-start | bytes 393224 | tf_op jit(solution)/shard_map/ppermute | solution.py:512
  32.6 0.0 collective-permute-done.1.rest_1_
  32.6 3.1 %collective-permute-start.6 = (bf16[32,2048]{1,0:T(8,128)(2,1)}, bf16[32,2048]{1,0:T(8,128)(2,1)S(1)}, u32[]{:S(2)}, u32[]{:S(2)}) collective-permute-start(bf16[32,2048]{1,0:T(8,128)(2,1)} %get-tuple-element.21), channel_id=1, source_target_pairs={{0,14},{1,15},{2,12},{3,13},{4,10},{5,11},{6,8},{7,9},{8,6},{9,7},... | collective-permute-start | bytes 393224 | tf_op jit(solution)/shard_map/ppermute | solution.py:512
  35.7 0.0 collective-permute-done.2.rest_2_
  35.7 3.4 %collective-permute-start.7 = (bf16[32,2048]{1,0:T(8,128)(2,1)}, bf16[32,2048]{1,0:T(8,128)(2,1)S(1)}, u32[]{:S(2)}, u32[]{:S(2)}) collective-permute-start(bf16[32,2048]{1,0:T(8,128)(2,1)} %get-tuple-element.22), channel_id=1, source_target_pairs={{0,15},{1,14},{2,13},{3,12},{4,11},{5,10},{6,9},{7,8},{8,7},{9,6},... | collective-permute-start | bytes 393224 | tf_op jit(solution)/shard_map/ppermute | solution.py:512
  39.1 0.0 collective-permute-done.3.rest_3_
  39.1 12.9 %collective-permute-done.4.rest_4_ = bf16[32,2048]{1,0:T(8,128)(2,1)S(1)} collective-permute-done((bf16[32,2048]{1,0:T(8,128)(2,1)}, bf16[32,2048]{1,0:T(8,128)(2,1)S(1)}, u32[]{:S(2)}, u32[]{:S(2)}) %collective-permute-start.4) | collective-permute-done | bytes 131104 | tf_op jit(solution)/shard_map/ppermute | solution.py:512
  52.1 5.5 %collective-permute-done.5.rest_5_ = bf16[32,2048]{1,0:T(8,128)(2,1)S(1)} collective-permute-done((bf16[32,2048]{1,0:T(8,128)(2,1)}, bf16[32,2048]{1,0:T(8,128)(2,1)S(1)}, u32[]{:S(2)}, u32[]{:S(2)}) %collective-permute-start.5) | collective-permute-done | bytes 131104 | tf_op jit(solution)/shard_map/ppermute | solution.py:512
  57.6 2.4 %collective-permute-done.6.rest_6_ = bf16[32,2048]{1,0:T(8,128)(2,1)S(1)} collective-permute-done((bf16[32,2048]{1,0:T(8,128)(2,1)}, bf16[32,2048]{1,0:T(8,128)(2,1)S(1)}, u32[]{:S(2)}, u32[]{:S(2)}) %collective-permute-start.6) | collective-permute-done | bytes 131104 | tf_op jit(solution)/shard_map/ppermute | solution.py:512
  60.0 3.3 %collective-permute-done.7.rest_7_ = bf16[32,2048]{1,0:T(8,128)(2,1)S(1)} collective-permute-done((bf16[32,2048]{1,0:T(8,128)(2,1)}, bf16[32,2048]{1,0:T(8,128)(2,1)S(1)}, u32[]{:S(2)}, u32[]{:S(2)}) %collective-permute-start.7) | collective-permute-done | bytes 131104 | tf_op jit(solution)/shard_map/ppermute | solution.py:512
  63.3 0.0 all-to-all-done
  63.3 11.2 %newton.1 = f32[8,64]{1,0:T(8,128)} custom-call(s32[1]{0:T(128)} %bitcast.place, bf16[256,2048]{1,0:T(8,128)(2,1)S(1)} %bitcast.5, bf16[32,2048]{1,0:T(8,128)(2,1)S(1)} %collective-permute-done.rest_0_, bf16[32,2048]{1,0:T(8,128)(2,1)S(1)} %collective-permute-done.1.rest_1_, bf16[32,2048]{1,0:T(8,128)(2,1)S(1)} %collective-permute-done.2.rest_2_, ...), custom_call_target="tpu_custom_call" | custom-call | tf_op jit(solution)/shard_map/newton/pallas_call | solution.py:448
  (1 shorter events, 0.0 us)
Async XLA Ops:
  0.0 20.3 %copy-start = (bf16[2048,128]{1,0:T(8,128)(2,1)S(1)}, bf16[2048,128]{1,0:T(8,128)(2,1)}, u32[]{:S(2)}) copy-start(bf16[2048,128]{1,0:T(8,128)(2,1)} %pheno_hbm.1) | copy-start | bytes 1572868
  9.2 54.1 %all-to-all-start = ((bf16[8,32,2048]{2,1,0:T(8,128)(2,1)}), bf16[8,32,2048]{2,1,0:T(8,128)(2,1)S(1)}, u32[]{:S(2)}, u32[]{:S(2)}) async-start(bf16[8,32,2048]{2,1,0:T(8,128)(2,1)} %bitcast.6), calls=%async_computation | async-start | bytes 2097152 | tf_op jit(solution)/shard_map/all_to_all | solution.py:508
  13.7 15.5 %collective-permute-start = (bf16[32,2048]{1,0:T(8,128)(2,1)}, bf16[32,2048]{1,0:T(8,128)(2,1)S(1)}, u32[]{:S(2)}, u32[]{:S(2)}) collective-permute-start(bf16[32,2048]{1,0:T(8,128)(2,1)} %get-tuple-element.15), channel_id=1, source_target_pairs={{0,8},{1,9},{2,10},{3,11},{4,12},{5,13},{6,14},{7,15},{8,0},{9,1},... | collective-permute-start | bytes 393224 | tf_op jit(solution)/shard_map/ppermute | solution.py:512
  13.7 18.9 %collective-permute-start.1 = (bf16[32,2048]{1,0:T(8,128)(2,1)}, bf16[32,2048]{1,0:T(8,128)(2,1)S(1)}, u32[]{:S(2)}, u32[]{:S(2)}) collective-permute-start(bf16[32,2048]{1,0:T(8,128)(2,1)} %get-tuple-element.16), channel_id=1, source_target_pairs={{0,9},{1,8},{2,11},{3,10},{4,13},{5,12},{6,15},{7,14},{8,1},{9,0},... | collective-permute-start | bytes 393224 | tf_op jit(solution)/shard_map/ppermute | solution.py:512
  16.2 19.5 %collective-permute-start.2 = (bf16[32,2048]{1,0:T(8,128)(2,1)}, bf16[32,2048]{1,0:T(8,128)(2,1)S(1)}, u32[]{:S(2)}, u32[]{:S(2)}) collective-permute-start(bf16[32,2048]{1,0:T(8,128)(2,1)} %get-tuple-element.17), channel_id=1, source_target_pairs={{0,10},{1,11},{2,8},{3,9},{4,14},{5,15},{6,12},{7,13},{8,2},{9,3},... | collective-permute-start | bytes 393224 | tf_op jit(solution)/shard_map/ppermute | solution.py:512
  17.7 21.4 %collective-permute-start.3 = (bf16[32,2048]{1,0:T(8,128)(2,1)}, bf16[32,2048]{1,0:T(8,128)(2,1)S(1)}, u32[]{:S(2)}, u32[]{:S(2)}) collective-permute-start(bf16[32,2048]{1,0:T(8,128)(2,1)} %get-tuple-element.18), channel_id=1, source_target_pairs={{0,11},{1,10},{2,9},{3,8},{4,15},{5,14},{6,13},{7,12},{8,3},{9,2},... | collective-permute-start | bytes 393224 | tf_op jit(solution)/shard_map/ppermute | solution.py:512
  19.9 32.2 %collective-permute-start.4 = (bf16[32,2048]{1,0:T(8,128)(2,1)}, bf16[32,2048]{1,0:T(8,128)(2,1)S(1)}, u32[]{:S(2)}, u32[]{:S(2)}) collective-permute-start(bf16[32,2048]{1,0:T(8,128)(2,1)} %get-tuple-element.19), channel_id=1, source_target_pairs={{0,12},{1,13},{2,14},{3,15},{4,8},{5,9},{6,10},{7,11},{8,4},{9,5},... | collective-permute-start | bytes 393224 | tf_op jit(solution)/shard_map/ppermute | solution.py:512
  29.1 28.4 %collective-permute-start.5 = (bf16[32,2048]{1,0:T(8,128)(2,1)}, bf16[32,2048]{1,0:T(8,128)(2,1)S(1)}, u32[]{:S(2)}, u32[]{:S(2)}) collective-permute-start(bf16[32,2048]{1,0:T(8,128)(2,1)} %get-tuple-element.20), channel_id=1, source_target_pairs={{0,13},{1,12},{2,15},{3,14},{4,9},{5,8},{6,11},{7,10},{8,5},{9,4},... | collective-permute-start | bytes 393224 | tf_op jit(solution)/shard_map/ppermute | solution.py:512
  32.6 27.4 %collective-permute-start.6 = (bf16[32,2048]{1,0:T(8,128)(2,1)}, bf16[32,2048]{1,0:T(8,128)(2,1)S(1)}, u32[]{:S(2)}, u32[]{:S(2)}) collective-permute-start(bf16[32,2048]{1,0:T(8,128)(2,1)} %get-tuple-element.21), channel_id=1, source_target_pairs={{0,14},{1,15},{2,12},{3,13},{4,10},{5,11},{6,8},{7,9},{8,6},{9,7},... | collective-permute-start | bytes 393224 | tf_op jit(solution)/shard_map/ppermute | solution.py:512
  35.7 27.6 %collective-permute-start.7 = (bf16[32,2048]{1,0:T(8,128)(2,1)}, bf16[32,2048]{1,0:T(8,128)(2,1)S(1)}, u32[]{:S(2)}, u32[]{:S(2)}) collective-permute-start(bf16[32,2048]{1,0:T(8,128)(2,1)} %get-tuple-element.22), channel_id=1, source_target_pairs={{0,15},{1,14},{2,13},{3,12},{4,11},{5,10},{6,9},{7,8},{8,7},{9,6},... | collective-permute-start | bytes 393224 | tf_op jit(solution)/shard_map/ppermute | solution.py:512

commit v7 on v6

--- a/solution.py
+++ b/solution.py
@@ -16,7 +16,7 @@
 SUBLANES = 8
 TILE = 256
 WIDE = 512
-HALF = 8
+ORDER = (12, 5, 10, 3, 13, 6, 11, 2, 14, 7, 8, 15, 4, 9, 1)
 
 
 def level_zero_kernel(
@@ -157,12 +157,9 @@
         predicted[:, n * WIDE : (n + 1) * WIDE] = (found - offset).astype(jnp.bfloat16)
         for i, out in enumerate(outs_hbm):
             height = out.shape[0]
-            if len(outs_hbm) == 1:
-                first = 0
-            elif i == 0:
-                first = pl.multiple_of((place[0] // HALF) * height, height)
-            else:
-                first = pl.multiple_of((place[0] ^ (HALF + i - 1)) * height, height)
+            first = 0
+            if len(outs_hbm) > 1:
+                first = pl.multiple_of((place[0] ^ i) * height, height)
             copy = pltpu.make_async_copy(
                 predicted.at[pl.ds(first, height), pl.ds(n * WIDE, WIDE)],
                 out.at[:, pl.ds(n * WIDE, WIDE)],
@@ -335,16 +332,19 @@
     return tiles
 
 
-def newton_kernel(traits, blocks, place, near, *rest):
-    *far, target, out, design, lhs, table_ref = rest
-    samples = near.shape[1]
+def newton_kernel(traits, blocks, place, *rest):
+    *given, target, out, design, lhs, table_ref = rest
+    arrays = [given[0]] + [given[1 + ORDER.index(j)] for j in range(1, blocks)]
+    samples = target.shape[1]
     predictors = RIDGES * blocks
     half = traits // 2
     parts = 2
     order = reorder_matrix(traits, blocks, parts)
     group = blocks // parts
     for part in range(parts):
-        arrived = near[...] if part == 0 else jnp.concatenate([block[...] for block in far], axis=0)
+        arrived = jnp.concatenate(
+            [block[...] for block in arrays[part * group : (part + 1) * group]], axis=0
+        )
         moved = jnp.dot(order, arrived, preferred_element_type=jnp.float32)
         for i in range(arrived.shape[0] // group):
             start = i * blocks + part * group
@@ -434,21 +434,19 @@
         result = jnp.where(sub == s, tile, result)
         result = jnp.where(sub == s + half, pltpu.roll(tile, predictors, 1), result)
     block = lane % blocks
-    own = block // HALF == place[0] // HALF
-    source = jnp.where(own, block % HALF, HALF + (block ^ place[0]) % HALF)
-    result = gather_lanes(result, (lane - block) + source)
+    result = gather_lanes(result, (lane - block) + (block ^ place[0]))
     out[...] = result[:, :predictors]
 
 
-def newton(place, near, far, target, blocks):
-    samples = near.shape[1]
+def newton(place, arrays, target, blocks):
+    samples = target.shape[1]
     traits = target.shape[0]
     predictors = RIDGES * blocks
     inside = pl.BlockSpec(memory_space=pltpu.VMEM)
     return pl.pallas_call(
         functools.partial(newton_kernel, traits, blocks),
         out_shape=jax.ShapeDtypeStruct((traits, predictors), jnp.float32),
-        in_specs=[pl.BlockSpec(memory_space=pltpu.SMEM)] + [inside] * (len(far) + 2),
+        in_specs=[pl.BlockSpec(memory_space=pltpu.SMEM)] + [inside] * (len(arrays) + 1),
         out_specs=inside,
         scratch_shapes=[
             pltpu.VMEM((traits * predictors, samples), jnp.bfloat16),
@@ -457,7 +455,7 @@
         ],
         compiler_params=pltpu.CompilerParams(vmem_limit_bytes=48 << 20),
         name="newton",
-    )(place, near, *far, target)
+    )(place, *arrays, target)
 
 
 def fit_traits(arrived, target):
@@ -500,19 +498,13 @@
     place = position.astype(jnp.int32).reshape(1)
     target = lax.dynamic_slice_in_dim(pheno, position * per_device, per_device, 1)
     target = target.astype(jnp.float32).T
-    if per_device == SUBLANES and regions == 2 * HALF:
-        near, *far = level_zero(
-            dosage, eigvec, eigval, pheno, place, [HALF * rows] + [rows] * HALF
-        )
-        halves = [list(range(HALF)), list(range(HALF, 2 * HALF))]
-        near = lax.all_to_all(
-            near, "region", split_axis=0, concat_axis=0, tiled=True, axis_index_groups=halves
-        )
-        far = [
-            lax.ppermute(block, "region", [(i, i ^ (HALF + j)) for i in range(regions)])
-            for j, block in enumerate(far)
+    if per_device == SUBLANES and regions == len(ORDER) + 1:
+        own, *arrays = level_zero(dosage, eigvec, eigval, pheno, place, [rows] * regions)
+        arrays = [
+            lax.ppermute(arrays[j - 1], "region", [(i, i ^ j) for i in range(regions)])
+            for j in ORDER
         ]
-        return newton(place, near, far, target, regions)
+        return newton(place, [own] + arrays, target, regions)
     (predicted,) = level_zero(dosage, eigvec, eigval, pheno, place, [RIDGES * traits])
     predicted = predicted.reshape(-1, RIDGES, SUBLANES // per_device, per_device, samples)
     predicted = predicted.swapaxes(1, 2).reshape(RIDGES * traits, samples)

time: 74.7 us -> 71.3 us (0.954)
  the two profiles are of different devices: /device:TPU:17 before, /device:TPU:1 now
where the time goes in v7:
time: 71.3 us; the launch traced here: 71.1 us
  starting transfers between devices  30.9 us (43%)
  Pallas kernels  20.6 us (29%)
  waiting for transfers between devices  18.2 us (26%)
  local copies, waits for them, and re-layouts  1.29 us (2%)
    ppermute x15, starting transfers between devices, on_device(): lax.ppermute(arrays[j - 1], 'region', [(i, i ^ j) for i in range(regions)])  30.9 us
    ppermute x15, waiting for transfers between devices, on_device(): lax.ppermute(arrays[j - 1], 'region', [(i, i ^ j) for i in range(regions)])  18.2 us
    pallas_call x1, Pallas kernels, newton(): pl.pallas_call(functools.partial(newton_kernel, traits, blocks), out_shap...  11.2 us
    pallas_call x1, Pallas kernels, level_zero(): pl.pallas_call(level_zero_kernel, out_shape=[jax.ShapeDtypeStruct((height...  9.44 us
  transfers between devices with their start and end apart: 15, of which 5 were waited for; matrix products, arithmetic and copies ran while one was open for 1% of the time, Pallas kernels for 0%

profile of v7, /device:TPU:1, one launch (start us, length us, event | category | flops | bytes accessed | tf_op | source)
XLA Modules:
  0.0 71.1 jit_solution(10927545595868978482)
XLA Ops:
  0.0 0.0 copy-start.1
  0.0 9.4 %level_zero.1 = (bf16[32,2048]{1,0:T(8,128)(2,1)}, bf16[32,2048]{1,0:T(8,128)(2,1)}, bf16[32,2048]{1,0:T(8,128)(2,1)}, bf16[32,2048]{1,0:T(8,128)(2,1)}, bf16[32...) custom-call(bf16[2048,1024]{1,0:T(8,128)(2,1)} %dosage_hbm.1, ...), custom_call_target="tpu_custom_call" | custom-call | tf_op jit(solution)/shard_map/level_zero/pallas_call | solution.py:180
  9.5 4.2 %collective-permute-start = (bf16[32,2048]{1,0:T(8,128)(2,1)}, bf16[32,2048]{1,0:T(8,128)(2,1)S(1)}, u32[]{:S(2)}, u32[]{:S(2)}) collective-permute-start(bf16[32,2048]{1,0:T(8,128)(2,1)} %get-tuple-element.22), channel_id=1, source_target_pairs={{0,12},{1,13},{2,14},{3,15},{4,8},{5,9},{6,10},{7,11},{8,4},{9,5},... | collective-permute-start | bytes 393224 | tf_op jit(solution)/shard_map/ppermute | solution.py:504
  13.7 0.1 collective-permute-start.1
  13.8 1.9 %collective-permute-start.2 = (bf16[32,2048]{1,0:T(8,128)(2,1)}, bf16[32,2048]{1,0:T(8,128)(2,1)S(1)}, u32[]{:S(2)}, u32[]{:S(2)}) collective-permute-start(bf16[32,2048]{1,0:T(8,128)(2,1)} %get-tuple-element.24), channel_id=1, source_target_pairs={{0,10},{1,11},{2,8},{3,9},{4,14},{5,15},{6,12},{7,13},{8,2},{9,3},... | collective-permute-start | bytes 393224 | tf_op jit(solution)/shard_map/ppermute | solution.py:504
  15.7 0.1 collective-permute-start.3
  15.8 3.7 %collective-permute-start.4 = (bf16[32,2048]{1,0:T(8,128)(2,1)}, bf16[32,2048]{1,0:T(8,128)(2,1)S(1)}, u32[]{:S(2)}, u32[]{:S(2)}) collective-permute-start(bf16[32,2048]{1,0:T(8,128)(2,1)} %get-tuple-element.26), channel_id=1, source_target_pairs={{0,13},{1,12},{2,15},{3,14},{4,9},{5,8},{6,11},{7,10},{8,5},{9,4},... | collective-permute-start | bytes 393224 | tf_op jit(solution)/shard_map/ppermute | solution.py:504
  19.5 0.0 collective-permute-done.rest_1_
  19.5 0.5 collective-permute-start.5
  20.1 1.7 %collective-permute-done.1.rest_2_ = bf16[32,2048]{1,0:T(8,128)(2,1)S(1)} collective-permute-done((bf16[32,2048]{1,0:T(8,128)(2,1)}, bf16[32,2048]{1,0:T(8,128)(2,1)S(1)}, u32[]{:S(2)}, u32[]{:S(2)}) %collective-permute-start.1) | collective-permute-done | bytes 131104 | tf_op jit(solution)/shard_map/ppermute | solution.py:504
  21.8 2.3 %collective-permute-start.6 = (bf16[32,2048]{1,0:T(8,128)(2,1)}, bf16[32,2048]{1,0:T(8,128)(2,1)S(1)}, u32[]{:S(2)}, u32[]{:S(2)}) collective-permute-start(bf16[32,2048]{1,0:T(8,128)(2,1)} %get-tuple-element.28), channel_id=1, source_target_pairs={{0,11},{1,10},{2,9},{3,8},{4,15},{5,14},{6,13},{7,12},{8,3},{9,2},... | collective-permute-start | bytes 393224 | tf_op jit(solution)/shard_map/ppermute | solution.py:504
  24.1 4.2 %collective-permute-done.2.rest_3_ = bf16[32,2048]{1,0:T(8,128)(2,1)S(1)} collective-permute-done((bf16[32,2048]{1,0:T(8,128)(2,1)}, bf16[32,2048]{1,0:T(8,128)(2,1)S(1)}, u32[]{:S(2)}, u32[]{:S(2)}) %collective-permute-start.2) | collective-permute-done | bytes 131104 | tf_op jit(solution)/shard_map/ppermute | solution.py:504
  28.2 0.3 collective-permute-start.7
  28.6 0.0 collective-permute-done.3.rest_4_
  28.6 2.3 %collective-permute-start.8 = (bf16[32,2048]{1,0:T(8,128)(2,1)}, bf16[32,2048]{1,0:T(8,128)(2,1)S(1)}, u32[]{:S(2)}, u32[]{:S(2)}) collective-permute-start(bf16[32,2048]{1,0:T(8,128)(2,1)} %get-tuple-element.30), channel_id=1, source_target_pairs={{0,14},{1,15},{2,12},{3,13},{4,10},{5,11},{6,8},{7,9},{8,6},{9,7},... | collective-permute-start | bytes 393224 | tf_op jit(solution)/shard_map/ppermute | solution.py:504
  30.9 0.0 collective-permute-done.4.rest_5_
  30.9 6.1 %collective-permute-start.9 = (bf16[32,2048]{1,0:T(8,128)(2,1)}, bf16[32,2048]{1,0:T(8,128)(2,1)S(1)}, u32[]{:S(2)}, u32[]{:S(2)}) collective-permute-start(bf16[32,2048]{1,0:T(8,128)(2,1)} %get-tuple-element.31), channel_id=1, source_target_pairs={{0,7},{1,6},{2,5},{3,4},{4,3},{5,2},{6,1},{7,0},{8,15},{9,14},{10,... | collective-permute-start | bytes 393224 | tf_op jit(solution)/shard_map/ppermute | solution.py:504
  37.0 0.0 copy-done.1
  37.0 0.2 constant_dynamic-slice_fusion
  37.2 0.2 copy.6
  37.4 0.0 collective-permute-done.5.rest_6_
  37.4 0.2 collective-permute-start.10
  37.5 4.0 %collective-permute-done.6.rest_7_ = bf16[32,2048]{1,0:T(8,128)(2,1)S(1)} collective-permute-done((bf16[32,2048]{1,0:T(8,128)(2,1)}, bf16[32,2048]{1,0:T(8,128)(2,1)S(1)}, u32[]{:S(2)}, u32[]{:S(2)}) %collective-permute-start.6) | collective-permute-done | bytes 131104 | tf_op jit(solution)/shard_map/ppermute | solution.py:504
  41.5 0.8 %collective-permute-start.11 = (bf16[32,2048]{1,0:T(8,128)(2,1)}, bf16[32,2048]{1,0:T(8,128)(2,1)S(1)}, u32[]{:S(2)}, u32[]{:S(2)}) collective-permute-start(bf16[32,2048]{1,0:T(8,128)(2,1)} %get-tuple-element.33), channel_id=1, source_target_pairs={{0,15},{1,14},{2,13},{3,12},{4,11},{5,10},{6,9},{7,8},{8,7},{9,6},... | collective-permute-start | bytes 393224 | tf_op jit(solution)/shard_map/ppermute | solution.py:504
  42.3 0.0 collective-permute-done.7.rest_8_
  42.3 0.0 collective-permute-start.12
  42.3 0.0 collective-permute-done.8.rest_9_
  42.4 8.3 %collective-permute-start.13 = (bf16[32,2048]{1,0:T(8,128)(2,1)}, bf16[32,2048]{1,0:T(8,128)(2,1)S(1)}, u32[]{:S(2)}, u32[]{:S(2)}) collective-permute-start(bf16[32,2048]{1,0:T(8,128)(2,1)} %get-tuple-element.35), channel_id=1, source_target_pairs={{0,9},{1,8},{2,11},{3,10},{4,13},{5,12},{6,15},{7,14},{8,1},{9,0},... | collective-permute-start | bytes 393224 | tf_op jit(solution)/shard_map/ppermute | solution.py:504
  50.6 0.0 collective-permute-done.9.rest_10_
  50.6 0.0 collective-permute-start.14
  50.6 0.0 collective-permute-done.10.rest_11_
  50.6 0.0 collective-permute-done.11.rest_12_
  50.6 1.4 %collective-permute-done.12.rest_13_ = bf16[32,2048]{1,0:T(8,128)(2,1)S(1)} collective-permute-done((bf16[32,2048]{1,0:T(8,128)(2,1)}, bf16[32,2048]{1,0:T(8,128)(2,1)S(1)}, u32[]{:S(2)}, u32[]{:S(2)}) %collective-permute-start.12) | collective-permute-done | bytes 131104 | tf_op jit(solution)/shard_map/ppermute | solution.py:504
  52.1 6.9 %collective-permute-done.13.rest_14_ = bf16[32,2048]{1,0:T(8,128)(2,1)S(1)} collective-permute-done((bf16[32,2048]{1,0:T(8,128)(2,1)}, bf16[32,2048]{1,0:T(8,128)(2,1)S(1)}, u32[]{:S(2)}, u32[]{:S(2)}) %collective-permute-start.13) | collective-permute-done | bytes 131104 | tf_op jit(solution)/shard_map/ppermute | solution.py:504
  59.0 0.0 collective-permute-done.14.rest_15_
  59.0 0.0 copy-start
  59.0 0.9 %copy-done = bf16[32,2048]{1,0:T(8,128)(2,1)S(1)} copy-done((bf16[32,2048]{1,0:T(8,128)(2,1)S(1)}, bf16[32,2048]{1,0:T(8,128)(2,1)}, u32[]{:S(2)}) %copy-start) | copy-done | bytes 131096
  59.9 11.2 %newton.1 = f32[8,64]{1,0:T(8,128)} custom-call(s32[1]{0:T(128)} %bitcast.place, bf16[32,2048]{1,0:T(8,128)(2,1)S(1)} %copy-done, bf16[32,2048]{1,0:T(8,128)(2,1)S(1)} %collective-permute-done.rest_1_, bf16[32,2048]{1,0:T(8,128)(2,1)S(1)} %collective-permute-done.1.rest_2_, bf16[32,2048]{1,0:T(8,128)(2,1)S(1)} %collective-permute-done.2.rest_3_, ...), custom_call_target="tpu_custom_call" | custom-call | tf_op jit(solution)/shard_map/newton/pallas_call | solution.py:446
  (1 shorter events, 0.0 us)
Async XLA Ops:
  0.0 37.0 %copy-start.1 = (bf16[2048,128]{1,0:T(8,128)(2,1)S(1)}, bf16[2048,128]{1,0:T(8,128)(2,1)}, u32[]{:S(2)}) copy-start(bf16[2048,128]{1,0:T(8,128)(2,1)} %pheno_hbm.1) | copy-start | bytes 1572868
  9.5 10.1 %collective-permute-start = (bf16[32,2048]{1,0:T(8,128)(2,1)}, bf16[32,2048]{1,0:T(8,128)(2,1)S(1)}, u32[]{:S(2)}, u32[]{:S(2)}) collective-permute-start(bf16[32,2048]{1,0:T(8,128)(2,1)} %get-tuple-element.22), channel_id=1, source_target_pairs={{0,12},{1,13},{2,14},{3,15},{4,8},{5,9},{6,10},{7,11},{8,4},{9,5},... | collective-permute-start | bytes 393224 | tf_op jit(solution)/shard_map/ppermute | solution.py:504
  13.7 8.1 %collective-permute-start.1 = (bf16[32,2048]{1,0:T(8,128)(2,1)}, bf16[32,2048]{1,0:T(8,128)(2,1)S(1)}, u32[]{:S(2)}, u32[]{:S(2)}) collective-permute-start(bf16[32,2048]{1,0:T(8,128)(2,1)} %get-tuple-element.23), channel_id=1, source_target_pairs={{0,5},{1,4},{2,7},{3,6},{4,1},{5,0},{6,3},{7,2},{8,13},{9,12},{10,... | collective-permute-start | bytes 393224 | tf_op jit(solution)/shard_map/ppermute | solution.py:504
  13.8 14.5 %collective-permute-start.2 = (bf16[32,2048]{1,0:T(8,128)(2,1)}, bf16[32,2048]{1,0:T(8,128)(2,1)S(1)}, u32[]{:S(2)}, u32[]{:S(2)}) collective-permute-start(bf16[32,2048]{1,0:T(8,128)(2,1)} %get-tuple-element.24), channel_id=1, source_target_pairs={{0,10},{1,11},{2,8},{3,9},{4,14},{5,15},{6,12},{7,13},{8,2},{9,3},... | collective-permute-start | bytes 393224 | tf_op jit(solution)/shard_map/ppermute | solution.py:504
  15.7 12.9 %collective-permute-start.3 = (bf16[32,2048]{1,0:T(8,128)(2,1)}, bf16[32,2048]{1,0:T(8,128)(2,1)S(1)}, u32[]{:S(2)}, u32[]{:S(2)}) collective-permute-start(bf16[32,2048]{1,0:T(8,128)(2,1)} %get-tuple-element.25), channel_id=1, source_target_pairs={{0,3},{1,2},{2,1},{3,0},{4,7},{5,6},{6,5},{7,4},{8,11},{9,10},{10,... | collective-permute-start | bytes 393224 | tf_op jit(solution)/shard_map/ppermute | solution.py:504
  15.8 15.1 %collective-permute-start.4 = (bf16[32,2048]{1,0:T(8,128)(2,1)}, bf16[32,2048]{1,0:T(8,128)(2,1)S(1)}, u32[]{:S(2)}, u32[]{:S(2)}) collective-permute-start(bf16[32,2048]{1,0:T(8,128)(2,1)} %get-tuple-element.26), channel_id=1, source_target_pairs={{0,13},{1,12},{2,15},{3,14},{4,9},{5,8},{6,11},{7,10},{8,5},{9,4},... | collective-permute-start | bytes 393224 | tf_op jit(solution)/shard_map/ppermute | solution.py:504
  19.5 17.8 %collective-permute-start.5 = (bf16[32,2048]{1,0:T(8,128)(2,1)}, bf16[32,2048]{1,0:T(8,128)(2,1)S(1)}, u32[]{:S(2)}, u32[]{:S(2)}) collective-permute-start(bf16[32,2048]{1,0:T(8,128)(2,1)} %get-tuple-element.27), channel_id=1, source_target_pairs={{0,6},{1,7},{2,4},{3,5},{4,2},{5,3},{6,0},{7,1},{8,14},{9,15},{10,... | collective-permute-start | bytes 393224 | tf_op jit(solution)/shard_map/ppermute | solution.py:504
  21.8 19.8 %collective-permute-start.6 = (bf16[32,2048]{1,0:T(8,128)(2,1)}, bf16[32,2048]{1,0:T(8,128)(2,1)S(1)}, u32[]{:S(2)}, u32[]{:S(2)}) collective-permute-start(bf16[32,2048]{1,0:T(8,128)(2,1)} %get-tuple-element.28), channel_id=1, source_target_pairs={{0,11},{1,10},{2,9},{3,8},{4,15},{5,14},{6,13},{7,12},{8,3},{9,2},... | collective-permute-start | bytes 393224 | tf_op jit(solution)/shard_map/ppermute | solution.py:504
  28.2 14.1 %collective-permute-start.7 = (bf16[32,2048]{1,0:T(8,128)(2,1)}, bf16[32,2048]{1,0:T(8,128)(2,1)S(1)}, u32[]{:S(2)}, u32[]{:S(2)}) collective-permute-start(bf16[32,2048]{1,0:T(8,128)(2,1)} %get-tuple-element.29), channel_id=1, source_target_pairs={{0,2},{1,3},{2,0},{3,1},{4,6},{5,7},{6,4},{7,5},{8,10},{9,11},{10,... | collective-permute-start | bytes 393224 | tf_op jit(solution)/shard_map/ppermute | solution.py:504
  28.6 13.8 %collective-permute-start.8 = (bf16[32,2048]{1,0:T(8,128)(2,1)}, bf16[32,2048]{1,0:T(8,128)(2,1)S(1)}, u32[]{:S(2)}, u32[]{:S(2)}) collective-permute-start(bf16[32,2048]{1,0:T(8,128)(2,1)} %get-tuple-element.30), channel_id=1, source_target_pairs={{0,14},{1,15},{2,12},{3,13},{4,10},{5,11},{6,8},{7,9},{8,6},{9,7},... | collective-permute-start | bytes 393224 | tf_op jit(solution)/shard_map/ppermute | solution.py:504
  30.9 19.7 %collective-permute-start.9 = (bf16[32,2048]{1,0:T(8,128)(2,1)}, bf16[32,2048]{1,0:T(8,128)(2,1)S(1)}, u32[]{:S(2)}, u32[]{:S(2)}) collective-permute-start(bf16[32,2048]{1,0:T(8,128)(2,1)} %get-tuple-element.31), channel_id=1, source_target_pairs={{0,7},{1,6},{2,5},{3,4},{4,3},{5,2},{6,1},{7,0},{8,15},{9,14},{10,... | collective-permute-start | bytes 393224 | tf_op jit(solution)/shard_map/ppermute | solution.py:504
  37.4 13.3 %collective-permute-start.10 = (bf16[32,2048]{1,0:T(8,128)(2,1)}, bf16[32,2048]{1,0:T(8,128)(2,1)S(1)}, u32[]{:S(2)}, u32[]{:S(2)}) collective-permute-start(bf16[32,2048]{1,0:T(8,128)(2,1)} %get-tuple-element.32), channel_id=1, source_target_pairs={{0,8},{1,9},{2,10},{3,11},{4,12},{5,13},{6,14},{7,15},{8,0},{9,1},... | collective-permute-start | bytes 393224 | tf_op jit(solution)/shard_map/ppermute | solution.py:504
  41.5 9.1 %collective-permute-start.11 = (bf16[32,2048]{1,0:T(8,128)(2,1)}, bf16[32,2048]{1,0:T(8,128)(2,1)S(1)}, u32[]{:S(2)}, u32[]{:S(2)}) collective-permute-start(bf16[32,2048]{1,0:T(8,128)(2,1)} %get-tuple-element.33), channel_id=1, source_target_pairs={{0,15},{1,14},{2,13},{3,12},{4,11},{5,10},{6,9},{7,8},{8,7},{9,6},... | collective-permute-start | bytes 393224 | tf_op jit(solution)/shard_map/ppermute | solution.py:504
  42.3 9.7 %collective-permute-start.12 = (bf16[32,2048]{1,0:T(8,128)(2,1)}, bf16[32,2048]{1,0:T(8,128)(2,1)S(1)}, u32[]{:S(2)}, u32[]{:S(2)}) collective-permute-start(bf16[32,2048]{1,0:T(8,128)(2,1)} %get-tuple-element.34), channel_id=1, source_target_pairs={{0,4},{1,5},{2,6},{3,7},{4,0},{5,1},{6,2},{7,3},{8,12},{9,13},{10,... | collective-permute-start | bytes 393224 | tf_op jit(solution)/shard_map/ppermute | solution.py:504
  42.4 16.6 %collective-permute-start.13 = (bf16[32,2048]{1,0:T(8,128)(2,1)}, bf16[32,2048]{1,0:T(8,128)(2,1)S(1)}, u32[]{:S(2)}, u32[]{:S(2)}) collective-permute-start(bf16[32,2048]{1,0:T(8,128)(2,1)} %get-tuple-element.35), channel_id=1, source_target_pairs={{0,9},{1,8},{2,11},{3,10},{4,13},{5,12},{6,15},{7,14},{8,1},{9,0},... | collective-permute-start | bytes 393224 | tf_op jit(solution)/shard_map/ppermute | solution.py:504
  50.6 8.4 %collective-permute-start.14 = (bf16[32,2048]{1,0:T(8,128)(2,1)}, bf16[32,2048]{1,0:T(8,128)(2,1)S(1)}, u32[]{:S(2)}, u32[]{:S(2)}) collective-permute-start(bf16[32,2048]{1,0:T(8,128)(2,1)} %get-tuple-element.36), channel_id=1, source_target_pairs={{0,1},{1,0},{2,3},{3,2},{4,5},{5,4},{6,7},{7,6},{8,9},{9,8},{10,11... | collective-permute-start | bytes 393224 | tf_op jit(solution)/shard_map/ppermute | solution.py:504
  59.0 0.9 %copy-start = (bf16[32,2048]{1,0:T(8,128)(2,1)S(1)}, bf16[32,2048]{1,0:T(8,128)(2,1)}, u32[]{:S(2)}) copy-start(bf16[32,2048]{1,0:T(8,128)(2,1)} %get-tuple-element.21.rest_0_) | copy-start | bytes 393220

commit v8 on v7

--- a/solution.py
+++ b/solution.py
@@ -458,6 +458,25 @@
     )(place, *arrays, target)
 
 
+def fetch_kernel(block, out):
+    out[...] = block[...]
+
+
+def fetch(block):
+    inside = pl.BlockSpec(memory_space=pltpu.VMEM)
+    return pl.pallas_call(
+        fetch_kernel,
+        out_shape=jax.ShapeDtypeStruct(block.shape, block.dtype),
+        in_specs=[inside],
+        out_specs=inside,
+        cost_estimate=pl.CostEstimate(
+            flops=0, bytes_accessed=4 * block.size, transcendentals=0
+        ),
+        compiler_params=pltpu.CompilerParams(vmem_limit_bytes=2 << 20),
+        name="fetch",
+    )(block)
+
+
 def fit_traits(arrived, target):
     rows, samples = arrived.shape
     count = target.shape[0]
@@ -504,7 +523,7 @@
             lax.ppermute(arrays[j - 1], "region", [(i, i ^ j) for i in range(regions)])
             for j in ORDER
         ]
-        return newton(place, [own] + arrays, target, regions)
+        return newton(place, [fetch(own)] + arrays, target, regions)
     (predicted,) = level_zero(dosage, eigvec, eigval, pheno, place, [RIDGES * traits])
     predicted = predicted.reshape(-1, RIDGES, SUBLANES // per_device, per_device, samples)
     predicted = predicted.swapaxes(1, 2).reshape(RIDGES * traits, samples)

time: 71.3 us -> 70.3 us (0.986)
  waiting for transfers between devices: 18.2 us -> 17.3 us
    ppermute x15, waiting for transfers between devices: 18.2 us -> 17.3 us  [on_device(): lax.ppermute(arrays[j - 1], 'region', [(i, i ^ j) for i in range(regions)])]
where the time goes in v8:
time: 70.3 us; the launch traced here: 70.2 us
  starting transfers between devices  30.9 us (44%)
  Pallas kernels  20.7 us (29%)
  waiting for transfers between devices  17.3 us (25%)
  local copies, waits for them, and re-layouts  1.28 us (2%)
    ppermute x15, starting transfers between devices, on_device(): lax.ppermute(arrays[j - 1], 'region', [(i, i ^ j) for i in range(regions)])  30.9 us
    ppermute x15, waiting for transfers between devices, on_device(): lax.ppermute(arrays[j - 1], 'region', [(i, i ^ j) for i in range(regions)])  17.3 us
    pallas_call x1, Pallas kernels, newton(): pl.pallas_call(functools.partial(newton_kernel, traits, blocks), out_shap...  11.2 us
    pallas_call x1, Pallas kernels, level_zero(): pl.pallas_call(level_zero_kernel, out_shape=[jax.ShapeDtypeStruct((height...  9.44 us
  transfers between devices with their start and end apart: 15, of which 5 were waited for; matrix products, arithmetic and copies ran while one was open for 1% of the time, Pallas kernels for 0%

profile of v8, /device:TPU:1, one launch (start us, length us, event | category | flops | bytes accessed | tf_op | source)
XLA Modules:
  0.0 70.2 jit_solution(9669163753867944480)
XLA Ops:
  0.0 0.0 copy-start.1
  0.0 9.4 %level_zero.1 = (bf16[32,2048]{1,0:T(8,128)(2,1)}, bf16[32,2048]{1,0:T(8,128)(2,1)}, bf16[32,2048]{1,0:T(8,128)(2,1)}, bf16[32,2048]{1,0:T(8,128)(2,1)}, bf16[32...) custom-call(bf16[2048,1024]{1,0:T(8,128)(2,1)} %dosage_hbm.1, ...), custom_call_target="tpu_custom_call" | custom-call | tf_op jit(solution)/shard_map/level_zero/pallas_call | solution.py:180
  9.5 4.2 %collective-permute-start = (bf16[32,2048]{1,0:T(8,128)(2,1)}, bf16[32,2048]{1,0:T(8,128)(2,1)S(1)}, u32[]{:S(2)}, u32[]{:S(2)}) collective-permute-start(bf16[32,2048]{1,0:T(8,128)(2,1)} %get-tuple-element.22), channel_id=1, source_target_pairs={{0,12},{1,13},{2,14},{3,15},{4,8},{5,9},{6,10},{7,11},{8,4},{9,5},... | collective-permute-start | bytes 393224 | tf_op jit(solution)/shard_map/ppermute | solution.py:523
  13.7 0.1 collective-permute-start.1
  13.8 1.9 %collective-permute-start.2 = (bf16[32,2048]{1,0:T(8,128)(2,1)}, bf16[32,2048]{1,0:T(8,128)(2,1)S(1)}, u32[]{:S(2)}, u32[]{:S(2)}) collective-permute-start(bf16[32,2048]{1,0:T(8,128)(2,1)} %get-tuple-element.24), channel_id=1, source_target_pairs={{0,10},{1,11},{2,8},{3,9},{4,14},{5,15},{6,12},{7,13},{8,2},{9,3},... | collective-permute-start | bytes 393224 | tf_op jit(solution)/shard_map/ppermute | solution.py:523
  15.7 0.1 collective-permute-start.3
  15.8 3.7 %collective-permute-start.4 = (bf16[32,2048]{1,0:T(8,128)(2,1)}, bf16[32,2048]{1,0:T(8,128)(2,1)S(1)}, u32[]{:S(2)}, u32[]{:S(2)}) collective-permute-start(bf16[32,2048]{1,0:T(8,128)(2,1)} %get-tuple-element.26), channel_id=1, source_target_pairs={{0,13},{1,12},{2,15},{3,14},{4,9},{5,8},{6,11},{7,10},{8,5},{9,4},... | collective-permute-start | bytes 393224 | tf_op jit(solution)/shard_map/ppermute | solution.py:523
  19.5 0.0 collective-permute-done.rest_1_
  19.5 0.5 collective-permute-start.5
  20.1 1.7 %collective-permute-done.1.rest_2_ = bf16[32,2048]{1,0:T(8,128)(2,1)S(1)} collective-permute-done((bf16[32,2048]{1,0:T(8,128)(2,1)}, bf16[32,2048]{1,0:T(8,128)(2,1)S(1)}, u32[]{:S(2)}, u32[]{:S(2)}) %collective-permute-start.1) | collective-permute-done | bytes 131104 | tf_op jit(solution)/shard_map/ppermute | solution.py:523
  21.8 2.3 %collective-permute-start.6 = (bf16[32,2048]{1,0:T(8,128)(2,1)}, bf16[32,2048]{1,0:T(8,128)(2,1)S(1)}, u32[]{:S(2)}, u32[]{:S(2)}) collective-permute-start(bf16[32,2048]{1,0:T(8,128)(2,1)} %get-tuple-element.28), channel_id=1, source_target_pairs={{0,11},{1,10},{2,9},{3,8},{4,15},{5,14},{6,13},{7,12},{8,3},{9,2},... | collective-permute-start | bytes 393224 | tf_op jit(solution)/shard_map/ppermute | solution.py:523
  24.1 4.2 %collective-permute-done.2.rest_3_ = bf16[32,2048]{1,0:T(8,128)(2,1)S(1)} collective-permute-done((bf16[32,2048]{1,0:T(8,128)(2,1)}, bf16[32,2048]{1,0:T(8,128)(2,1)S(1)}, u32[]{:S(2)}, u32[]{:S(2)}) %collective-permute-start.2) | collective-permute-done | bytes 131104 | tf_op jit(solution)/shard_map/ppermute | solution.py:523
  28.2 0.3 collective-permute-start.7
  28.6 0.0 collective-permute-done.3.rest_4_
  28.6 2.3 %collective-permute-start.8 = (bf16[32,2048]{1,0:T(8,128)(2,1)}, bf16[32,2048]{1,0:T(8,128)(2,1)S(1)}, u32[]{:S(2)}, u32[]{:S(2)}) collective-permute-start(bf16[32,2048]{1,0:T(8,128)(2,1)} %get-tuple-element.30), channel_id=1, source_target_pairs={{0,14},{1,15},{2,12},{3,13},{4,10},{5,11},{6,8},{7,9},{8,6},{9,7},... | collective-permute-start | bytes 393224 | tf_op jit(solution)/shard_map/ppermute | solution.py:523
  30.9 0.0 collective-permute-done.4.rest_5_
  30.9 6.1 %collective-permute-start.9 = (bf16[32,2048]{1,0:T(8,128)(2,1)}, bf16[32,2048]{1,0:T(8,128)(2,1)S(1)}, u32[]{:S(2)}, u32[]{:S(2)}) collective-permute-start(bf16[32,2048]{1,0:T(8,128)(2,1)} %get-tuple-element.31), channel_id=1, source_target_pairs={{0,7},{1,6},{2,5},{3,4},{4,3},{5,2},{6,1},{7,0},{8,15},{9,14},{10,... | collective-permute-start | bytes 393224 | tf_op jit(solution)/shard_map/ppermute | solution.py:523
  37.0 0.0 copy-done.1
  37.0 0.2 constant_dynamic-slice_fusion
  37.2 0.2 copy.6
  37.4 0.0 collective-permute-done.5.rest_6_
  37.4 0.2 collective-permute-start.10
  37.5 4.0 %collective-permute-done.6.rest_7_ = bf16[32,2048]{1,0:T(8,128)(2,1)S(1)} collective-permute-done((bf16[32,2048]{1,0:T(8,128)(2,1)}, bf16[32,2048]{1,0:T(8,128)(2,1)S(1)}, u32[]{:S(2)}, u32[]{:S(2)}) %collective-permute-start.6) | collective-permute-done | bytes 131104 | tf_op jit(solution)/shard_map/ppermute | solution.py:523
  41.5 0.8 %collective-permute-start.11 = (bf16[32,2048]{1,0:T(8,128)(2,1)}, bf16[32,2048]{1,0:T(8,128)(2,1)S(1)}, u32[]{:S(2)}, u32[]{:S(2)}) collective-permute-start(bf16[32,2048]{1,0:T(8,128)(2,1)} %get-tuple-element.33), channel_id=1, source_target_pairs={{0,15},{1,14},{2,13},{3,12},{4,11},{5,10},{6,9},{7,8},{8,7},{9,6},... | collective-permute-start | bytes 393224 | tf_op jit(solution)/shard_map/ppermute | solution.py:523
  42.3 0.0 collective-permute-done.7.rest_8_
  42.3 0.0 collective-permute-start.12
  42.3 0.0 collective-permute-done.8.rest_9_
  42.4 8.3 %collective-permute-start.13 = (bf16[32,2048]{1,0:T(8,128)(2,1)}, bf16[32,2048]{1,0:T(8,128)(2,1)S(1)}, u32[]{:S(2)}, u32[]{:S(2)}) collective-permute-start(bf16[32,2048]{1,0:T(8,128)(2,1)} %get-tuple-element.35), channel_id=1, source_target_pairs={{0,9},{1,8},{2,11},{3,10},{4,13},{5,12},{6,15},{7,14},{8,1},{9,0},... | collective-permute-start | bytes 393224 | tf_op jit(solution)/shard_map/ppermute | solution.py:523
  50.6 0.0 collective-permute-done.9.rest_10_
  50.6 0.0 collective-permute-start.14
  50.6 0.0 copy-start
  50.6 0.9 %copy-done = bf16[32,2048]{1,0:T(8,128)(2,1)S(1)} copy-done((bf16[32,2048]{1,0:T(8,128)(2,1)S(1)}, bf16[32,2048]{1,0:T(8,128)(2,1)}, u32[]{:S(2)}) %copy-start) | copy-done | bytes 131096
  51.5 0.0 collective-permute-done.10.rest_11_
  51.6 0.0 collective-permute-done.11.rest_12_
  51.6 0.5 collective-permute-done.12.rest_13_
  52.1 6.9 %collective-permute-done.13.rest_14_ = bf16[32,2048]{1,0:T(8,128)(2,1)S(1)} collective-permute-done((bf16[32,2048]{1,0:T(8,128)(2,1)}, bf16[32,2048]{1,0:T(8,128)(2,1)S(1)}, u32[]{:S(2)}, u32[]{:S(2)}) %collective-permute-start.13) | collective-permute-done | bytes 131104 | tf_op jit(solution)/shard_map/ppermute | solution.py:523
  59.0 0.0 collective-permute-done.14.rest_15_
  59.0 11.2 %newton.1 = f32[8,64]{1,0:T(8,128)} custom-call(s32[1]{0:T(128)} %bitcast.place, bf16[32,2048]{1,0:T(8,128)(2,1)S(1)} %fetch.1.rest_0_, bf16[32,2048]{1,0:T(8,128)(2,1)S(1)} %collective-permute-done.rest_1_, bf16[32,2048]{1,0:T(8,128)(2,1)S(1)} %collective-permute-done.1.rest_2_, bf16[32,2048]{1,0:T(8,128)(2,1)S(1)} %collective-permute-done.2.rest_3_, ...), custom_call_target="tpu_custom_call" | custom-call | tf_op jit(solution)/shard_map/newton/pallas_call | solution.py:446
  (2 shorter events, 0.0 us)
Async XLA Ops:
  0.0 37.0 %copy-start.1 = (bf16[2048,128]{1,0:T(8,128)(2,1)S(1)}, bf16[2048,128]{1,0:T(8,128)(2,1)}, u32[]{:S(2)}) copy-start(bf16[2048,128]{1,0:T(8,128)(2,1)} %pheno_hbm.1) | copy-start | bytes 1572868
  9.5 10.1 %collective-permute-start = (bf16[32,2048]{1,0:T(8,128)(2,1)}, bf16[32,2048]{1,0:T(8,128)(2,1)S(1)}, u32[]{:S(2)}, u32[]{:S(2)}) collective-permute-start(bf16[32,2048]{1,0:T(8,128)(2,1)} %get-tuple-element.22), channel_id=1, source_target_pairs={{0,12},{1,13},{2,14},{3,15},{4,8},{5,9},{6,10},{7,11},{8,4},{9,5},... | collective-permute-start | bytes 393224 | tf_op jit(solution)/shard_map/ppermute | solution.py:523
  13.7 8.1 %collective-permute-start.1 = (bf16[32,2048]{1,0:T(8,128)(2,1)}, bf16[32,2048]{1,0:T(8,128)(2,1)S(1)}, u32[]{:S(2)}, u32[]{:S(2)}) collective-permute-start(bf16[32,2048]{1,0:T(8,128)(2,1)} %get-tuple-element.23), channel_id=1, source_target_pairs={{0,5},{1,4},{2,7},{3,6},{4,1},{5,0},{6,3},{7,2},{8,13},{9,12},{10,... | collective-permute-start | bytes 393224 | tf_op jit(solution)/shard_map/ppermute | solution.py:523
  13.8 14.5 %collective-permute-start.2 = (bf16[32,2048]{1,0:T(8,128)(2,1)}, bf16[32,2048]{1,0:T(8,128)(2,1)S(1)}, u32[]{:S(2)}, u32[]{:S(2)}) collective-permute-start(bf16[32,2048]{1,0:T(8,128)(2,1)} %get-tuple-element.24), channel_id=1, source_target_pairs={{0,10},{1,11},{2,8},{3,9},{4,14},{5,15},{6,12},{7,13},{8,2},{9,3},... | collective-permute-start | bytes 393224 | tf_op jit(solution)/shard_map/ppermute | solution.py:523
  15.7 12.9 %collective-permute-start.3 = (bf16[32,2048]{1,0:T(8,128)(2,1)}, bf16[32,2048]{1,0:T(8,128)(2,1)S(1)}, u32[]{:S(2)}, u32[]{:S(2)}) collective-permute-start(bf16[32,2048]{1,0:T(8,128)(2,1)} %get-tuple-element.25), channel_id=1, source_target_pairs={{0,3},{1,2},{2,1},{3,0},{4,7},{5,6},{6,5},{7,4},{8,11},{9,10},{10,... | collective-permute-start | bytes 393224 | tf_op jit(solution)/shard_map/ppermute | solution.py:523
  15.8 15.1 %collective-permute-start.4 = (bf16[32,2048]{1,0:T(8,128)(2,1)}, bf16[32,2048]{1,0:T(8,128)(2,1)S(1)}, u32[]{:S(2)}, u32[]{:S(2)}) collective-permute-start(bf16[32,2048]{1,0:T(8,128)(2,1)} %get-tuple-element.26), channel_id=1, source_target_pairs={{0,13},{1,12},{2,15},{3,14},{4,9},{5,8},{6,11},{7,10},{8,5},{9,4},... | collective-permute-start | bytes 393224 | tf_op jit(solution)/shard_map/ppermute | solution.py:523
  19.5 17.8 %collective-permute-start.5 = (bf16[32,2048]{1,0:T(8,128)(2,1)}, bf16[32,2048]{1,0:T(8,128)(2,1)S(1)}, u32[]{:S(2)}, u32[]{:S(2)}) collective-permute-start(bf16[32,2048]{1,0:T(8,128)(2,1)} %get-tuple-element.27), channel_id=1, source_target_pairs={{0,6},{1,7},{2,4},{3,5},{4,2},{5,3},{6,0},{7,1},{8,14},{9,15},{10,... | collective-permute-start | bytes 393224 | tf_op jit(solution)/shard_map/ppermute | solution.py:523
  21.8 19.8 %collective-permute-start.6 = (bf16[32,2048]{1,0:T(8,128)(2,1)}, bf16[32,2048]{1,0:T(8,128)(2,1)S(1)}, u32[]{:S(2)}, u32[]{:S(2)}) collective-permute-start(bf16[32,2048]{1,0:T(8,128)(2,1)} %get-tuple-element.28), channel_id=1, source_target_pairs={{0,11},{1,10},{2,9},{3,8},{4,15},{5,14},{6,13},{7,12},{8,3},{9,2},... | collective-permute-start | bytes 393224 | tf_op jit(solution)/shard_map/ppermute | solution.py:523
  28.2 14.1 %collective-permute-start.7 = (bf16[32,2048]{1,0:T(8,128)(2,1)}, bf16[32,2048]{1,0:T(8,128)(2,1)S(1)}, u32[]{:S(2)}, u32[]{:S(2)}) collective-permute-start(bf16[32,2048]{1,0:T(8,128)(2,1)} %get-tuple-element.29), channel_id=1, source_target_pairs={{0,2},{1,3},{2,0},{3,1},{4,6},{5,7},{6,4},{7,5},{8,10},{9,11},{10,... | collective-permute-start | bytes 393224 | tf_op jit(solution)/shard_map/ppermute | solution.py:523
  28.6 13.8 %collective-permute-start.8 = (bf16[32,2048]{1,0:T(8,128)(2,1)}, bf16[32,2048]{1,0:T(8,128)(2,1)S(1)}, u32[]{:S(2)}, u32[]{:S(2)}) collective-permute-start(bf16[32,2048]{1,0:T(8,128)(2,1)} %get-tuple-element.30), channel_id=1, source_target_pairs={{0,14},{1,15},{2,12},{3,13},{4,10},{5,11},{6,8},{7,9},{8,6},{9,7},... | collective-permute-start | bytes 393224 | tf_op jit(solution)/shard_map/ppermute | solution.py:523
  30.9 19.7 %collective-permute-start.9 = (bf16[32,2048]{1,0:T(8,128)(2,1)}, bf16[32,2048]{1,0:T(8,128)(2,1)S(1)}, u32[]{:S(2)}, u32[]{:S(2)}) collective-permute-start(bf16[32,2048]{1,0:T(8,128)(2,1)} %get-tuple-element.31), channel_id=1, source_target_pairs={{0,7},{1,6},{2,5},{3,4},{4,3},{5,2},{6,1},{7,0},{8,15},{9,14},{10,... | collective-permute-start | bytes 393224 | tf_op jit(solution)/shard_map/ppermute | solution.py:523
  37.4 14.2 %collective-permute-start.10 = (bf16[32,2048]{1,0:T(8,128)(2,1)}, bf16[32,2048]{1,0:T(8,128)(2,1)S(1)}, u32[]{:S(2)}, u32[]{:S(2)}) collective-permute-start(bf16[32,2048]{1,0:T(8,128)(2,1)} %get-tuple-element.32), channel_id=1, source_target_pairs={{0,8},{1,9},{2,10},{3,11},{4,12},{5,13},{6,14},{7,15},{8,0},{9,1},... | collective-permute-start | bytes 393224 | tf_op jit(solution)/shard_map/ppermute | solution.py:523
  41.5 10.0 %collective-permute-start.11 = (bf16[32,2048]{1,0:T(8,128)(2,1)}, bf16[32,2048]{1,0:T(8,128)(2,1)S(1)}, u32[]{:S(2)}, u32[]{:S(2)}) collective-permute-start(bf16[32,2048]{1,0:T(8,128)(2,1)} %get-tuple-element.33), channel_id=1, source_target_pairs={{0,15},{1,14},{2,13},{3,12},{4,11},{5,10},{6,9},{7,8},{8,7},{9,6},... | collective-permute-start | bytes 393224 | tf_op jit(solution)/shard_map/ppermute | solution.py:523
  42.3 9.7 %collective-permute-start.12 = (bf16[32,2048]{1,0:T(8,128)(2,1)}, bf16[32,2048]{1,0:T(8,128)(2,1)S(1)}, u32[]{:S(2)}, u32[]{:S(2)}) collective-permute-start(bf16[32,2048]{1,0:T(8,128)(2,1)} %get-tuple-element.34), channel_id=1, source_target_pairs={{0,4},{1,5},{2,6},{3,7},{4,0},{5,1},{6,2},{7,3},{8,12},{9,13},{10,... | collective-permute-start | bytes 393224 | tf_op jit(solution)/shard_map/ppermute | solution.py:523
  42.4 16.6 %collective-permute-start.13 = (bf16[32,2048]{1,0:T(8,128)(2,1)}, bf16[32,2048]{1,0:T(8,128)(2,1)S(1)}, u32[]{:S(2)}, u32[]{:S(2)}) collective-permute-start(bf16[32,2048]{1,0:T(8,128)(2,1)} %get-tuple-element.35), channel_id=1, source_target_pairs={{0,9},{1,8},{2,11},{3,10},{4,13},{5,12},{6,15},{7,14},{8,1},{9,0},... | collective-permute-start | bytes 393224 | tf_op jit(solution)/shard_map/ppermute | solution.py:523
  50.6 8.4 %collective-permute-start.14 = (bf16[32,2048]{1,0:T(8,128)(2,1)}, bf16[32,2048]{1,0:T(8,128)(2,1)S(1)}, u32[]{:S(2)}, u32[]{:S(2)}) collective-permute-start(bf16[32,2048]{1,0:T(8,128)(2,1)} %get-tuple-element.36), channel_id=1, source_target_pairs={{0,1},{1,0},{2,3},{3,2},{4,5},{5,4},{6,7},{7,6},{8,9},{9,8},{10,11... | collective-permute-start | bytes 393224 | tf_op jit(solution)/shard_map/ppermute | solution.py:523
  50.6 0.9 %copy-start = (bf16[32,2048]{1,0:T(8,128)(2,1)S(1)}, bf16[32,2048]{1,0:T(8,128)(2,1)}, u32[]{:S(2)}) copy-start(bf16[32,2048]{1,0:T(8,128)(2,1)} %get-tuple-element.21.block) | copy-start | bytes 393220

commit v9 on v8

--- a/solution.py
+++ b/solution.py
@@ -333,7 +333,7 @@
 
 
 def newton_kernel(traits, blocks, place, *rest):
-    *given, target, out, design, lhs, table_ref = rest
+    *given, target, out, design, lhs = rest
     arrays = [given[0]] + [given[1 + ORDER.index(j)] for j in range(1, blocks)]
     samples = target.shape[1]
     predictors = RIDGES * blocks
@@ -403,6 +403,7 @@
             gradient = jnp.where(upper[:1], result[second : second + 1], result[first : first + 1])
             tiles.append(jnp.broadcast_to(gradient, (SUBLANES, LANES)))
             found.append(tiles)
+        table = [[] for _ in range(RIDGES)]
         for r in range(rows + 1):
             for h, tile in enumerate(exchange([found[s][r] for s in range(half)], blocks)):
                 if r < rows:
@@ -410,25 +411,19 @@
                     tile = tile + jnp.where(same, level_ridge, 0.0)
                 elif weights is not None:
                     tile = tile - level_ridge * weights[h]
-                table_ref[h, r] = tile
-
-    def step(index, weights):
-        table = [[table_ref[h, r] for r in range(rows + 1)] for h in range(RIDGES)]
+                table[h].append(tile)
+        return table
+
+    table = systems(None)
+    weights = tuple(jnp.zeros((SUBLANES, LANES), jnp.float32) for _ in range(RIDGES))
+    for index in range(NEWTON):
         solved = solve(table, blocks)
         weights = tuple(
             weights[h] + jnp.broadcast_to(solved[h][0:1], (SUBLANES, LANES))
             for h in range(RIDGES)
         )
-
-        @pl.when(index < NEWTON - 1)
-        def _():
-            systems(weights)
-
-        return weights
-
-    systems(None)
-    start = tuple(jnp.zeros((SUBLANES, LANES), jnp.float32) for _ in range(RIDGES))
-    weights = lax.fori_loop(0, NEWTON, step, start)
+        if index < NEWTON - 1:
+            table = systems(weights)
     result = jnp.zeros((SUBLANES, LANES), jnp.float32)
     for s, tile in enumerate(exchange(weights, blocks)):
         result = jnp.where(sub == s, tile, result)
@@ -451,7 +446,6 @@
         scratch_shapes=[
             pltpu.VMEM((traits * predictors, samples), jnp.bfloat16),
             pltpu.VMEM((traits // 2, 2 * predictors + 2 * traits, samples), jnp.bfloat16),
-            pltpu.VMEM((RIDGES, predictors // SUBLANES + 1, SUBLANES, LANES), jnp.float32),
         ],
         compiler_params=pltpu.CompilerParams(vmem_limit_bytes=48 << 20),
         name="newton",

time: 70.3 us -> 70.2 us (level)
  no operation moved by 1% of the time
where the time goes in v9:
time: 70.2 us; the launch traced here: 70 us
  starting transfers between devices  30.9 us (44%)
  Pallas kernels  20.5 us (29%)
  waiting for transfers between devices  17.3 us (25%)
  local copies, waits for them, and re-layouts  1.28 us (2%)
    ppermute x15, starting transfers between devices, on_device(): lax.ppermute(arrays[j - 1], 'region', [(i, i ^ j) for i in range(regions)])  30.9 us
    ppermute x15, waiting for transfers between devices, on_device(): lax.ppermute(arrays[j - 1], 'region', [(i, i ^ j) for i in range(regions)])  17.3 us
    pallas_call x1, Pallas kernels, newton(): pl.pallas_call(functools.partial(newton_kernel, traits, blocks), out_shap...  11 us
    pallas_call x1, Pallas kernels, level_zero(): pl.pallas_call(level_zero_kernel, out_shape=[jax.ShapeDtypeStruct((height...  9.43 us
  transfers between devices with their start and end apart: 15, of which 5 were waited for; matrix products, arithmetic and copies ran while one was open for 1% of the time, Pallas kernels for 0%

profile of v9, /device:TPU:1, one launch (start us, length us, event | category | flops | bytes accessed | tf_op | source)
XLA Modules:
  0.0 70.0 jit_solution(7853875309718710063)
XLA Ops:
  0.0 0.0 copy-start.1
  0.0 9.4 %level_zero.1 = (bf16[32,2048]{1,0:T(8,128)(2,1)}, bf16[32,2048]{1,0:T(8,128)(2,1)}, bf16[32,2048]{1,0:T(8,128)(2,1)}, bf16[32,2048]{1,0:T(8,128)(2,1)}, bf16[32...) custom-call(bf16[2048,1024]{1,0:T(8,128)(2,1)} %dosage_hbm.1, ...), custom_call_target="tpu_custom_call" | custom-call | tf_op jit(solution)/shard_map/level_zero/pallas_call | solution.py:180
  9.4 4.2 %collective-permute-start = (bf16[32,2048]{1,0:T(8,128)(2,1)}, bf16[32,2048]{1,0:T(8,128)(2,1)S(1)}, u32[]{:S(2)}, u32[]{:S(2)}) collective-permute-start(bf16[32,2048]{1,0:T(8,128)(2,1)} %get-tuple-element.22), channel_id=1, source_target_pairs={{0,12},{1,13},{2,14},{3,15},{4,8},{5,9},{6,10},{7,11},{8,4},{9,5},... | collective-permute-start | bytes 393224 | tf_op jit(solution)/shard_map/ppermute | solution.py:517
  13.7 0.1 collective-permute-start.1
  13.8 1.9 %collective-permute-start.2 = (bf16[32,2048]{1,0:T(8,128)(2,1)}, bf16[32,2048]{1,0:T(8,128)(2,1)S(1)}, u32[]{:S(2)}, u32[]{:S(2)}) collective-permute-start(bf16[32,2048]{1,0:T(8,128)(2,1)} %get-tuple-element.24), channel_id=1, source_target_pairs={{0,10},{1,11},{2,8},{3,9},{4,14},{5,15},{6,12},{7,13},{8,2},{9,3},... | collective-permute-start | bytes 393224 | tf_op jit(solution)/shard_map/ppermute | solution.py:517
  15.7 0.1 collective-permute-start.3
  15.8 3.7 %collective-permute-start.4 = (bf16[32,2048]{1,0:T(8,128)(2,1)}, bf16[32,2048]{1,0:T(8,128)(2,1)S(1)}, u32[]{:S(2)}, u32[]{:S(2)}) collective-permute-start(bf16[32,2048]{1,0:T(8,128)(2,1)} %get-tuple-element.26), channel_id=1, source_target_pairs={{0,13},{1,12},{2,15},{3,14},{4,9},{5,8},{6,11},{7,10},{8,5},{9,4},... | collective-permute-start | bytes 393224 | tf_op jit(solution)/shard_map/ppermute | solution.py:517
  19.5 0.0 collective-permute-done.rest_1_
  19.5 0.6 collective-permute-start.5
  20.1 1.7 %collective-permute-done.1.rest_2_ = bf16[32,2048]{1,0:T(8,128)(2,1)S(1)} collective-permute-done((bf16[32,2048]{1,0:T(8,128)(2,1)}, bf16[32,2048]{1,0:T(8,128)(2,1)S(1)}, u32[]{:S(2)}, u32[]{:S(2)}) %collective-permute-start.1) | collective-permute-done | bytes 131104 | tf_op jit(solution)/shard_map/ppermute | solution.py:517
  21.7 2.3 %collective-permute-start.6 = (bf16[32,2048]{1,0:T(8,128)(2,1)}, bf16[32,2048]{1,0:T(8,128)(2,1)S(1)}, u32[]{:S(2)}, u32[]{:S(2)}) collective-permute-start(bf16[32,2048]{1,0:T(8,128)(2,1)} %get-tuple-element.28), channel_id=1, source_target_pairs={{0,11},{1,10},{2,9},{3,8},{4,15},{5,14},{6,13},{7,12},{8,3},{9,2},... | collective-permute-start | bytes 393224 | tf_op jit(solution)/shard_map/ppermute | solution.py:517
  24.1 4.2 %collective-permute-done.2.rest_3_ = bf16[32,2048]{1,0:T(8,128)(2,1)S(1)} collective-permute-done((bf16[32,2048]{1,0:T(8,128)(2,1)}, bf16[32,2048]{1,0:T(8,128)(2,1)S(1)}, u32[]{:S(2)}, u32[]{:S(2)}) %collective-permute-start.2) | collective-permute-done | bytes 131104 | tf_op jit(solution)/shard_map/ppermute | solution.py:517
  28.3 0.3 collective-permute-start.7
  28.6 0.0 collective-permute-done.3.rest_4_
  28.6 2.3 %collective-permute-start.8 = (bf16[32,2048]{1,0:T(8,128)(2,1)}, bf16[32,2048]{1,0:T(8,128)(2,1)S(1)}, u32[]{:S(2)}, u32[]{:S(2)}) collective-permute-start(bf16[32,2048]{1,0:T(8,128)(2,1)} %get-tuple-element.30), channel_id=1, source_target_pairs={{0,14},{1,15},{2,12},{3,13},{4,10},{5,11},{6,8},{7,9},{8,6},{9,7},... | collective-permute-start | bytes 393224 | tf_op jit(solution)/shard_map/ppermute | solution.py:517
  30.9 0.0 collective-permute-done.4.rest_5_
  30.9 6.1 %collective-permute-start.9 = (bf16[32,2048]{1,0:T(8,128)(2,1)}, bf16[32,2048]{1,0:T(8,128)(2,1)S(1)}, u32[]{:S(2)}, u32[]{:S(2)}) collective-permute-start(bf16[32,2048]{1,0:T(8,128)(2,1)} %get-tuple-element.31), channel_id=1, source_target_pairs={{0,7},{1,6},{2,5},{3,4},{4,3},{5,2},{6,1},{7,0},{8,15},{9,14},{10,... | collective-permute-start | bytes 393224 | tf_op jit(solution)/shard_map/ppermute | solution.py:517
  37.0 0.0 copy-done.1
  37.0 0.2 constant_dynamic-slice_fusion
  37.2 0.2 copy.6
  37.3 0.0 collective-permute-done.5.rest_6_
  37.3 0.2 collective-permute-start.10
  37.5 4.0 %collective-permute-done.6.rest_7_ = bf16[32,2048]{1,0:T(8,128)(2,1)S(1)} collective-permute-done((bf16[32,2048]{1,0:T(8,128)(2,1)}, bf16[32,2048]{1,0:T(8,128)(2,1)S(1)}, u32[]{:S(2)}, u32[]{:S(2)}) %collective-permute-start.6) | collective-permute-done | bytes 131104 | tf_op jit(solution)/shard_map/ppermute | solution.py:517
  41.5 0.8 %collective-permute-start.11 = (bf16[32,2048]{1,0:T(8,128)(2,1)}, bf16[32,2048]{1,0:T(8,128)(2,1)S(1)}, u32[]{:S(2)}, u32[]{:S(2)}) collective-permute-start(bf16[32,2048]{1,0:T(8,128)(2,1)} %get-tuple-element.33), channel_id=1, source_target_pairs={{0,15},{1,14},{2,13},{3,12},{4,11},{5,10},{6,9},{7,8},{8,7},{9,6},... | collective-permute-start | bytes 393224 | tf_op jit(solution)/shard_map/ppermute | solution.py:517
  42.3 0.0 collective-permute-done.7.rest_8_
  42.3 0.0 collective-permute-start.12
  42.3 0.0 collective-permute-done.8.rest_9_
  42.3 8.3 %collective-permute-start.13 = (bf16[32,2048]{1,0:T(8,128)(2,1)}, bf16[32,2048]{1,0:T(8,128)(2,1)S(1)}, u32[]{:S(2)}, u32[]{:S(2)}) collective-permute-start(bf16[32,2048]{1,0:T(8,128)(2,1)} %get-tuple-element.35), channel_id=1, source_target_pairs={{0,9},{1,8},{2,11},{3,10},{4,13},{5,12},{6,15},{7,14},{8,1},{9,0},... | collective-permute-start | bytes 393224 | tf_op jit(solution)/shard_map/ppermute | solution.py:517
  50.6 0.0 collective-permute-done.9.rest_10_
  50.6 0.0 collective-permute-start.14
  50.6 0.0 copy-start
  50.6 0.9 %copy-done = bf16[32,2048]{1,0:T(8,128)(2,1)S(1)} copy-done((bf16[32,2048]{1,0:T(8,128)(2,1)S(1)}, bf16[32,2048]{1,0:T(8,128)(2,1)}, u32[]{:S(2)}) %copy-start) | copy-done | bytes 131096
  51.5 0.0 collective-permute-done.10.rest_11_
  51.6 0.0 collective-permute-done.11.rest_12_
  51.6 0.5 collective-permute-done.12.rest_13_
  52.1 6.9 %collective-permute-done.13.rest_14_ = bf16[32,2048]{1,0:T(8,128)(2,1)S(1)} collective-permute-done((bf16[32,2048]{1,0:T(8,128)(2,1)}, bf16[32,2048]{1,0:T(8,128)(2,1)S(1)}, u32[]{:S(2)}, u32[]{:S(2)}) %collective-permute-start.13) | collective-permute-done | bytes 131104 | tf_op jit(solution)/shard_map/ppermute | solution.py:517
  59.0 0.0 collective-permute-done.14.rest_15_
  59.0 11.0 %newton.1 = f32[8,64]{1,0:T(8,128)} custom-call(s32[1]{0:T(128)} %bitcast.place, bf16[32,2048]{1,0:T(8,128)(2,1)S(1)} %fetch.1.rest_0_, bf16[32,2048]{1,0:T(8,128)(2,1)S(1)} %collective-permute-done.rest_1_, bf16[32,2048]{1,0:T(8,128)(2,1)S(1)} %collective-permute-done.1.rest_2_, bf16[32,2048]{1,0:T(8,128)(2,1)S(1)} %collective-permute-done.2.rest_3_, ...), custom_call_target="tpu_custom_call" | custom-call | tf_op jit(solution)/shard_map/newton/pallas_call | solution.py:441
  (2 shorter events, 0.0 us)
Async XLA Ops:
  0.0 37.0 %copy-start.1 = (bf16[2048,128]{1,0:T(8,128)(2,1)S(1)}, bf16[2048,128]{1,0:T(8,128)(2,1)}, u32[]{:S(2)}) copy-start(bf16[2048,128]{1,0:T(8,128)(2,1)} %pheno_hbm.1) | copy-start | bytes 1572868
  9.4 10.1 %collective-permute-start = (bf16[32,2048]{1,0:T(8,128)(2,1)}, bf16[32,2048]{1,0:T(8,128)(2,1)S(1)}, u32[]{:S(2)}, u32[]{:S(2)}) collective-permute-start(bf16[32,2048]{1,0:T(8,128)(2,1)} %get-tuple-element.22), channel_id=1, source_target_pairs={{0,12},{1,13},{2,14},{3,15},{4,8},{5,9},{6,10},{7,11},{8,4},{9,5},... | collective-permute-start | bytes 393224 | tf_op jit(solution)/shard_map/ppermute | solution.py:517
  13.7 8.1 %collective-permute-start.1 = (bf16[32,2048]{1,0:T(8,128)(2,1)}, bf16[32,2048]{1,0:T(8,128)(2,1)S(1)}, u32[]{:S(2)}, u32[]{:S(2)}) collective-permute-start(bf16[32,2048]{1,0:T(8,128)(2,1)} %get-tuple-element.23), channel_id=1, source_target_pairs={{0,5},{1,4},{2,7},{3,6},{4,1},{5,0},{6,3},{7,2},{8,13},{9,12},{10,... | collective-permute-start | bytes 393224 | tf_op jit(solution)/shard_map/ppermute | solution.py:517
  13.8 14.5 %collective-permute-start.2 = (bf16[32,2048]{1,0:T(8,128)(2,1)}, bf16[32,2048]{1,0:T(8,128)(2,1)S(1)}, u32[]{:S(2)}, u32[]{:S(2)}) collective-permute-start(bf16[32,2048]{1,0:T(8,128)(2,1)} %get-tuple-element.24), channel_id=1, source_target_pairs={{0,10},{1,11},{2,8},{3,9},{4,14},{5,15},{6,12},{7,13},{8,2},{9,3},... | collective-permute-start | bytes 393224 | tf_op jit(solution)/shard_map/ppermute | solution.py:517
  15.7 12.9 %collective-permute-start.3 = (bf16[32,2048]{1,0:T(8,128)(2,1)}, bf16[32,2048]{1,0:T(8,128)(2,1)S(1)}, u32[]{:S(2)}, u32[]{:S(2)}) collective-permute-start(bf16[32,2048]{1,0:T(8,128)(2,1)} %get-tuple-element.25), channel_id=1, source_target_pairs={{0,3},{1,2},{2,1},{3,0},{4,7},{5,6},{6,5},{7,4},{8,11},{9,10},{10,... | collective-permute-start | bytes 393224 | tf_op jit(solution)/shard_map/ppermute | solution.py:517
  15.8 15.1 %collective-permute-start.4 = (bf16[32,2048]{1,0:T(8,128)(2,1)}, bf16[32,2048]{1,0:T(8,128)(2,1)S(1)}, u32[]{:S(2)}, u32[]{:S(2)}) collective-permute-start(bf16[32,2048]{1,0:T(8,128)(2,1)} %get-tuple-element.26), channel_id=1, source_target_pairs={{0,13},{1,12},{2,15},{3,14},{4,9},{5,8},{6,11},{7,10},{8,5},{9,4},... | collective-permute-start | bytes 393224 | tf_op jit(solution)/shard_map/ppermute | solution.py:517
  19.5 17.8 %collective-permute-start.5 = (bf16[32,2048]{1,0:T(8,128)(2,1)}, bf16[32,2048]{1,0:T(8,128)(2,1)S(1)}, u32[]{:S(2)}, u32[]{:S(2)}) collective-permute-start(bf16[32,2048]{1,0:T(8,128)(2,1)} %get-tuple-element.27), channel_id=1, source_target_pairs={{0,6},{1,7},{2,4},{3,5},{4,2},{5,3},{6,0},{7,1},{8,14},{9,15},{10,... | collective-permute-start | bytes 393224 | tf_op jit(solution)/shard_map/ppermute | solution.py:517
  21.7 19.8 %collective-permute-start.6 = (bf16[32,2048]{1,0:T(8,128)(2,1)}, bf16[32,2048]{1,0:T(8,128)(2,1)S(1)}, u32[]{:S(2)}, u32[]{:S(2)}) collective-permute-start(bf16[32,2048]{1,0:T(8,128)(2,1)} %get-tuple-element.28), channel_id=1, source_target_pairs={{0,11},{1,10},{2,9},{3,8},{4,15},{5,14},{6,13},{7,12},{8,3},{9,2},... | collective-permute-start | bytes 393224 | tf_op jit(solution)/shard_map/ppermute | solution.py:517
  28.3 14.1 %collective-permute-start.7 = (bf16[32,2048]{1,0:T(8,128)(2,1)}, bf16[32,2048]{1,0:T(8,128)(2,1)S(1)}, u32[]{:S(2)}, u32[]{:S(2)}) collective-permute-start(bf16[32,2048]{1,0:T(8,128)(2,1)} %get-tuple-element.29), channel_id=1, source_target_pairs={{0,2},{1,3},{2,0},{3,1},{4,6},{5,7},{6,4},{7,5},{8,10},{9,11},{10,... | collective-permute-start | bytes 393224 | tf_op jit(solution)/shard_map/ppermute | solution.py:517
  28.6 13.8 %collective-permute-start.8 = (bf16[32,2048]{1,0:T(8,128)(2,1)}, bf16[32,2048]{1,0:T(8,128)(2,1)S(1)}, u32[]{:S(2)}, u32[]{:S(2)}) collective-permute-start(bf16[32,2048]{1,0:T(8,128)(2,1)} %get-tuple-element.30), channel_id=1, source_target_pairs={{0,14},{1,15},{2,12},{3,13},{4,10},{5,11},{6,8},{7,9},{8,6},{9,7},... | collective-permute-start | bytes 393224 | tf_op jit(solution)/shard_map/ppermute | solution.py:517
  30.9 19.7 %collective-permute-start.9 = (bf16[32,2048]{1,0:T(8,128)(2,1)}, bf16[32,2048]{1,0:T(8,128)(2,1)S(1)}, u32[]{:S(2)}, u32[]{:S(2)}) collective-permute-start(bf16[32,2048]{1,0:T(8,128)(2,1)} %get-tuple-element.31), channel_id=1, source_target_pairs={{0,7},{1,6},{2,5},{3,4},{4,3},{5,2},{6,1},{7,0},{8,15},{9,14},{10,... | collective-permute-start | bytes 393224 | tf_op jit(solution)/shard_map/ppermute | solution.py:517
  37.3 14.2 %collective-permute-start.10 = (bf16[32,2048]{1,0:T(8,128)(2,1)}, bf16[32,2048]{1,0:T(8,128)(2,1)S(1)}, u32[]{:S(2)}, u32[]{:S(2)}) collective-permute-start(bf16[32,2048]{1,0:T(8,128)(2,1)} %get-tuple-element.32), channel_id=1, source_target_pairs={{0,8},{1,9},{2,10},{3,11},{4,12},{5,13},{6,14},{7,15},{8,0},{9,1},... | collective-permute-start | bytes 393224 | tf_op jit(solution)/shard_map/ppermute | solution.py:517
  41.5 10.0 %collective-permute-start.11 = (bf16[32,2048]{1,0:T(8,128)(2,1)}, bf16[32,2048]{1,0:T(8,128)(2,1)S(1)}, u32[]{:S(2)}, u32[]{:S(2)}) collective-permute-start(bf16[32,2048]{1,0:T(8,128)(2,1)} %get-tuple-element.33), channel_id=1, source_target_pairs={{0,15},{1,14},{2,13},{3,12},{4,11},{5,10},{6,9},{7,8},{8,7},{9,6},... | collective-permute-start | bytes 393224 | tf_op jit(solution)/shard_map/ppermute | solution.py:517
  42.3 9.7 %collective-permute-start.12 = (bf16[32,2048]{1,0:T(8,128)(2,1)}, bf16[32,2048]{1,0:T(8,128)(2,1)S(1)}, u32[]{:S(2)}, u32[]{:S(2)}) collective-permute-start(bf16[32,2048]{1,0:T(8,128)(2,1)} %get-tuple-element.34), channel_id=1, source_target_pairs={{0,4},{1,5},{2,6},{3,7},{4,0},{5,1},{6,2},{7,3},{8,12},{9,13},{10,... | collective-permute-start | bytes 393224 | tf_op jit(solution)/shard_map/ppermute | solution.py:517
  42.3 16.7 %collective-permute-start.13 = (bf16[32,2048]{1,0:T(8,128)(2,1)}, bf16[32,2048]{1,0:T(8,128)(2,1)S(1)}, u32[]{:S(2)}, u32[]{:S(2)}) collective-permute-start(bf16[32,2048]{1,0:T(8,128)(2,1)} %get-tuple-element.35), channel_id=1, source_target_pairs={{0,9},{1,8},{2,11},{3,10},{4,13},{5,12},{6,15},{7,14},{8,1},{9,0},... | collective-permute-start | bytes 393224 | tf_op jit(solution)/shard_map/ppermute | solution.py:517
  50.6 8.4 %collective-permute-start.14 = (bf16[32,2048]{1,0:T(8,128)(2,1)}, bf16[32,2048]{1,0:T(8,128)(2,1)S(1)}, u32[]{:S(2)}, u32[]{:S(2)}) collective-permute-start(bf16[32,2048]{1,0:T(8,128)(2,1)} %get-tuple-element.36), channel_id=1, source_target_pairs={{0,1},{1,0},{2,3},{3,2},{4,5},{5,4},{6,7},{7,6},{8,9},{9,8},{10,11... | collective-permute-start | bytes 393224 | tf_op jit(solution)/shard_map/ppermute | solution.py:517
  50.6 0.9 %copy-start = (bf16[32,2048]{1,0:T(8,128)(2,1)S(1)}, bf16[32,2048]{1,0:T(8,128)(2,1)}, u32[]{:S(2)}) copy-start(bf16[32,2048]{1,0:T(8,128)(2,1)} %get-tuple-element.21.block) | copy-start | bytes 393220

commit v10 on v9

--- a/solution.py
+++ b/solution.py
@@ -16,7 +16,7 @@
 SUBLANES = 8
 TILE = 256
 WIDE = 512
-ORDER = (12, 5, 10, 3, 13, 6, 11, 2, 14, 7, 8, 15, 4, 9, 1)
+ORDER = (12, 6, 10, 3, 13, 5, 11, 2, 14, 4, 8, 15, 7, 9, 1)
 
 
 def level_zero_kernel(

time: 70.2 us -> 70.2 us (level)
  waiting for transfers between devices: 17.3 us -> 15.4 us
  starting transfers between devices: 30.9 us -> 32.8 us
    ppermute x15, waiting for transfers between devices: 17.3 us -> 15.4 us  [on_device(): lax.ppermute(arrays[j - 1], 'region', [(i, i ^ j) for i in range(regions)])]
    ppermute x15, starting transfers between devices: 30.9 us -> 32.8 us  [on_device(): lax.ppermute(arrays[j - 1], 'region', [(i, i ^ j) for i in range(regions)])]
  transfers between devices with their start and end apart: 15 -> 15, of which waited for: 5 -> 4; matrix products, arithmetic and copies ran while one was open for 1% -> 1% of each run, Pallas kernels for 0% -> 0%
where the time goes in v10:
time: 70.2 us; the launch traced here: 70 us
  starting transfers between devices  32.8 us (47%)
  Pallas kernels  20.5 us (29%)
  waiting for transfers between devices  15.4 us (22%)
  local copies, waits for them, and re-layouts  1.28 us (2%)
    ppermute x15, starting transfers between devices, on_device(): lax.ppermute(arrays[j - 1], 'region', [(i, i ^ j) for i in range(regions)])  32.8 us
    ppermute x15, waiting for transfers between devices, on_device(): lax.ppermute(arrays[j - 1], 'region', [(i, i ^ j) for i in range(regions)])  15.4 us
    pallas_call x1, Pallas kernels, newton(): pl.pallas_call(functools.partial(newton_kernel, traits, blocks), out_shap...  11 us
    pallas_call x1, Pallas kernels, level_zero(): pl.pallas_call(level_zero_kernel, out_shape=[jax.ShapeDtypeStruct((height...  9.43 us
  transfers between devices with their start and end apart: 15, of which 4 were waited for; matrix products, arithmetic and copies ran while one was open for 1% of the time, Pallas kernels for 0%

profile of v10, /device:TPU:1, one launch (start us, length us, event | category | flops | bytes accessed | tf_op | source)
XLA Modules:
  0.0 70.0 jit_solution(3501636250146027316)
XLA Ops:
  0.0 0.0 copy-start.1
  0.0 9.4 %level_zero.1 = (bf16[32,2048]{1,0:T(8,128)(2,1)}, bf16[32,2048]{1,0:T(8,128)(2,1)}, bf16[32,2048]{1,0:T(8,128)(2,1)}, bf16[32,2048]{1,0:T(8,128)(2,1)}, bf16[32...) custom-call(bf16[2048,1024]{1,0:T(8,128)(2,1)} %dosage_hbm.1, ...), custom_call_target="tpu_custom_call" | custom-call | tf_op jit(solution)/shard_map/level_zero/pallas_call | solution.py:180
  9.4 4.2 %collective-permute-start = (bf16[32,2048]{1,0:T(8,128)(2,1)}, bf16[32,2048]{1,0:T(8,128)(2,1)S(1)}, u32[]{:S(2)}, u32[]{:S(2)}) collective-permute-start(bf16[32,2048]{1,0:T(8,128)(2,1)} %get-tuple-element.22), channel_id=1, source_target_pairs={{0,12},{1,13},{2,14},{3,15},{4,8},{5,9},{6,10},{7,11},{8,4},{9,5},... | collective-permute-start | bytes 393224 | tf_op jit(solution)/shard_map/ppermute | solution.py:517
  13.7 0.2 collective-permute-start.1
  13.9 1.0 %collective-permute-start.2 = (bf16[32,2048]{1,0:T(8,128)(2,1)}, bf16[32,2048]{1,0:T(8,128)(2,1)S(1)}, u32[]{:S(2)}, u32[]{:S(2)}) collective-permute-start(bf16[32,2048]{1,0:T(8,128)(2,1)} %get-tuple-element.24), channel_id=1, source_target_pairs={{0,10},{1,11},{2,8},{3,9},{4,14},{5,15},{6,12},{7,13},{8,2},{9,3},... | collective-permute-start | bytes 393224 | tf_op jit(solution)/shard_map/ppermute | solution.py:517
  14.9 2.5 %collective-permute-start.3 = (bf16[32,2048]{1,0:T(8,128)(2,1)}, bf16[32,2048]{1,0:T(8,128)(2,1)S(1)}, u32[]{:S(2)}, u32[]{:S(2)}) collective-permute-start(bf16[32,2048]{1,0:T(8,128)(2,1)} %get-tuple-element.25), channel_id=1, source_target_pairs={{0,3},{1,2},{2,1},{3,0},{4,7},{5,6},{6,5},{7,4},{8,11},{9,10},{10,... | collective-permute-start | bytes 393224 | tf_op jit(solution)/shard_map/ppermute | solution.py:517
  17.4 2.2 %collective-permute-start.4 = (bf16[32,2048]{1,0:T(8,128)(2,1)}, bf16[32,2048]{1,0:T(8,128)(2,1)S(1)}, u32[]{:S(2)}, u32[]{:S(2)}) collective-permute-start(bf16[32,2048]{1,0:T(8,128)(2,1)} %get-tuple-element.26), channel_id=1, source_target_pairs={{0,13},{1,12},{2,15},{3,14},{4,9},{5,8},{6,11},{7,10},{8,5},{9,4},... | collective-permute-start | bytes 393224 | tf_op jit(solution)/shard_map/ppermute | solution.py:517
  19.6 0.0 collective-permute-done.rest_1_
  19.6 2.6 %collective-permute-start.5 = (bf16[32,2048]{1,0:T(8,128)(2,1)}, bf16[32,2048]{1,0:T(8,128)(2,1)S(1)}, u32[]{:S(2)}, u32[]{:S(2)}) collective-permute-start(bf16[32,2048]{1,0:T(8,128)(2,1)} %get-tuple-element.27), channel_id=1, source_target_pairs={{0,5},{1,4},{2,7},{3,6},{4,1},{5,0},{6,3},{7,2},{8,13},{9,12},{10,... | collective-permute-start | bytes 393224 | tf_op jit(solution)/shard_map/ppermute | solution.py:517
  22.2 0.0 collective-permute-done.1.rest_2_
  22.3 1.0 %collective-permute-start.6 = (bf16[32,2048]{1,0:T(8,128)(2,1)}, bf16[32,2048]{1,0:T(8,128)(2,1)S(1)}, u32[]{:S(2)}, u32[]{:S(2)}) collective-permute-start(bf16[32,2048]{1,0:T(8,128)(2,1)} %get-tuple-element.28), channel_id=1, source_target_pairs={{0,11},{1,10},{2,9},{3,8},{4,15},{5,14},{6,13},{7,12},{8,3},{9,2},... | collective-permute-start | bytes 393224 | tf_op jit(solution)/shard_map/ppermute | solution.py:517
  23.2 4.9 %collective-permute-done.2.rest_3_ = bf16[32,2048]{1,0:T(8,128)(2,1)S(1)} collective-permute-done((bf16[32,2048]{1,0:T(8,128)(2,1)}, bf16[32,2048]{1,0:T(8,128)(2,1)S(1)}, u32[]{:S(2)}, u32[]{:S(2)}) %collective-permute-start.2) | collective-permute-done | bytes 131104 | tf_op jit(solution)/shard_map/ppermute | solution.py:517
  28.1 0.2 collective-permute-start.7
  28.3 0.0 collective-permute-done.3.rest_4_
  28.3 1.3 %collective-permute-start.8 = (bf16[32,2048]{1,0:T(8,128)(2,1)}, bf16[32,2048]{1,0:T(8,128)(2,1)S(1)}, u32[]{:S(2)}, u32[]{:S(2)}) collective-permute-start(bf16[32,2048]{1,0:T(8,128)(2,1)} %get-tuple-element.30), channel_id=1, source_target_pairs={{0,14},{1,15},{2,12},{3,13},{4,10},{5,11},{6,8},{7,9},{8,6},{9,7},... | collective-permute-start | bytes 393224 | tf_op jit(solution)/shard_map/ppermute | solution.py:517
  29.6 0.0 collective-permute-done.4.rest_5_
  29.6 6.7 %collective-permute-start.9 = (bf16[32,2048]{1,0:T(8,128)(2,1)}, bf16[32,2048]{1,0:T(8,128)(2,1)S(1)}, u32[]{:S(2)}, u32[]{:S(2)}) collective-permute-start(bf16[32,2048]{1,0:T(8,128)(2,1)} %get-tuple-element.31), channel_id=1, source_target_pairs={{0,4},{1,5},{2,6},{3,7},{4,0},{5,1},{6,2},{7,3},{8,12},{9,13},{10,... | collective-permute-start | bytes 393224 | tf_op jit(solution)/shard_map/ppermute | solution.py:517
  36.3 0.0 copy-done.1
  36.3 0.2 constant_dynamic-slice_fusion
  36.5 0.2 copy.6
  36.7 0.0 collective-permute-done.5.rest_6_
  36.7 0.8 %collective-permute-start.10 = (bf16[32,2048]{1,0:T(8,128)(2,1)}, bf16[32,2048]{1,0:T(8,128)(2,1)S(1)}, u32[]{:S(2)}, u32[]{:S(2)}) collective-permute-start(bf16[32,2048]{1,0:T(8,128)(2,1)} %get-tuple-element.32), channel_id=1, source_target_pairs={{0,8},{1,9},{2,10},{3,11},{4,12},{5,13},{6,14},{7,15},{8,0},{9,1},... | collective-permute-start | bytes 393224 | tf_op jit(solution)/shard_map/ppermute | solution.py:517
  37.5 3.7 %collective-permute-done.6.rest_7_ = bf16[32,2048]{1,0:T(8,128)(2,1)S(1)} collective-permute-done((bf16[32,2048]{1,0:T(8,128)(2,1)}, bf16[32,2048]{1,0:T(8,128)(2,1)S(1)}, u32[]{:S(2)}, u32[]{:S(2)}) %collective-permute-start.6) | collective-permute-done | bytes 131104 | tf_op jit(solution)/shard_map/ppermute | solution.py:517
  41.2 1.1 %collective-permute-start.11 = (bf16[32,2048]{1,0:T(8,128)(2,1)}, bf16[32,2048]{1,0:T(8,128)(2,1)S(1)}, u32[]{:S(2)}, u32[]{:S(2)}) collective-permute-start(bf16[32,2048]{1,0:T(8,128)(2,1)} %get-tuple-element.33), channel_id=1, source_target_pairs={{0,15},{1,14},{2,13},{3,12},{4,11},{5,10},{6,9},{7,8},{8,7},{9,6},... | collective-permute-start | bytes 393224 | tf_op jit(solution)/shard_map/ppermute | solution.py:517
  42.3 0.0 collective-permute-done.7.rest_8_
  42.3 0.0 collective-permute-start.12
  42.3 0.0 collective-permute-done.8.rest_9_
  42.3 8.9 %collective-permute-start.13 = (bf16[32,2048]{1,0:T(8,128)(2,1)}, bf16[32,2048]{1,0:T(8,128)(2,1)S(1)}, u32[]{:S(2)}, u32[]{:S(2)}) collective-permute-start(bf16[32,2048]{1,0:T(8,128)(2,1)} %get-tuple-element.35), channel_id=1, source_target_pairs={{0,9},{1,8},{2,11},{3,10},{4,13},{5,12},{6,15},{7,14},{8,1},{9,0},... | collective-permute-start | bytes 393224 | tf_op jit(solution)/shard_map/ppermute | solution.py:517
  51.2 0.0 collective-permute-done.9.rest_10_
  51.2 0.0 collective-permute-start.14
  51.2 0.0 copy-start
  51.2 0.9 %copy-done = bf16[32,2048]{1,0:T(8,128)(2,1)S(1)} copy-done((bf16[32,2048]{1,0:T(8,128)(2,1)S(1)}, bf16[32,2048]{1,0:T(8,128)(2,1)}, u32[]{:S(2)}) %copy-start) | copy-done | bytes 131096
  52.1 0.0 collective-permute-done.10.rest_11_
  52.2 0.0 collective-permute-done.11.rest_12_
  52.2 1.5 %collective-permute-done.12.rest_13_ = bf16[32,2048]{1,0:T(8,128)(2,1)S(1)} collective-permute-done((bf16[32,2048]{1,0:T(8,128)(2,1)}, bf16[32,2048]{1,0:T(8,128)(2,1)S(1)}, u32[]{:S(2)}, u32[]{:S(2)}) %collective-permute-start.12) | collective-permute-done | bytes 131104 | tf_op jit(solution)/shard_map/ppermute | solution.py:517
  53.6 5.4 %collective-permute-done.13.rest_14_ = bf16[32,2048]{1,0:T(8,128)(2,1)S(1)} collective-permute-done((bf16[32,2048]{1,0:T(8,128)(2,1)}, bf16[32,2048]{1,0:T(8,128)(2,1)S(1)}, u32[]{:S(2)}, u32[]{:S(2)}) %collective-permute-start.13) | collective-permute-done | bytes 131104 | tf_op jit(solution)/shard_map/ppermute | solution.py:517
  59.0 0.0 collective-permute-done.14.rest_15_
  59.0 11.0 %newton.1 = f32[8,64]{1,0:T(8,128)} custom-call(s32[1]{0:T(128)} %bitcast.place, bf16[32,2048]{1,0:T(8,128)(2,1)S(1)} %fetch.1.rest_0_, bf16[32,2048]{1,0:T(8,128)(2,1)S(1)} %collective-permute-done.rest_1_, bf16[32,2048]{1,0:T(8,128)(2,1)S(1)} %collective-permute-done.1.rest_2_, bf16[32,2048]{1,0:T(8,128)(2,1)S(1)} %collective-permute-done.2.rest_3_, ...), custom_call_target="tpu_custom_call" | custom-call | tf_op jit(solution)/shard_map/newton/pallas_call | solution.py:441
  (2 shorter events, 0.0 us)
Async XLA Ops:
  0.0 36.3 %copy-start.1 = (bf16[2048,128]{1,0:T(8,128)(2,1)S(1)}, bf16[2048,128]{1,0:T(8,128)(2,1)}, u32[]{:S(2)}) copy-start(bf16[2048,128]{1,0:T(8,128)(2,1)} %pheno_hbm.1) | copy-start | bytes 1572868
  9.4 10.2 %collective-permute-start = (bf16[32,2048]{1,0:T(8,128)(2,1)}, bf16[32,2048]{1,0:T(8,128)(2,1)S(1)}, u32[]{:S(2)}, u32[]{:S(2)}) collective-permute-start(bf16[32,2048]{1,0:T(8,128)(2,1)} %get-tuple-element.22), channel_id=1, source_target_pairs={{0,12},{1,13},{2,14},{3,15},{4,8},{5,9},{6,10},{7,11},{8,4},{9,5},... | collective-permute-start | bytes 393224 | tf_op jit(solution)/shard_map/ppermute | solution.py:517
  13.7 8.6 %collective-permute-start.1 = (bf16[32,2048]{1,0:T(8,128)(2,1)}, bf16[32,2048]{1,0:T(8,128)(2,1)S(1)}, u32[]{:S(2)}, u32[]{:S(2)}) collective-permute-start(bf16[32,2048]{1,0:T(8,128)(2,1)} %get-tuple-element.23), channel_id=1, source_target_pairs={{0,6},{1,7},{2,4},{3,5},{4,2},{5,3},{6,0},{7,1},{8,14},{9,15},{10,... | collective-permute-start | bytes 393224 | tf_op jit(solution)/shard_map/ppermute | solution.py:517
  13.9 14.2 %collective-permute-start.2 = (bf16[32,2048]{1,0:T(8,128)(2,1)}, bf16[32,2048]{1,0:T(8,128)(2,1)S(1)}, u32[]{:S(2)}, u32[]{:S(2)}) collective-permute-start(bf16[32,2048]{1,0:T(8,128)(2,1)} %get-tuple-element.24), channel_id=1, source_target_pairs={{0,10},{1,11},{2,8},{3,9},{4,14},{5,15},{6,12},{7,13},{8,2},{9,3},... | collective-permute-start | bytes 393224 | tf_op jit(solution)/shard_map/ppermute | solution.py:517
  14.9 13.4 %collective-permute-start.3 = (bf16[32,2048]{1,0:T(8,128)(2,1)}, bf16[32,2048]{1,0:T(8,128)(2,1)S(1)}, u32[]{:S(2)}, u32[]{:S(2)}) collective-permute-start(bf16[32,2048]{1,0:T(8,128)(2,1)} %get-tuple-element.25), channel_id=1, source_target_pairs={{0,3},{1,2},{2,1},{3,0},{4,7},{5,6},{6,5},{7,4},{8,11},{9,10},{10,... | collective-permute-start | bytes 393224 | tf_op jit(solution)/shard_map/ppermute | solution.py:517
  17.4 12.2 %collective-permute-start.4 = (bf16[32,2048]{1,0:T(8,128)(2,1)}, bf16[32,2048]{1,0:T(8,128)(2,1)S(1)}, u32[]{:S(2)}, u32[]{:S(2)}) collective-permute-start(bf16[32,2048]{1,0:T(8,128)(2,1)} %get-tuple-element.26), channel_id=1, source_target_pairs={{0,13},{1,12},{2,15},{3,14},{4,9},{5,8},{6,11},{7,10},{8,5},{9,4},... | collective-permute-start | bytes 393224 | tf_op jit(solution)/shard_map/ppermute | solution.py:517
  19.6 17.1 %collective-permute-start.5 = (bf16[32,2048]{1,0:T(8,128)(2,1)}, bf16[32,2048]{1,0:T(8,128)(2,1)S(1)}, u32[]{:S(2)}, u32[]{:S(2)}) collective-permute-start(bf16[32,2048]{1,0:T(8,128)(2,1)} %get-tuple-element.27), channel_id=1, source_target_pairs={{0,5},{1,4},{2,7},{3,6},{4,1},{5,0},{6,3},{7,2},{8,13},{9,12},{10,... | collective-permute-start | bytes 393224 | tf_op jit(solution)/shard_map/ppermute | solution.py:517
  22.3 18.9 %collective-permute-start.6 = (bf16[32,2048]{1,0:T(8,128)(2,1)}, bf16[32,2048]{1,0:T(8,128)(2,1)S(1)}, u32[]{:S(2)}, u32[]{:S(2)}) collective-permute-start(bf16[32,2048]{1,0:T(8,128)(2,1)} %get-tuple-element.28), channel_id=1, source_target_pairs={{0,11},{1,10},{2,9},{3,8},{4,15},{5,14},{6,13},{7,12},{8,3},{9,2},... | collective-permute-start | bytes 393224 | tf_op jit(solution)/shard_map/ppermute | solution.py:517
  28.1 14.2 %collective-permute-start.7 = (bf16[32,2048]{1,0:T(8,128)(2,1)}, bf16[32,2048]{1,0:T(8,128)(2,1)S(1)}, u32[]{:S(2)}, u32[]{:S(2)}) collective-permute-start(bf16[32,2048]{1,0:T(8,128)(2,1)} %get-tuple-element.29), channel_id=1, source_target_pairs={{0,2},{1,3},{2,0},{3,1},{4,6},{5,7},{6,4},{7,5},{8,10},{9,11},{10,... | collective-permute-start | bytes 393224 | tf_op jit(solution)/shard_map/ppermute | solution.py:517
  28.3 14.0 %collective-permute-start.8 = (bf16[32,2048]{1,0:T(8,128)(2,1)}, bf16[32,2048]{1,0:T(8,128)(2,1)S(1)}, u32[]{:S(2)}, u32[]{:S(2)}) collective-permute-start(bf16[32,2048]{1,0:T(8,128)(2,1)} %get-tuple-element.30), channel_id=1, source_target_pairs={{0,14},{1,15},{2,12},{3,13},{4,10},{5,11},{6,8},{7,9},{8,6},{9,7},... | collective-permute-start | bytes 393224 | tf_op jit(solution)/shard_map/ppermute | solution.py:517
  29.6 21.6 %collective-permute-start.9 = (bf16[32,2048]{1,0:T(8,128)(2,1)}, bf16[32,2048]{1,0:T(8,128)(2,1)S(1)}, u32[]{:S(2)}, u32[]{:S(2)}) collective-permute-start(bf16[32,2048]{1,0:T(8,128)(2,1)} %get-tuple-element.31), channel_id=1, source_target_pairs={{0,4},{1,5},{2,6},{3,7},{4,0},{5,1},{6,2},{7,3},{8,12},{9,13},{10,... | collective-permute-start | bytes 393224 | tf_op jit(solution)/shard_map/ppermute | solution.py:517
  36.7 15.4 %collective-permute-start.10 = (bf16[32,2048]{1,0:T(8,128)(2,1)}, bf16[32,2048]{1,0:T(8,128)(2,1)S(1)}, u32[]{:S(2)}, u32[]{:S(2)}) collective-permute-start(bf16[32,2048]{1,0:T(8,128)(2,1)} %get-tuple-element.32), channel_id=1, source_target_pairs={{0,8},{1,9},{2,10},{3,11},{4,12},{5,13},{6,14},{7,15},{8,0},{9,1},... | collective-permute-start | bytes 393224 | tf_op jit(solution)/shard_map/ppermute | solution.py:517
  41.2 11.0 %collective-permute-start.11 = (bf16[32,2048]{1,0:T(8,128)(2,1)}, bf16[32,2048]{1,0:T(8,128)(2,1)S(1)}, u32[]{:S(2)}, u32[]{:S(2)}) collective-permute-start(bf16[32,2048]{1,0:T(8,128)(2,1)} %get-tuple-element.33), channel_id=1, source_target_pairs={{0,15},{1,14},{2,13},{3,12},{4,11},{5,10},{6,9},{7,8},{8,7},{9,6},... | collective-permute-start | bytes 393224 | tf_op jit(solution)/shard_map/ppermute | solution.py:517
  42.3 11.3 %collective-permute-start.12 = (bf16[32,2048]{1,0:T(8,128)(2,1)}, bf16[32,2048]{1,0:T(8,128)(2,1)S(1)}, u32[]{:S(2)}, u32[]{:S(2)}) collective-permute-start(bf16[32,2048]{1,0:T(8,128)(2,1)} %get-tuple-element.34), channel_id=1, source_target_pairs={{0,7},{1,6},{2,5},{3,4},{4,3},{5,2},{6,1},{7,0},{8,15},{9,14},{10,... | collective-permute-start | bytes 393224 | tf_op jit(solution)/shard_map/ppermute | solution.py:517
  42.3 16.7 %collective-permute-start.13 = (bf16[32,2048]{1,0:T(8,128)(2,1)}, bf16[32,2048]{1,0:T(8,128)(2,1)S(1)}, u32[]{:S(2)}, u32[]{:S(2)}) collective-permute-start(bf16[32,2048]{1,0:T(8,128)(2,1)} %get-tuple-element.35), channel_id=1, source_target_pairs={{0,9},{1,8},{2,11},{3,10},{4,13},{5,12},{6,15},{7,14},{8,1},{9,0},... | collective-permute-start | bytes 393224 | tf_op jit(solution)/shard_map/ppermute | solution.py:517
  51.2 7.8 %collective-permute-start.14 = (bf16[32,2048]{1,0:T(8,128)(2,1)}, bf16[32,2048]{1,0:T(8,128)(2,1)S(1)}, u32[]{:S(2)}, u32[]{:S(2)}) collective-permute-start(bf16[32,2048]{1,0:T(8,128)(2,1)} %get-tuple-element.36), channel_id=1, source_target_pairs={{0,1},{1,0},{2,3},{3,2},{4,5},{5,4},{6,7},{7,6},{8,9},{9,8},{10,11... | collective-permute-start | bytes 393224 | tf_op jit(solution)/shard_map/ppermute | solution.py:517
  51.2 0.9 %copy-start = (bf16[32,2048]{1,0:T(8,128)(2,1)S(1)}, bf16[32,2048]{1,0:T(8,128)(2,1)}, u32[]{:S(2)}) copy-start(bf16[32,2048]{1,0:T(8,128)(2,1)} %get-tuple-element.21.block) | copy-start | bytes 393220
